TPU v7x, 32 devices: a whole 2x2x4 slice. The times are simulated.
32 devices in a mesh: row: 4 (over z), col: 8 (over y, x, core).
Axes of the slice: x: 2, y: 2, z: 4, core: 2. Of those that a mesh axis runs over, the one named last changes fastest.
Arguments:
- activations: bfloat16 [4096, 8192], P('row', 'col'), may hold values from -6 to 6
- errors: bfloat16 [4096, 8192], P('row', 'col'), may hold values from -6 to 6
- act_proj: bfloat16 [8192, 128], P('col'), may hold values from -0.0625 to 0.0625
- err_proj: bfloat16 [8192, 128], P('col'), may hold values from -0.0625 to 0.0625
- lengths: int32 [4, 64], P('row'), may hold values from 1 to 256, 1024 in all within a row
- ridge: float32 [16384, 16384], P('row', 'col'), may hold values from -4 to 36, as said below
- pivot_inverse: float32 [2, 512, 512], replicated, may hold values from -1 to 1
Outputs:
- eliminated: float32 [16384, 16384], P('row', 'col')
Inputs may be any that keep to these rules, and one draw needn't show every extreme that they name: The lengths of one row group sum to 1024. `ridge`: Symmetric.
All inputs are finite; a program needn't handle non-finite values.
Results may differ from a plain program's by a relative error of at most 0.0074.
Values may be sent and summed in bfloat16 or wider, within the bound.
No kernel may reach another device: no remote copies, remote signals or barrier semaphores. Data moves between devices by JAX's collectives and lax.ppermute only.
A program may use at most 192 MiB of HBM per device.

v0:
```python
import jax
import jax.numpy as jnp
from jax import lax
from jax.sharding import PartitionSpec as P


def spread_2(array, axis, root):
    mine = lax.axis_index(axis) == root
    return lax.psum(jnp.where(mine, array, jnp.zeros_like(array)), axis)


def as_sent(array):

    def short(part):
        return part.astype(jnp.bfloat16) if part.dtype == jnp.float32 else part

    return jax.tree.map(short, array)


def per_device(activations, errors, act_proj, err_proj, lengths, ridge, pivot_inverse):
    part_act = jnp.dot(activations, act_proj, preferred_element_type=jnp.float32)
    part_err = jnp.dot(errors, err_proj, preferred_element_type=jnp.float32)
    summed_act, summed_err = lax.psum((part_act, part_err), "col")
    proj_act = summed_act.astype(jnp.bfloat16)
    col_count = lax.axis_size("col")
    row_count = lax.axis_size("row")
    col_ratio = col_count // row_count
    col_idx = lax.axis_index("col")
    row_idx = lax.axis_index("row")
    proj_width = act_proj.shape[1]
    err_share = proj_width // col_count
    err_part = lax.dynamic_slice_in_dim(summed_err, col_idx * err_share, err_share, 1).astype(
        jnp.bfloat16
    )
    lengths_row = lengths[0]
    captions_dev = lengths_row.shape[0]
    tokens_dev = activations.shape[0]
    caption_end = jnp.cumsum(lengths_row)
    caption_start = caption_end - lengths_row
    positions = jnp.arange(tokens_dev, dtype=jnp.int32)[:, None]
    member = ((positions >= caption_start[None, :]) & (positions < caption_end[None, :])).astype(
        jnp.bfloat16
    )
    weighted = (member[:, :, None] * err_part[:, None, :]).reshape(
        tokens_dev, captions_dev * err_share
    )
    local_grads = lax.dot_general(
        weighted, proj_act, (((0,), (0,)), ((), ())), preferred_element_type=jnp.float32
    )
    local_grads = local_grads.reshape(captions_dev, err_share * proj_width).astype(jnp.bfloat16)
    col_grads = lax.all_gather(local_grads, "row", axis=0, tiled=True)
    row_parts = []
    for column_step in range(col_ratio):
        row_parts.append(spread_2(col_grads, "col", row_idx * col_ratio + column_step))
    row_grads = jnp.concatenate(row_parts, axis=1)
    captions_all = col_grads.shape[0]
    gram_tile = lax.dot_general(
        row_grads, col_grads, (((0,), (0,)), ((), ())), preferred_element_type=jnp.float32
    )
    matrix = ridge + gram_tile / captions_all
    tile_rows, tile_cols = ridge.shape
    row_start = row_idx * tile_rows
    col_start = col_idx * tile_cols
    row_ids = row_start + jnp.arange(tile_rows, dtype=jnp.int32)
    col_ids = col_start + jnp.arange(tile_cols, dtype=jnp.int32)
    panel_width = pivot_inverse.shape[1]

    def apply_inverse(columns, start_col, inverse):
        result = jnp.dot(columns, inverse.T, precision=lax.Precision.HIGHEST)
        return jnp.where(row_ids[:, None] >= start_col, result, 0.0)

    first_panel = apply_inverse(matrix[:, 0:panel_width], 0, pivot_inverse[0])
    pivot_block = spread_2(
        first_panel[panel_width : 2 * panel_width].astype(jnp.bfloat16), "row", 0
    ).astype(jnp.float32)
    lower_first = jnp.where(row_ids[:, None] >= panel_width, first_panel, 0.0)
    second_block = matrix[:, panel_width : 2 * panel_width] - jnp.dot(
        lower_first, pivot_block.T, precision=lax.Precision.HIGHEST
    )
    second_panel = apply_inverse(second_block, panel_width, pivot_inverse[1])
    both_panels = jnp.concatenate([first_panel, second_panel], axis=1)
    row_panel = spread_2(as_sent(both_panels), "col", 0).astype(both_panels.dtype)
    col_piece = lax.dynamic_slice_in_dim(row_panel, col_idx % col_ratio * tile_cols, tile_cols, 0)
    col_panel = spread_2(as_sent(col_piece), "row", col_idx // col_ratio).astype(col_piece.dtype)
    row_panel, col_panel = (row_panel, col_panel)
    current = matrix
    stop_col = 2 * panel_width
    lower_part = jnp.where(row_ids[:, None] >= stop_col, row_panel, 0.0)
    upper_part = jnp.where(col_ids[:, None] >= stop_col, col_panel, 0.0)
    current = current - jnp.dot(lower_part, upper_part.T, precision=lax.Precision.HIGHEST)
    offset = jnp.clip(0 - col_start, 0, tile_cols - (stop_col - 0))
    placed = lax.dynamic_update_slice(jnp.zeros_like(current), row_panel, (jnp.int32(0), offset))
    in_panel = (col_ids >= 0) & (col_ids < stop_col)
    current = jnp.where(in_panel[None, :], placed, current)
    above_panel = ((row_ids >= 0) & (row_ids < stop_col))[:, None] & (col_ids >= stop_col)[None, :]
    return jnp.where(above_panel, 0.0, current)


def solution(mesh):
    in_specs = (
        P("row", "col"),
        P("row", "col"),
        P("col", None),
        P("col", None),
        P("row", None),
        P("row", "col"),
        P(),
    )
    out_specs = P("row", "col")
    return jax.shard_map(
        per_device, mesh=mesh, in_specs=in_specs, out_specs=out_specs, check_vma=False
    )
```

profile of v0, /device:TPU:0, one launch (start us, length us, event | category | flops | bytes accessed | tf_op | source)
XLA Modules:
  0.0 710.1 jit_solution(3458219125566349725)
XLA Ops:
  6.5 0.0 copy-start
  6.5 0.0 all-gather.2.cloned.1.call-start
  6.5 1.6 copy-done
  8.1 1.8 fusion.41
  9.9 2.3 fusion.42
  12.2 0.7 copy.12
  13.0 0.1 reduce-window.4
  13.0 0.1 reduce
  13.2 0.7 fusion.37
  13.8 0.1 fusion.27
  13.9 52.8 %all-reduce.15 = (bf16[1024,128]{0,1:T(8,128)(2,1)S(1)}, bf16[1024,128]{1,0:T(8,128)(2,1)S(1)}) all-reduce(f32[1024,128]{0,1:T(8,128)S(1)} %fusion.41, f32[1024,128]{1,0:T(8,128)S(1)} %fusion.42), channel_id=1, replica_groups=mesh['row'=4,'col'=8] {'col'}, use_global_device_ids=true, to_apply=%region_1.0 | all-reduce | flops 262144 | bytes 1572864 | tf_op jit(solution)/shard_map/psum | solution.py:23
  66.8 0.2 broadcast_multiply_fusion
  67.0 0.7 convolution_convert_fusion
  67.7 0.8 convert_element_type.35
  68.5 0.0 all-gather.2.cloned.1.call-update
  68.5 0.0 all-reduce.14.cloned.1.call-start
  68.6 27.7 %all-gather.2.cloned.1.call-done = bf16[256,2048]{1,0:T(8,128)(2,1)} async-done(((bf16[64,2048]{1,0:T(8,128)(2,1)}), bf16[256,2048]{1,0:T(8,128)(2,1)}) %all-gather.2.cloned.1.call-update) | async-done | bytes 1048592 | tf_op jit(solution)/shard_map/all_gather | solution.py:51
  96.3 2.7 broadcast_select_fusion.1
  99.0 0.0 all-reduce.14.cloned.1.call-update
  99.0 0.0 all-reduce.8.cloned.1.call-start
  99.0 61.7 %all-reduce.14.cloned.1.call-done = (bf16[256,2048]{1,0:T(8,128)(2,1)}, bf16[256,2048]{1,0:T(8,128)(2,1)}) async-done(((bf16[256,2048]{1,0:T(8,128)(2,1)}, bf16[256,2048]{1,0:T(8,128)(2,1)}), (bf16[256,2048]{1,0:T(8,128)(2,1)}, bf16[256,2048]{1,0:T(8,128)(2,1)})) %all-reduce.14.cloned.1.call-update) | async-done | bytes 2097168 | tf_op jit(solution)/shard_map/psum | solution.py:9
  160.8 0.0 copy-start.4
  160.8 25.6 %multiply_add_fusion = f32[4096,2048]{1,0:T(8,128)} fusion(f32[4096,2048]{1,0:T(8,128)} %param.12, bf16[256,2048]{1,0:T(8,128)(2,1)} %all-gather.2.cloned.1.call-done, bf16[256,2048]{1,0:T(8,128)(2,1)} %get-tuple-element.7, bf16[256,2048]{1,0:T(8,128)(2,1)} %get-tuple-element.8), kind=kOutput, calls=%fused_computation.1 | convolution fusion | flops 4315938816 | bytes 70254592 | tf_op jit(solution)/shard_map/dot_general | solution.py:57
  186.4 0.0 copy-done.4
  186.4 18.0 %select_convert_fusion.1 = (bf16[4096,512]{1,0:T(8,128)(2,1)S(1)}, f32[4096,512]{1,0:T(8,128)}) fusion(pred[4096]{0:T(1024)(128)(4,1)S(1)} %fusion.31, f32[2,512,512]{2,1,0:T(8,128)S(1)} %copy-done.4, f32[4096,2048]{1,0:T(8,128)} %multiply_add_fusion), kind=kOutput, calls=%fused_computation.17 | convolution fusion | flops 12886999040 | bytes 22024192 | tf_op jit(solution)/shard_map/dot_general | solution.py:69
  204.4 0.0 copy-start.2
  204.4 2.0 copy-done.2
  206.5 0.9 slice_select_fusion
  207.3 0.0 all-reduce.8.cloned.1.call-update
  207.4 0.2 all-reduce.10.cloned.1.call-start
  207.6 37.6 %all-reduce.8.cloned.1.call-done = bf16[512,512]{1,0:T(8,128)(2,1)} async-done(((bf16[512,512]{1,0:T(8,128)(2,1)}), bf16[512,512]{1,0:T(8,128)(2,1)}) %all-reduce.8.cloned.1.call-update) | async-done | bytes 524304 | tf_op jit(solution)/shard_map/psum | solution.py:9
  245.2 9.5 %fusion.7 = f32[4096,512]{1,0:T(8,128)S(1)} fusion(bf16[512,512]{1,0:T(8,128)(2,1)} %all-reduce.8.cloned.1.call-done, f32[4096,512]{1,0:T(8,128)} %get-tuple-element.12, pred[4096]{0:T(1024)(128)(4,1)S(1)} %fusion.29, pred[4096]{0:T(1024)(128)(4,1)S(1)} %fusion.31), kind=kOutput, calls=%fused_computation.13 | convolution fusion | flops 12889096192 | bytes 17309696 | tf_op jit(solution)/shard_map/dot_general | solution.py:77
  254.7 0.0 copy-start.3
  254.7 16.7 %select_convert_fusion = bf16[4096,512]{1,0:T(8,128)(2,1)S(1)} fusion(f32[4096,512]{1,0:T(8,128)S(1)} %fusion.7, f32[4096,2048]{1,0:T(8,128)} %multiply_add_fusion, pred[4096]{0:T(1024)(128)(4,1)S(1)} %fusion.29, f32[2,512,512]{2,1,0:T(8,128)S(1)} %copy-done.4), kind=kOutput, calls=%fused_computation.12 | convolution fusion | flops 12891193344 | bytes 22024192 | tf_op jit(solution)/shard_map/dot_general | solution.py:69
  271.4 0.0 copy-done.3
  271.4 4.3 maximum_select_fusion
  275.8 0.0 all-reduce.10.cloned.1.call-update
  275.8 0.3 all-reduce.12.cloned.1.call-start
  276.1 125.9 %all-reduce.10.cloned.1.call-done = bf16[4096,1024]{1,0:T(8,128)(2,1)} async-done(((bf16[4096,1024]{1,0:T(8,128)(2,1)}), bf16[4096,1024]{1,0:T(8,128)(2,1)}) %all-reduce.10.cloned.1.call-update) | async-done | bytes 8388624 | tf_op jit(solution)/shard_map/psum | solution.py:9
  401.9 11.2 %convert_element_type.36 = f32[4096,1024]{1,0:T(8,128)} convert(bf16[4096,1024]{1,0:T(8,128)(2,1)} %all-reduce.10.cloned.1.call-done) | non-fusion elementwise | flops 4194304 | bytes 25165824 | tf_op jit(solution)/shard_map/convert_element_type | solution.py:82
  413.2 6.6 fusion.11
  419.8 0.0 all-reduce.12.cloned.1.call-update
  419.8 11.5 %broadcast_in_dim.81 = f32[4096,2048]{1,0:T(8,128)} broadcast(f32[]{:T(128)} %constant.29.clone.1), dimensions={} | broadcast | bytes 33554436 | tf_op jit(solution)/shard_map/jit(_where)/broadcast_in_dim | solution.py:96
  431.4 78.0 %dynamic_update_slice.3 = f32[4096,2048]{1,0:T(8,128)} dynamic-update-slice(f32[4096,2048]{1,0:T(8,128)} %broadcast_in_dim.81, f32[4096,1024]{1,0:T(8,128)} %convert_element_type.36, s32[]{:T(128)} %constant.24.clone.1, s32[]{:T(128)S(6)} %min.4) | dynamic-update-slice | bytes 33554436 | tf_op jit(solution)/shard_map/dynamic_update_slice | solution.py:92
  509.4 65.7 %all-reduce.12.cloned.1.call-done = bf16[2048,1024]{1,0:T(8,128)(2,1)} async-done(((bf16[2048,1024]{1,0:T(8,128)(2,1)}), bf16[2048,1024]{1,0:T(8,128)(2,1)}) %all-reduce.12.cloned.1.call-update) | async-done | bytes 4194320 | tf_op jit(solution)/shard_map/psum | solution.py:9
  575.0 5.2 fusion.57
  580.2 0.0 copy-start.1
  580.2 123.4 %select_select_fusion = f32[4096,2048]{1,0:T(8,128)} fusion(f32[4096,2048]{1,0:T(8,128)} %dynamic_update_slice.3, f32[4096,2048]{1,0:T(8,128)} %multiply_add_fusion, pred[2048]{0:T(1024)(128)(4,1)S(1)} %get-tuple-element.16, pred[2048]{0:T(1024)(128)(4,1)S(1)} %get-tuple-element.15, pred[4096]{0:T(1024)(128)(4,1)S(1)} %get-tuple-element.14, ...), kind=kOutput, calls=%fused_computation | convolution fusion | flops 103121158144 | bytes 117452800 | tf_op jit(solution)/shard_map/dot_general | solution.py:90
  703.6 0.0 copy-done.1
  (5 shorter events, 0.1 us)
Async XLA Ops:
  6.5 1.6 copy-start
  6.5 89.7 %all-gather.2.cloned.1.call-start = ((), (), s32[]{:S(2)}) async-start(), calls=%async_computation | async-start | bytes 1310720 | tf_op jit(solution)/shard_map/all_gather | solution.py:51
  68.5 92.2 %all-reduce.14.cloned.1.call-start = ((), (), s32[]{:S(2)}) async-start(), calls=%async_computation.4 | async-start | bytes 4194304 | tf_op jit(solution)/shard_map/psum | solution.py:9
  99.0 146.3 %all-reduce.8.cloned.1.call-start = ((), (), s32[]{:S(2)}) async-start(), calls=%async_computation.1 | async-start | bytes 1048576 | tf_op jit(solution)/shard_map/psum | solution.py:9
  160.8 25.6 %copy-start.4 = (f32[2,512,512]{2,1,0:T(8,128)S(1)}, f32[2,512,512]{2,1,0:T(8,128)}, u32[]{:S(2)}) copy-start(f32[2,512,512]{2,1,0:T(8,128)} %param.13) | copy-start | bytes 6291460
  204.4 2.0 copy-start.2
  207.4 194.6 %all-reduce.10.cloned.1.call-start = ((), (), s32[]{:S(2)}) async-start(), calls=%async_computation.2 | async-start | bytes 16777216 | tf_op jit(solution)/shard_map/psum | solution.py:9
  254.7 16.7 %copy-start.3 = (bf16[4096,512]{1,0:T(8,128)(2,1)S(1)}, bf16[4096,512]{1,0:T(8,128)(2,1)}, u32[]{:S(2)}) copy-start(bf16[4096,512]{1,0:T(8,128)(2,1)} %copy-done.2) | copy-start | bytes 12582916
  275.8 299.3 %all-reduce.12.cloned.1.call-start = ((), (), s32[]{:S(2)}) async-start(), calls=%async_computation.3 | async-start | bytes 8388608 | tf_op jit(solution)/shard_map/psum | solution.py:9
  580.2 123.4 %copy-start.1 = (bf16[1024,1024]{1,0:T(8,128)(2,1)S(1)}, bf16[1024,1024]{1,0:T(8,128)(2,1)}, u32[]{:S(2)}) copy-start(bf16[1024,1024]{1,0:T(8,128)(2,1)} %param.8) | copy-start | bytes 6291460
Sparse Core Ops, SparseCore 0:
  68.7 27.5 all-gather.1
  99.5 61.1 all-reduce.13
  207.5 37.6 all-reduce.7
  275.9 125.9 all-reduce.9
  419.9 155.1 all-reduce.11
where the time goes:
time: 712 us; the launch traced here: 710 us
  waiting for transfers between devices  319 us (45%)
  matrix products  198 us (28%)
  local copies, waits for them, and re-layouts  94.8 us (13%)
  blocking collectives  52.8 us (7%)
  other arithmetic  32 us (4%)
  between operations  13.3 us (2%)
    psum x4, waiting for transfers between devices, spread_2(): return lax.psum(jnp.where(mine, array, jnp.zeros_like(array)), axis)  291 us
    dot_general x1, matrix products, per_device(): jnp.dot(lower_part, upper_part.T, precision=lax.Precision.HIGHEST)  123 us
    dynamic_update_slice x1, local copies, waits for them, and re-layouts, per_device(): lax.dynamic_update_slice(jnp.zeros_like(current), row_panel, (jnp.int32(0...  78 us
    psum x1, blocking collectives, per_device(): summed_act, summed_err = lax.psum((part_act, part_err), 'col')  52.8 us
    dot_general x2, matrix products, apply_inverse(): result = jnp.dot(columns, inverse.T, precision=lax.Precision.HIGHEST)  34.7 us
    all_gather x1, waiting for transfers between devices, per_device(): col_grads = lax.all_gather(local_grads, 'row', axis=0, tiled=True)  27.7 us
    dot_general x1, matrix products, per_device(): lax.dot_general(row_grads, col_grads, (((0,), (0,)), ((), ())), preferred...  25.6 us
    select_n x4, other arithmetic, spread_2(): return lax.psum(jnp.where(mine, array, jnp.zeros_like(array)), axis)  14.4 us
  transfers between devices with their start and end apart: 5, of which 5 were waited for; matrix products, arithmetic and copies ran while one was open for 13% of the time, Pallas kernels for 0%

commit v1 on v0

v1 whole, which is shorter than its diff:
```python
import functools

import jax
import jax.numpy as jnp
from jax import lax
from jax.experimental import pallas as pl
from jax.experimental.pallas import tpu as pltpu
from jax.sharding import PartitionSpec as P


BF16 = jnp.bfloat16
F32 = jnp.float32
PLANE_CHUNKS = 4
LINE_CHUNKS = 8
CHAINS = 2
CALLS = ((0, 1, 2, 3), (4, 5, 6, 7))
SPLITS = (((0,), (1,)), ((0, 1),))
ROW_BLOCK = 512


def xor_pairs(count, bit):
    return [(i, i ^ bit) for i in range(count)]


def dot(a, b, contract):
    return lax.dot_general(a, b, (contract, ((), ())), preferred_element_type=F32)


def grads_kernel(
    sizes, info, own_ref, recv_ref, start_ref, end_ref, row_ref, col_ref, panel_ref, err_t
):
    half_pieces, piece, width, col_bits = sizes
    tokens = 2 * half_pieces * piece
    acts = []
    for index in range(2 * half_pieces):
        source = own_ref if index < half_pieces else recv_ref
        both = source[index % half_pieces, 0]
        acts.append(both[:, :width])
        err_t[:, index * piece : (index + 1) * piece] = both[:, width:].astype(F32).T
    act = jnp.concatenate(acts, axis=0)
    lane = lax.broadcasted_iota(jnp.int32, (1, tokens), 1)
    place = lane // piece
    position = lane % piece
    for k in range(col_bits):
        mine = (info[2] >> (col_bits - 1 - k)) & 1
        position = position + (mine ^ ((place >> k) & 1)) * (tokens >> (col_bits - k))
    member = (position >= start_ref[0]) & (position < end_ref[0])
    captions = member.shape[0]

    def fill(out_ref, first):
        for group in range(out_ref.shape[1] // (8 * width)):
            base = first + group * 8
            if not isinstance(base, int):
                base = pl.multiple_of(base, 8)
            rows = err_t[pl.ds(base, 8), :]
            weighted = [
                jnp.where(member, rows[k : k + 1, :], 0.0).astype(BF16) for k in range(8)
            ]
            summed = dot(jnp.concatenate(weighted, axis=0), act, ((1,), (0,)))
            for k in range(8):
                column = (group * 8 + k) * width
                out_ref[:, column : column + width] = summed[
                    k * captions : (k + 1) * captions
                ].astype(BF16)

    fill(row_ref, info[4])
    fill(col_ref, info[5])
    fill(panel_ref, 0)


def all_grads(info, own, recv, starts, ends, half_rows, tile_cols, stop, width, col_bits):
    half_pieces, groups, piece, both = own.shape
    captions = starts.shape[1]
    sizes = (half_pieces, piece, width, col_bits)
    pieces = pl.BlockSpec((half_pieces, 1, piece, both), lambda a, info: (0, a, 0, 0))
    bounds = pl.BlockSpec((1, captions, 1), lambda a, info: (a, 0, 0))
    outs = [half_rows, tile_cols, stop]
    total = sum(outs) // width
    return pl.pallas_call(
        functools.partial(grads_kernel, sizes),
        grid_spec=pltpu.PrefetchScalarGridSpec(
            num_scalar_prefetch=1,
            grid=(groups,),
            in_specs=[pieces, pieces, bounds, bounds],
            out_specs=[pl.BlockSpec((captions, n), lambda a, info: (a, 0)) for n in outs],
            scratch_shapes=[pltpu.VMEM((width, 2 * half_pieces * piece), F32)],
        ),
        out_shape=[jax.ShapeDtypeStruct((groups * captions, n), BF16) for n in outs],
        cost_estimate=pl.CostEstimate(
            flops=4 * groups * total * captions * 2 * half_pieces * piece * width,
            bytes_accessed=2 * own.size * 2 + 2 * groups * captions * sum(outs),
            transcendentals=0,
        ),
        name="grads",
    )(info, own, recv, starts, ends)


def row_panel_kernel(sizes, info, inverse_ref, panel_grads, row_grads, *refs):
    chunks, options, rows, pivot_rows, scale = sizes
    sources = refs[: chunks * options]
    out_ref, pivot_ref, held, sem = refs[chunks * options :]
    width = inverse_ref.shape[1]
    step = rows // chunks
    turn = pl.program_id(0)

    def target(chunk):
        extra = pivot_rows if chunk == chunks - 1 else 0
        return held.at[pl.ds(chunk * step, step + extra)]

    def wait(chunk):
        pltpu.make_async_copy(sources[chunk * options], target(chunk), sem.at[chunk]).wait()

    @pl.when(turn == 0)
    def _():
        for chunk in reversed(range(chunks)):
            for option in range(options):

                @pl.when(info[3] == option)
                def _():
                    pltpu.make_async_copy(
                        sources[chunk * options + option], target(chunk), sem.at[chunk]
                    ).start()

        wait(chunks - 1)
        grads = panel_grads[...]
        packed = held[rows : rows + pivot_rows, :]
        pivot = jnp.concatenate([packed[:, :width], packed[:, width:]], axis=0).astype(F32)
        pivot = pivot + scale * dot(grads[:, width:], grads[:, :width], ((0,), (0,)))
        pivot = dot(pivot.astype(BF16), inverse_ref[0], ((1,), (1,))).astype(BF16)
        pivot_ref[...] = pivot

    for chunk in range(chunks - 1):

        @pl.when(turn == chunk)
        def _():
            wait(chunk)

    at = pl.multiple_of(turn * step, step)
    mine = row_grads[...].T
    start = held[pl.ds(at, step), :].astype(F32)
    both = start + scale * dot(mine, panel_grads[...], ((1,), (0,)))
    first = dot(both[:, :width].astype(BF16), inverse_ref[0], ((1,), (1,))).astype(BF16)
    second = both[:, width:] - dot(first, pivot_ref[...], ((1,), (1,)))
    second = dot(second.astype(BF16), inverse_ref[1], ((1,), (1,)))
    ids = info[6] + at + lax.broadcasted_iota(jnp.int32, second.shape, 0)
    out_ref[:, :width] = first
    out_ref[:, width : 2 * width] = jnp.where(ids >= width, second, 0.0).astype(BF16)
    out_ref[:, 2 * width :] = mine


def row_panel(info, inverse, panel_grads, row_grads, pieces, scale):
    chunks, options = len(pieces), len(pieces[0])
    captions, rows = row_grads.shape
    stop = panel_grads.shape[1]
    width = stop // 2
    step = rows // chunks
    pivot_rows = pieces[-1][0].shape[0] - pieces[0][0].shape[0]
    whole = pl.BlockSpec(memory_space=pltpu.VMEM)
    return pl.pallas_call(
        functools.partial(row_panel_kernel, (chunks, options, rows, pivot_rows, scale)),
        grid=(chunks,),
        in_specs=[
            pl.BlockSpec(memory_space=pltpu.SMEM),
            whole,
            whole,
            pl.BlockSpec((captions, step), lambda s: (0, s)),
        ]
        + [pl.BlockSpec(memory_space=pl.ANY)] * (chunks * options),
        out_specs=[
            pl.BlockSpec((step, stop + captions), lambda s: (s, 0)),
            pl.BlockSpec((width, width), lambda s: (0, 0)),
        ],
        out_shape=[
            jax.ShapeDtypeStruct((rows, stop + captions), BF16),
            jax.ShapeDtypeStruct((width, width), BF16),
        ],
        scratch_shapes=[
            pltpu.VMEM((rows + pivot_rows, stop), BF16),
            pltpu.SemaphoreType.DMA((chunks,)),
        ],
        cost_estimate=pl.CostEstimate(
            flops=2 * rows * (stop * captions + 3 * width * width),
            bytes_accessed=4 * rows * stop + 2 * captions * (rows + stop),
            transcendentals=0,
        ),
        name="row_panel",
    )(info, inverse, panel_grads, row_grads, *[p for piece in pieces for p in piece])


def col_panel_kernel(sizes, info, inverse_ref, pivot_ref, panel_grads, col_grads, *refs):
    chunks, options, scale = sizes
    sources = refs[: chunks * options]
    out_ref, held, sem = refs[chunks * options :]
    width = inverse_ref.shape[1]
    step = out_ref.shape[1] // chunks

    def target(chunk):
        return held.at[:, pl.ds(chunk * step, step)]

    for chunk in range(chunks):
        for option in range(options):

            @pl.when(info[1] == option)
            def _():
                pltpu.make_async_copy(
                    sources[chunk * options + option], target(chunk), sem.at[chunk]
                ).start()

    grads = panel_grads[...]
    first_inverse, second_inverse = inverse_ref[0], inverse_ref[1]
    for chunk in range(chunks):
        pltpu.make_async_copy(sources[chunk * options], target(chunk), sem.at[chunk]).wait()

    mine = col_grads[...]
    both = held[...].astype(F32) + scale * dot(grads, mine, ((0,), (0,)))
    first = dot(first_inverse, both[:width].astype(BF16), ((1,), (0,))).astype(BF16)
    second = both[width:] - dot(pivot_ref[...], first, ((1,), (0,)))
    second = dot(second_inverse, second.astype(BF16), ((1,), (0,))).astype(BF16)
    out_ref[:width] = -first
    out_ref[width : 2 * width] = -second
    out_ref[2 * width :] = (mine.astype(F32) * scale).astype(BF16)


def col_panel(info, inverse, pivot, panel_grads, col_grads, pieces, first_col, scale):
    chunks, options = len(pieces), len(pieces[0])
    stop, step = pieces[0][0].shape
    captions = col_grads.shape[0]
    width = stop // 2
    whole = pl.BlockSpec(memory_space=pltpu.VMEM)
    columns = chunks * step
    return pl.pallas_call(
        functools.partial(col_panel_kernel, (chunks, options, scale)),
        grid=(1,),
        in_specs=[pl.BlockSpec(memory_space=pltpu.SMEM)]
        + [whole] * 3
        + [pl.BlockSpec((captions, columns), lambda s: (0, first_col // columns))]
        + [pl.BlockSpec(memory_space=pl.ANY)] * (chunks * options),
        out_specs=whole,
        out_shape=jax.ShapeDtypeStruct((stop + captions, columns), BF16),
        scratch_shapes=[
            pltpu.VMEM((stop, columns), BF16),
            pltpu.SemaphoreType.DMA((chunks,)),
        ],
        cost_estimate=pl.CostEstimate(
            flops=2 * columns * (stop * captions + 3 * width * width),
            bytes_accessed=4 * columns * stop + 2 * captions * (columns + stop),
            transcendentals=0,
        ),
        name="col_panel",
    )(info, inverse, pivot, panel_grads, col_grads, *[p for piece in pieces for p in piece])


def update_kernel(sizes, info, mine, other, right, ridge_ref, *refs):
    first_col, stop, base, blocks = sizes
    out_ref = refs[-1]
    step = pl.program_id(0) + base
    block, columns = out_ref.shape
    inside = max(0, min(columns, stop - first_col))

    def write(left):
        which = step // blocks
        row = info[7] + ((info[0] ^ which) * blocks + step - which * blocks) * block
        panel_part = jnp.logical_and(info[2] == 0, inside > 0)

        @pl.when(jnp.logical_and(row >= stop, jnp.logical_not(panel_part & (inside == columns))))
        def _():
            out_ref[...] = ridge_ref[...] + dot(left[...], right[...], ((1,), (0,)))

        @pl.when(row < stop)
        def _():
            out_ref[...] = jnp.zeros_like(out_ref)

        if inside:

            @pl.when(panel_part)
            def _():
                out_ref[:, :inside] = left[:, first_col : first_col + inside].astype(F32)

    @pl.when(step < blocks)
    def _():
        write(mine)

    @pl.when(step >= blocks)
    def _():
        write(other)


def update(info, out, mine, other, right, ridge, first_col, stop, halves):
    depth, columns = right.shape
    half_rows = mine.shape[0]
    block = min(ROW_BLOCK, half_rows)
    blocks = half_rows // block
    at = first_col // columns
    assert at * columns == first_col and stop % block == 0

    base = halves[0] * blocks

    def rows_of(step, info):
        which = (step + base) // blocks
        return (info[0] ^ which) * blocks + step + base - which * blocks

    tile = pl.BlockSpec((block, columns), lambda s, i: (rows_of(s, i), at))
    specs = [
        pl.BlockSpec((block, depth), lambda s, i: (jnp.minimum(s + base, blocks - 1), 0)),
        pl.BlockSpec((block, depth), lambda s, i: (jnp.maximum(s + base - blocks, 0), 0)),
        pl.BlockSpec((depth, columns), lambda s, i: (0, 0)),
        tile,
    ]
    operands = [mine, other, right, ridge]
    aliases = {}
    if out is not None:
        specs.append(pl.BlockSpec(memory_space=pl.ANY))
        operands.append(out)
        aliases = {len(operands): 0}
    rows = len(halves) * half_rows
    return pl.pallas_call(
        functools.partial(update_kernel, (first_col, stop, base, blocks)),
        grid_spec=pltpu.PrefetchScalarGridSpec(
            num_scalar_prefetch=1, grid=(len(halves) * blocks,), in_specs=specs, out_specs=tile
        ),
        out_shape=jax.ShapeDtypeStruct(ridge.shape, F32),
        input_output_aliases=aliases,
        cost_estimate=pl.CostEstimate(
            flops=2 * rows * columns * depth,
            bytes_accessed=8 * rows * columns + 2 * depth * (rows + columns),
            transcendentals=0,
        ),
        name="update",
    )(info, *operands)


def chunk_kernel(boxes, who, info, ridge_ref, *refs):
    count = len(boxes)
    wide, narrow, in_sem, out_sem = refs[-4:]
    outs = refs[-4 - count : -4]
    extra = refs[0] if len(refs) > count + 4 else None
    rows, columns = wide.shape[1:]

    @pl.when(info[who] == 0)
    def _():
        loads, stores = [], []
        for k, (row, column) in enumerate(boxes):
            source = ridge_ref.at[pl.ds(row, rows), pl.ds(column, columns)]
            loads.append([pltpu.make_async_copy(source, wide.at[k], in_sem.at[k])])
            if extra is not None:
                target = narrow.at[k, pl.ds(rows, outs[k].shape[0] - rows)]
                loads[k].append(pltpu.make_async_copy(extra, target, in_sem.at[count + k]))
            for load in loads[k]:
                load.start()
        for k in range(count):
            for load in loads[k]:
                load.wait()
            narrow[k, :rows] = wide[k].astype(BF16)
            stores.append(pltpu.make_async_copy(narrow.at[k], outs[k], out_sem.at[k]))
            stores[k].start()
        for store in stores:
            store.wait()


def chunks_of(info, ridge, boxes, shape, who, extra=None):
    count = len(boxes)
    rows, columns = shape
    total = rows + (0 if extra is None else extra.shape[0])
    place = pl.BlockSpec(memory_space=pl.ANY)
    operands = [ridge] if extra is None else [ridge, extra]
    return pl.pallas_call(
        functools.partial(chunk_kernel, boxes, who),
        in_specs=[pl.BlockSpec(memory_space=pltpu.SMEM)] + [place] * len(operands),
        out_specs=[place] * count,
        out_shape=[jax.ShapeDtypeStruct((total, columns), BF16)] * count,
        scratch_shapes=[
            pltpu.VMEM((count, rows, columns), F32),
            pltpu.VMEM((count, total, columns), BF16),
            pltpu.SemaphoreType.DMA((2 * count,)),
            pltpu.SemaphoreType.DMA((count,)),
        ],
        cost_estimate=pl.CostEstimate(
            flops=0, bytes_accessed=6 * count * rows * columns, transcendentals=0
        ),
        name="chunks",
    )(info, *operands)


def gray_order(count):
    forward = [i ^ (i >> 1) for i in range(count)]
    return forward, [forward[0]] + forward[:0:-1]


def per_device(activations, errors, act_proj, err_proj, lengths, ridge, pivot_inverse):
    col_count, row_count = lax.axis_size("col"), lax.axis_size("row")
    col_idx, row_idx = lax.axis_index("col"), lax.axis_index("row")
    core = col_idx & 1
    tile_rows, tile_cols = ridge.shape
    half_rows = tile_rows // 2
    width = pivot_inverse.shape[1]
    stop = 2 * width
    proj_width = act_proj.shape[1]
    captions = lengths.shape[1]
    scale = 1.0 / (captions * row_count)
    inverse = pivot_inverse.astype(BF16)

    pairs = col_count // 2
    orders = gray_order(pairs)
    depth = jnp.int32(0)
    for c, order in enumerate(orders):
        for d, pair in enumerate(order):
            depth = jnp.where(col_idx == 2 * pair + c, d, depth)

    row_err = (row_idx * tile_rows + core * half_rows) // proj_width
    col_err = (col_idx * tile_cols) // proj_width
    facts = [
        core,
        row_idx,
        col_idx,
        depth,
        row_err,
        col_err,
        row_idx * tile_rows + core * half_rows,
        row_idx * tile_rows,
    ]
    slot = jnp.arange(len(facts), dtype=jnp.int32)
    info = jnp.zeros_like(slot)
    for k, fact in enumerate(facts):
        info = jnp.where(slot == k, fact, info)

    boxes = [(width, 0), (width + width // 2, 0)]
    pivot = chunks_of(info, ridge, boxes, (width // 2, width), 2)
    pivot = jnp.concatenate(pivot, axis=1)
    sent = []
    for z in range(1, row_count):
        sent.append(lax.ppermute(pivot, ("row", "col"), [(0, z * col_count)]))
    pivot = jnp.where(row_idx == 0, pivot, functools.reduce(jnp.add, sent))

    line_step = tile_cols // LINE_CHUNKS
    steps = LINE_CHUNKS + CHAINS * (row_count - 2)
    arrived, source, first = [], [], []
    for ns in (range(CHAINS), range(CHAINS, LINE_CHUNKS)):
        boxes = [(0, n * line_step) for n in ns]
        first += chunks_of(info, ridge, boxes, (stop, line_step), 1)
    for k in range(steps):
        if k >= LINE_CHUNKS:
            piece = arrived[k - CHAINS]
        elif k >= CHAINS:
            piece = jnp.where(row_idx == 0, first[k], arrived[k - CHAINS])
        else:
            piece = first[k]
        source.append(piece)
        arrived.append(lax.ppermute(piece, "row", [(z - 1, z) for z in range(1, row_count)]))
    line = [
        [source[n]] + [arrived[n + CHAINS * (z - 1)] for z in range(1, row_count)]
        for n in range(LINE_CHUNKS)
    ]

    plane_step = half_rows // PLANE_CHUNKS
    plane = []
    last = PLANE_CHUNKS - 1
    made = {}
    for name, ns in (("a", (0,)), ("b", tuple(range(1, last))), ("c", (last,))):
        boxes = [(half_rows + n * plane_step, 0) for n in ns]
        boxes += [(n * plane_step, 0) for n in ns]
        extra = pivot if name == "c" else None
        got = chunks_of(info, ridge, boxes, (plane_step, stop), 2, extra)
        for k, n in enumerate(ns):
            made[n] = (got[k], got[len(ns) + k])
    for n in range(PLANE_CHUNKS):
        other, own = made[n]
        other = lax.ppermute(other, "col", [(0, 1)])
        hops = [jnp.where(col_idx == 1, other, own)]
        for d in range(1, pairs):
            perm = [(2 * o[d - 1] + c, 2 * o[d] + c) for c, o in enumerate(orders)]
            hops.append(lax.ppermute(hops[-1], "col", perm))
        plane.append(hops)

    all_lengths = lengths
    for k in range(row_count.bit_length() - 1):
        got = lax.ppermute(all_lengths, "row", xor_pairs(row_count, 1 << k))
        all_lengths = jnp.concatenate([all_lengths, got], axis=0)
    before = jnp.arange(captions)[:, None] < jnp.arange(captions)[None, :]
    starts = jnp.sum(jnp.where(before[None], all_lengths[:, :, None], 0), axis=1)
    ends = (starts + all_lengths)[:, :, None]
    starts = starts[:, :, None]

    total = jnp.concatenate(
        [
            jnp.dot(activations, act_proj, preferred_element_type=F32),
            jnp.dot(errors, err_proj, preferred_element_type=F32),
        ],
        axis=1,
    )
    col_bits = col_count.bit_length() - 1
    for k in range(col_bits):
        half = total.shape[0] // 2
        upper = ((col_idx >> k) & 1) == 1
        low, high = total[:half], total[half:]
        send = jnp.where(upper, low, high)
        keep = jnp.where(upper, high, low)
        got = lax.ppermute(send, "col", xor_pairs(col_count, 1 << k))
        total = keep + got
    held = total.astype(BF16)[None, None]
    for k in range(row_count.bit_length() - 1):
        got = lax.ppermute(held, "row", xor_pairs(row_count, 1 << k))
        held = jnp.concatenate([held, got], axis=1)
    for k in reversed(range(col_bits)):
        got = lax.ppermute(held, "col", xor_pairs(col_count, 1 << k))
        if k:
            held = jnp.concatenate([held, got], axis=0)

    row_grads, col_grads, panel_grads = all_grads(
        info, held, got, starts, ends, half_rows, tile_cols, stop, proj_width, col_bits
    )
    mine, pivot_panel = row_panel(info, inverse, panel_grads, row_grads, plane, scale)
    other = lax.ppermute(mine, "col", xor_pairs(col_count, 1))

    out = None
    for index, call in enumerate(CALLS):
        first_col = call[0] * line_step
        pieces = [line[n] for n in call]
        right = col_panel(
            info,
            inverse,
            pivot_panel,
            panel_grads,
            col_grads,
            pieces,
            first_col,
            scale,
        )
        for halves in SPLITS[index]:
            rest = other if 1 in halves else mine
            out = update(info, out, mine, rest, right, ridge, first_col, stop, halves)
    return out


def solution(mesh):
    in_specs = (
        P("row", "col"),
        P("row", "col"),
        P("col", None),
        P("col", None),
        P("row", None),
        P("row", "col"),
        P(),
    )

    return jax.shard_map(
        per_device, mesh=mesh, in_specs=in_specs, out_specs=P("row", "col"), check_vma=False
    )
```

time: 712 us -> 389 us (0.55)
  the two profiles are of different devices: /device:TPU:0 before, /device:TPU:10 now
where the time goes in v1:
time: 389 us; the launch traced here: 388 us
  waiting for transfers between devices  152 us (39%)
  starting transfers between devices  131 us (34%)
  Pallas kernels  87.2 us (22%)
  other arithmetic  9.68 us (2%)
    ppermute x12, waiting for transfers between devices, per_device(): lax.ppermute(piece, 'row', [(z - 1, z) for z in range(1, row_count)])  90.5 us
    pallas_call x3, Pallas kernels, update(): pl.pallas_call(functools.partial(update_kernel, (first_col, stop, base, b...  48.7 us
    ppermute x12, starting transfers between devices, per_device(): lax.ppermute(piece, 'row', [(z - 1, z) for z in range(1, row_count)])  40.8 us
    ppermute x3, starting transfers between devices, per_device(): got = lax.ppermute(send, 'col', xor_pairs(col_count, 1 << k))  38.2 us
    ppermute x12, waiting for transfers between devices, per_device(): hops.append(lax.ppermute(hops[-1], 'col', perm))  29.7 us
    ppermute x12, starting transfers between devices, per_device(): hops.append(lax.ppermute(hops[-1], 'col', perm))  21.6 us
    ppermute x1, starting transfers between devices, per_device(): other = lax.ppermute(mine, 'col', xor_pairs(col_count, 1))  19.7 us
    ppermute x3, waiting for transfers between devices, per_device(): got = lax.ppermute(held, 'col', xor_pairs(col_count, 1 << k))  16.3 us
  transfers between devices with their start and end apart: 42, of which 22 were waited for; matrix products, arithmetic and copies ran while one was open for 3% of the time, Pallas kernels for 10%

profile of v1, /device:TPU:10, one launch (start us, length us, event | category | flops | bytes accessed | tf_op | source)
XLA Modules:
  0.0 387.5 jit_solution(1282014188245157590)
XLA Ops:
  4.1 1.5 collective-permute-start.23
  5.5 1.5 collective-permute-start.22
  7.0 2.1 add_select_fusion.refs_0_
  10.0 2.0 collective-permute-start.25
  12.7 2.3 fusion.3
  15.9 1.7 collective-permute-start.10
  18.4 1.6 collective-permute-start.14
  20.2 38.1 %collective-permute-start.1 = (f32[256,256]{1,0:T(8,128)S(1)}, f32[256,256]{1,0:T(8,128)S(1)}, u32[]{:S(2)}, u32[]{:S(2)}) collective-permute-start(f32[256,256]{1,0:T(8,128)S(1)} %slice_select_fusion), channel_id=1, source_target_pairs={{0,2},{1,3},{2,0},{3,1},{4,6},{5,7},{6,4},{7,5},{8,10},{9,11},{10,... | collective-permute-start | bytes 786440 | tf_op jit(solution)/shard_map/ppermute | solution.py:497
  58.3 1.6 broadcast_select_fusion.refs_12_
  59.9 1.3 collective-permute-start.26
  61.2 1.7 collective-permute-start.18
  63.0 1.4 broadcast_select_fusion.3.refs_0_
  64.5 1.4 collective-permute-start.11
  66.1 1.3 collective-permute-start.15
  67.6 1.3 collective-permute-start.19
  68.9 13.4 %collective-permute-done.26.refs_13_ = bf16[768,1024]{1,0:T(8,128)(2,1)} collective-permute-done((bf16[768,1024]{1,0:T(8,128)(2,1)S(1)}, bf16[768,1024]{1,0:T(8,128)(2,1)}, u32[]{:S(2)}, u32[]{:S(2)}) %collective-permute-start.26) | collective-permute-done | bytes 1572896 | tf_op jit(solution)/shard_map/ppermute | solution.py:471
  82.3 2.4 collective-permute-start.27
  84.9 4.3 %collective-permute-done.3 = bf16[1,1,128,256]{3,2,1,0:T(8,128)(2,1)S(1)} collective-permute-done((bf16[1,1,128,256]{3,2,1,0:T(8,128)(2,1)S(1)}, bf16[1,1,128,256]{3,2,1,0:T(8,128)(2,1)S(1)}, u32[]{:S(2)}, u32[]{:S(2)}) %collective-permute-start.3) | collective-permute-done | bytes 65568 | tf_op jit(solution)/shard_map/ppermute | solution.py:501
  89.2 5.9 %collective-permute-done.4 = bf16[1,2,128,256]{3,2,1,0:T(8,128)(2,1)S(1)} collective-permute-done((bf16[1,2,128,256]{3,2,1,0:T(8,128)(2,1)S(1)}, bf16[1,2,128,256]{3,2,1,0:T(8,128)(2,1)S(1)}, u32[]{:S(2)}, u32[]{:S(2)}) %collective-permute-start.4) | collective-permute-done | bytes 131104 | tf_op jit(solution)/shard_map/ppermute | solution.py:501
  95.2 9.3 %collective-permute-done.5 = bf16[1,4,128,256]{3,2,1,0:T(8,128)(2,1)S(1)} collective-permute-done((bf16[1,4,128,256]{3,2,1,0:T(8,128)(2,1)S(1)}, bf16[1,4,128,256]{3,2,1,0:T(8,128)(2,1)S(1)}, u32[]{:S(2)}, u32[]{:S(2)}) %collective-permute-start.5) | collective-permute-done | bytes 262176 | tf_op jit(solution)/shard_map/ppermute | solution.py:504
  104.6 3.5 collective-permute-done.8
  108.1 4.4 %collective-permute-start.12 = (bf16[512,1024]{1,0:T(8,128)(2,1)}, bf16[512,1024]{1,0:T(8,128)(2,1)S(1)}, u32[]{:S(2)}, u32[]{:S(2)}) collective-permute-start(bf16[512,1024]{1,0:T(8,128)(2,1)} %collective-permute-done.11.refs_1_), channel_id=1, source_target_pairs={{2,6},{5,7},{10,14},{13,15},{18,22},{21,23},{26,30},{29,31}} | collective-permute-start | bytes 3145736 | tf_op jit(solution)/shard_map/ppermute | solution.py:471
  112.6 2.3 collective-permute-start.16
  114.8 3.0 collective-permute-done.19.refs_9_
  117.8 2.3 collective-permute-start.20
  120.1 7.0 %collective-permute-done.6 = bf16[2,4,128,256]{3,2,1,0:T(8,128)(2,1)S(1)} collective-permute-done((bf16[2,4,128,256]{3,2,1,0:T(8,128)(2,1)S(1)}, bf16[2,4,128,256]{3,2,1,0:T(8,128)(2,1)S(1)}, u32[]{:S(2)}, u32[]{:S(2)}) %collective-permute-start.6) | collective-permute-done | bytes 524320 | tf_op jit(solution)/shard_map/ppermute | solution.py:504
  127.1 1.8 collective-permute-start.28
  129.0 1.1 pad_maximum_fusion.own_ref
  130.1 1.5 collective-permute-done.9
  131.7 1.1 convert_element_type.6.inverse_ref
  133.6 2.8 collective-permute-done.16.refs_6_
  137.1 10.5 %collective-permute-done.20.refs_10_ = bf16[512,1024]{1,0:T(8,128)(2,1)} collective-permute-done((bf16[512,1024]{1,0:T(8,128)(2,1)}, bf16[512,1024]{1,0:T(8,128)(2,1)}, u32[]{:S(2)}, u32[]{:S(2)}) %collective-permute-start.20) | collective-permute-done | bytes 1048608 | tf_op jit(solution)/shard_map/ppermute | solution.py:471
  147.6 1.6 collective-permute-start.21
  150.4 9.3 %grads.1 = (bf16[256,2048]{1,0:T(8,128)(2,1)}, bf16[256,2048]{1,0:T(8,128)(2,1)}, bf16[256,1024]{1,0:T(8,128)(2,1)}) custom-call(s32[8]{0:T(128)} %compare_select_fusion.7.info, bf16[4,4,128,256]{3,2,1,0:T(8,128)(2,1)} %pad_maximum_fusion.own_ref, bf16[4,4,128,256]{3,2,1,0:T(8,128)(2,1)} %collective-permute-done.7.recv_ref, s32[4,64,1]{2,1,0:T(8,128)} %copy-done.28, ...), custom_call_target="tpu_custom_call" | custom-call | flops 5368709120 | bytes 4718592 | tf_op jit(solution)/shard_map/grads/pallas_call | solution.py:79
  161.0 10.2 %row_panel.1 = (bf16[2048,1280]{1,0:T(8,128)(2,1)}, bf16[512,512]{1,0:T(8,128)(2,1)}) custom-call(s32[8]{0:T(128)} %compare_select_fusion.7.info, bf16[2,512,512]{2,1,0:T(8,128)(2,1)} %convert_element_type.6.inverse_ref, bf16[256,1024]{1,0:T(8,128)(2,1)} %get-tuple-element.28.panel_grads, bf16[256,2048]{1,0:T(8,128)(2,1)} %get-tuple-element.29.row_grads, ...), custom_call_target="tpu_custom_call" | custom-call | flops 4294967296 | bytes 9961472 | tf_op jit(solution)/shard_map/row_panel/pallas_call | solution.py:159
  171.2 19.7 %collective-permute-start.29 = (bf16[2048,1280]{1,0:T(8,128)(2,1)}, bf16[2048,1280]{1,0:T(8,128)(2,1)}, u32[]{:S(2)}, u32[]{:S(2)}) collective-permute-start(bf16[2048,1280]{1,0:T(8,128)(2,1)} %get-tuple-element.40.mine.other), channel_id=1, source_target_pairs={{0,1},{1,0},{2,3},{3,2},{4,5},{5,4},{6,7},{7,6},{8,9},{9,8},{10,11... | collective-permute-start | bytes 15728648 | tf_op jit(solution)/shard_map/ppermute | solution.py:512
  191.7 3.4 collective-permute-start.35
  195.1 3.6 collective-permute-start.30
  199.6 9.1 %collective-permute-done.35.refs_5_ = bf16[1024,256]{1,0:T(8,128)(2,1)S(1)} collective-permute-done((bf16[1024,256]{1,0:T(8,128)(2,1)}, bf16[1024,256]{1,0:T(8,128)(2,1)S(1)}, u32[]{:S(2)}, u32[]{:S(2)}) %collective-permute-start.35) | collective-permute-done | bytes 524320 | tf_op jit(solution)/shard_map/ppermute | solution.py:448
  208.7 3.5 collective-permute-start.36
  212.2 7.7 %collective-permute-done.30.refs_1_ = bf16[1024,256]{1,0:T(8,128)(2,1)S(1)} collective-permute-done((bf16[1024,256]{1,0:T(8,128)(2,1)}, bf16[1024,256]{1,0:T(8,128)(2,1)S(1)}, u32[]{:S(2)}, u32[]{:S(2)}) %collective-permute-start.30) | collective-permute-done | bytes 524320 | tf_op jit(solution)/shard_map/ppermute | solution.py:448
  219.9 3.5 collective-permute-start.31
  223.4 7.7 %collective-permute-done.36.refs_6_.refs_13_ = bf16[1024,256]{1,0:T(8,128)(2,1)S(1)} collective-permute-done((bf16[1024,256]{1,0:T(8,128)(2,1)S(1)}, bf16[1024,256]{1,0:T(8,128)(2,1)S(1)}, u32[]{:S(2)}, u32[]{:S(2)}) %collective-permute-start.36) | collective-permute-done | bytes 524320 | tf_op jit(solution)/shard_map/ppermute | solution.py:448
  231.2 3.5 collective-permute-start.37
  234.6 7.7 %collective-permute-done.31.refs_2_.refs_9_ = bf16[1024,256]{1,0:T(8,128)(2,1)S(1)} collective-permute-done((bf16[1024,256]{1,0:T(8,128)(2,1)S(1)}, bf16[1024,256]{1,0:T(8,128)(2,1)S(1)}, u32[]{:S(2)}, u32[]{:S(2)}) %collective-permute-start.31) | collective-permute-done | bytes 524320 | tf_op jit(solution)/shard_map/ppermute | solution.py:448
  242.4 3.3 collective-permute-start.32
  245.7 7.8 %collective-permute-done.37.refs_5_.refs_7_.refs_14_ = bf16[1024,256]{1,0:T(8,128)(2,1)S(1)} collective-permute-done((bf16[1024,256]{1,0:T(8,128)(2,1)S(1)}, bf16[1024,256]{1,0:T(8,128)(2,1)S(1)}, u32[]{:S(2)}, u32[]{:S(2)}) %collective-permute-start.37) | collective-permute-done | bytes 524320 | tf_op jit(solution)/shard_map/ppermute | solution.py:448
  253.7 3.3 collective-permute-start.38
  257.0 7.8 %collective-permute-done.32.refs_1_.refs_3_.refs_10_ = bf16[1024,256]{1,0:T(8,128)(2,1)S(1)} collective-permute-done((bf16[1024,256]{1,0:T(8,128)(2,1)S(1)}, bf16[1024,256]{1,0:T(8,128)(2,1)S(1)}, u32[]{:S(2)}, u32[]{:S(2)}) %collective-permute-start.32) | collective-permute-done | bytes 524320 | tf_op jit(solution)/shard_map/ppermute | solution.py:448
  264.9 3.3 collective-permute-start.33
  268.2 7.8 %collective-permute-done.38.refs_6_.refs_13_.refs_15_ = bf16[1024,256]{1,0:T(8,128)(2,1)S(1)} collective-permute-done((bf16[1024,256]{1,0:T(8,128)(2,1)S(1)}, bf16[1024,256]{1,0:T(8,128)(2,1)S(1)}, u32[]{:S(2)}, u32[]{:S(2)}) %collective-permute-start.38) | collective-permute-done | bytes 524320 | tf_op jit(solution)/shard_map/ppermute | solution.py:448
  276.0 3.5 collective-permute-start.39
  279.5 7.7 %collective-permute-done.33.refs_2_.refs_9_.refs_11_ = bf16[1024,256]{1,0:T(8,128)(2,1)S(1)} collective-permute-done((bf16[1024,256]{1,0:T(8,128)(2,1)S(1)}, bf16[1024,256]{1,0:T(8,128)(2,1)S(1)}, u32[]{:S(2)}, u32[]{:S(2)}) %collective-permute-start.33) | collective-permute-done | bytes 524320 | tf_op jit(solution)/shard_map/ppermute | solution.py:448
  287.3 3.3 collective-permute-start.34
  290.6 7.9 %collective-permute-done.39.refs_7_.refs_14_ = bf16[1024,256]{1,0:T(8,128)(2,1)S(1)} collective-permute-done((bf16[1024,256]{1,0:T(8,128)(2,1)S(1)}, bf16[1024,256]{1,0:T(8,128)(2,1)S(1)}, u32[]{:S(2)}, u32[]{:S(2)}) %collective-permute-start.39) | collective-permute-done | bytes 524320 | tf_op jit(solution)/shard_map/ppermute | solution.py:448
  298.5 3.3 collective-permute-start.41
  301.8 7.9 %collective-permute-done.34.refs_3_.refs_10_ = bf16[1024,256]{1,0:T(8,128)(2,1)S(1)} collective-permute-done((bf16[1024,256]{1,0:T(8,128)(2,1)S(1)}, bf16[1024,256]{1,0:T(8,128)(2,1)S(1)}, u32[]{:S(2)}, u32[]{:S(2)}) %collective-permute-start.34) | collective-permute-done | bytes 524320 | tf_op jit(solution)/shard_map/ppermute | solution.py:448
  309.7 3.3 collective-permute-start.40
  313.1 7.1 %col_panel.3.right = bf16[1280,1024]{1,0:T(8,128)(2,1)} custom-call(s32[8]{0:T(128)} %compare_select_fusion.7.info, bf16[2,512,512]{2,1,0:T(8,128)(2,1)} %convert_element_type.6.inverse_ref, bf16[512,512]{1,0:T(8,128)(2,1)} %get-tuple-element.41.pivot_ref, bf16[256,1024]{1,0:T(8,128)(2,1)} %get-tuple-element.28.panel_grads, ...), custom_call_target="tpu_custom_call" | custom-call | flops 2147483648 | bytes 5242880 | tf_op jit(solution)/shard_map/col_panel/pallas_call | solution.py:231
  321.1 10.6 %collective-permute-done.40.refs_11_ = bf16[1024,256]{1,0:T(8,128)(2,1)} collective-permute-done((bf16[1024,256]{1,0:T(8,128)(2,1)S(1)}, bf16[1024,256]{1,0:T(8,128)(2,1)}, u32[]{:S(2)}, u32[]{:S(2)}) %collective-permute-start.40) | collective-permute-done | bytes 524320 | tf_op jit(solution)/shard_map/ppermute | solution.py:448
  331.6 7.2 %col_panel.2.right = bf16[1280,1024]{1,0:T(8,128)(2,1)} custom-call(s32[8]{0:T(128)} %compare_select_fusion.7.info, bf16[2,512,512]{2,1,0:T(8,128)(2,1)} %convert_element_type.6.inverse_ref, bf16[512,512]{1,0:T(8,128)(2,1)} %get-tuple-element.41.pivot_ref, bf16[256,1024]{1,0:T(8,128)(2,1)} %get-tuple-element.28.panel_grads, ...), custom_call_target="tpu_custom_call" | custom-call | flops 2147483648 | bytes 5242880 | tf_op jit(solution)/shard_map/col_panel/pallas_call | solution.py:231
  338.8 13.1 %update.3.refs_0_ = f32[4096,2048]{1,0:T(8,128)} custom-call(s32[8]{0:T(128)} %compare_select_fusion.7.info, bf16[2048,1280]{1,0:T(8,128)(2,1)} %get-tuple-element.40.mine.other, bf16[2048,1280]{1,0:T(8,128)(2,1)} %get-tuple-element.40.mine.other, bf16[1280,1024]{1,0:T(8,128)(2,1)} %col_panel.3.right, f32[4096,2048]{1,0:T(8,128)} %ridge_ref.17), custom_call_target="tpu_custom_call" | custom-call | flops 5368709120 | bytes 24641536 | tf_op jit(solution)/shard_map/update/pallas_call | solution.py:316
  352.0 13.4 %update.4.refs_0_ = f32[4096,2048]{1,0:T(8,128)} custom-call(s32[8]{0:T(128)} %compare_select_fusion.7.info, bf16[2048,1280]{1,0:T(8,128)(2,1)} %get-tuple-element.40.mine.other, bf16[2048,1280]{1,0:T(8,128)(2,1)} %collective-permute-done.29.other, bf16[1280,1024]{1,0:T(8,128)(2,1)} %col_panel.3.right, ...), custom_call_target="tpu_custom_call", output_to_operand_aliasing={{}: (5, {})} | custom-call | flops 5368709120 | bytes 24641536 | tf_op jit(solution)/shard_map/update/pallas_call | solution.py:316
  365.4 22.1 %update.5 = f32[4096,2048]{1,0:T(8,128)} custom-call(s32[8]{0:T(128)} %compare_select_fusion.7.info, bf16[2048,1280]{1,0:T(8,128)(2,1)} %get-tuple-element.40.mine.other, bf16[2048,1280]{1,0:T(8,128)(2,1)} %collective-permute-done.29.other, bf16[1280,1024]{1,0:T(8,128)(2,1)} %col_panel.2.right, ...), custom_call_target="tpu_custom_call", output_to_operand_aliasing={{}: (5, {})} | custom-call | flops 10737418240 | bytes 46661632 | tf_op jit(solution)/shard_map/update/pallas_call | solution.py:316
  (141 shorter events, 15.0 us)
Async XLA Ops:
  3.4 3.7 collective-permute-start.24
  4.1 3.0 collective-permute-start.23
  5.5 1.5 collective-permute-start.22
  10.0 48.3 %collective-permute-start.25 = (bf16[768,1024]{1,0:T(8,128)(2,1)}, bf16[768,1024]{1,0:T(8,128)(2,1)}, u32[]{:S(2)}, u32[]{:S(2)}) collective-permute-start(bf16[768,1024]{1,0:T(8,128)(2,1)} %get-tuple-element.38), channel_id=1, source_target_pairs={{0,1},{8,9},{16,17},{24,25}} | collective-permute-start | bytes 4718600 | tf_op jit(solution)/shard_map/ppermute | solution.py:467
  15.1 5.0 %collective-permute-start = (f32[512,256]{1,0:T(8,128)S(1)}, f32[512,256]{1,0:T(8,128)S(1)}, u32[]{:S(2)}, u32[]{:S(2)}) collective-permute-start(f32[512,256]{1,0:T(8,128)S(1)} %broadcast_select_fusion.10), channel_id=1, source_target_pairs={{0,1},{1,0},{2,3},{3,2},{4,5},{5,4},{6,7},{7,6},{8,9},{9,8},{10,11... | collective-permute-start | bytes 1572872 | tf_op jit(solution)/shard_map/ppermute | solution.py:497
  15.9 47.1 %collective-permute-start.10 = (bf16[512,1024]{1,0:T(8,128)(2,1)}, bf16[512,1024]{1,0:T(8,128)(2,1)}, u32[]{:S(2)}, u32[]{:S(2)}) collective-permute-start(bf16[512,1024]{1,0:T(8,128)(2,1)} %get-tuple-element.30), channel_id=1, source_target_pairs={{0,1},{8,9},{16,17},{24,25}} | collective-permute-start | bytes 3145736 | tf_op jit(solution)/shard_map/ppermute | solution.py:467
  18.4 47.5 %collective-permute-start.14 = (bf16[512,1024]{1,0:T(8,128)(2,1)}, bf16[512,1024]{1,0:T(8,128)(2,1)}, u32[]{:S(2)}, u32[]{:S(2)}) collective-permute-start(bf16[512,1024]{1,0:T(8,128)(2,1)} %get-tuple-element.32), channel_id=1, source_target_pairs={{0,1},{8,9},{16,17},{24,25}} | collective-permute-start | bytes 3145736 | tf_op jit(solution)/shard_map/ppermute | solution.py:467
  20.2 42.7 %collective-permute-start.1 = (f32[256,256]{1,0:T(8,128)S(1)}, f32[256,256]{1,0:T(8,128)S(1)}, u32[]{:S(2)}, u32[]{:S(2)}) collective-permute-start(f32[256,256]{1,0:T(8,128)S(1)} %slice_select_fusion), channel_id=1, source_target_pairs={{0,2},{1,3},{2,0},{3,1},{4,6},{5,7},{6,4},{7,5},{8,10},{9,11},{10,... | collective-permute-start | bytes 786440 | tf_op jit(solution)/shard_map/ppermute | solution.py:497
  59.9 22.4 %collective-permute-start.26 = (bf16[768,1024]{1,0:T(8,128)(2,1)S(1)}, bf16[768,1024]{1,0:T(8,128)(2,1)}, u32[]{:S(2)}, u32[]{:S(2)}) collective-permute-start(bf16[768,1024]{1,0:T(8,128)(2,1)S(1)} %broadcast_select_fusion.refs_12_), channel_id=1, source_target_pairs={{0,2},{1,5},{8,10},{9,13},{16,18},{17,21},{24,26},{25,29}} | collective-permute-start | bytes 4718600 | tf_op jit(solution)/shard_map/ppermute | solution.py:471
  61.2 6.2 %collective-permute-start.18 = (bf16[512,1024]{1,0:T(8,128)(2,1)}, bf16[512,1024]{1,0:T(8,128)(2,1)}, u32[]{:S(2)}, u32[]{:S(2)}) collective-permute-start(bf16[512,1024]{1,0:T(8,128)(2,1)} %get-tuple-element.34), channel_id=1, source_target_pairs={{0,1},{8,9},{16,17},{24,25}} | collective-permute-start | bytes 3145736 | tf_op jit(solution)/shard_map/ppermute | solution.py:467
  62.9 21.8 %collective-permute-start.2 = (f32[128,256]{1,0:T(8,128)S(1)}, f32[128,256]{1,0:T(8,128)S(1)}, u32[]{:S(2)}, u32[]{:S(2)}) collective-permute-start(f32[128,256]{1,0:T(8,128)S(1)} %slice_select_fusion.1), channel_id=1, source_target_pairs={{0,4},{1,5},{2,6},{3,7},{4,0},{5,1},{6,2},{7,3},{8,12},{9,13},{10,... | collective-permute-start | bytes 393224 | tf_op jit(solution)/shard_map/ppermute | solution.py:497
  64.5 43.6 %collective-permute-start.11 = (bf16[512,1024]{1,0:T(8,128)(2,1)S(1)}, bf16[512,1024]{1,0:T(8,128)(2,1)}, u32[]{:S(2)}, u32[]{:S(2)}) collective-permute-start(bf16[512,1024]{1,0:T(8,128)(2,1)S(1)} %broadcast_select_fusion.3.refs_0_), channel_id=1, source_target_pairs={{0,2},{1,5},{8,10},{9,13},{16,18},{17,21},{24,26},{25,29}} | collective-permute-start | bytes 3145736 | tf_op jit(solution)/shard_map/ppermute | solution.py:471
  66.1 29.0 %copy-start.10 = (bf16[512,1024]{1,0:T(8,128)(2,1)}, bf16[512,1024]{1,0:T(8,128)(2,1)S(1)}, u32[]{:S(2)}) copy-start(bf16[512,1024]{1,0:T(8,128)(2,1)S(1)} %broadcast_select_fusion.2.refs_4_) | copy-start | bytes 3145732
  66.1 46.5 %collective-permute-start.15 = (bf16[512,1024]{1,0:T(8,128)(2,1)S(1)}, bf16[512,1024]{1,0:T(8,128)(2,1)}, u32[]{:S(2)}, u32[]{:S(2)}) collective-permute-start(bf16[512,1024]{1,0:T(8,128)(2,1)S(1)} %broadcast_select_fusion.2.refs_4_), channel_id=1, source_target_pairs={{0,2},{1,5},{8,10},{9,13},{16,18},{17,21},{24,26},{25,29}} | collective-permute-start | bytes 3145736 | tf_op jit(solution)/shard_map/ppermute | solution.py:471
  67.4 37.1 %copy-start.35 = (s32[1,64]{1,0:T(1,128)S(1)}, s32[1,64]{1,0:T(1,128)}, u32[]{:S(2)}) copy-start(s32[1,64]{1,0:T(1,128)} %param.11) | copy-start | bytes 772
  67.6 62.5 %copy-start.11 = (bf16[512,1024]{1,0:T(8,128)(2,1)}, bf16[512,1024]{1,0:T(8,128)(2,1)S(1)}, u32[]{:S(2)}) copy-start(bf16[512,1024]{1,0:T(8,128)(2,1)S(1)} %broadcast_select_fusion.1.refs_8_) | copy-start | bytes 3145732
  67.6 50.3 %collective-permute-start.19 = (bf16[512,1024]{1,0:T(8,128)(2,1)S(1)}, bf16[512,1024]{1,0:T(8,128)(2,1)}, u32[]{:S(2)}, u32[]{:S(2)}) collective-permute-start(bf16[512,1024]{1,0:T(8,128)(2,1)S(1)} %broadcast_select_fusion.1.refs_8_), channel_id=1, source_target_pairs={{0,2},{1,5},{8,10},{9,13},{16,18},{17,21},{24,26},{25,29}} | collective-permute-start | bytes 3145736 | tf_op jit(solution)/shard_map/ppermute | solution.py:471
  82.3 44.8 %collective-permute-start.27 = (bf16[768,1024]{1,0:T(8,128)(2,1)}, bf16[768,1024]{1,0:T(8,128)(2,1)}, u32[]{:S(2)}, u32[]{:S(2)}) collective-permute-start(bf16[768,1024]{1,0:T(8,128)(2,1)} %collective-permute-done.26.refs_13_), channel_id=1, source_target_pairs={{2,6},{5,7},{10,14},{13,15},{18,22},{21,23},{26,30},{29,31}} | collective-permute-start | bytes 4718600 | tf_op jit(solution)/shard_map/ppermute | solution.py:471
  84.8 46.9 %copy-start.22 = (f32[2,512,512]{2,1,0:T(8,128)S(1)}, f32[2,512,512]{2,1,0:T(8,128)}, u32[]{:S(2)}) copy-start(f32[2,512,512]{2,1,0:T(8,128)} %param.13) | copy-start | bytes 6291460
  84.8 4.3 %collective-permute-start.3 = (bf16[1,1,128,256]{3,2,1,0:T(8,128)(2,1)S(1)}, bf16[1,1,128,256]{3,2,1,0:T(8,128)(2,1)S(1)}, u32[]{:S(2)}, u32[]{:S(2)}) collective-permute-start(bf16[1,1,128,256]{3,2,1,0:T(8,128)(2,1)S(1)} %fusion.1), channel_id=1, source_target_pairs={{0,8},{8,0},{16,24},{24,16},{1,9},{9,1},{17,25},{25,17},{2,10},{10... | collective-permute-start | bytes 196616 | tf_op jit(solution)/shard_map/ppermute | solution.py:501
  89.1 5.9 %collective-permute-start.4 = (bf16[1,2,128,256]{3,2,1,0:T(8,128)(2,1)S(1)}, bf16[1,2,128,256]{3,2,1,0:T(8,128)(2,1)S(1)}, u32[]{:S(2)}, u32[]{:S(2)}) collective-permute-start(bf16[1,2,128,256]{3,2,1,0:T(8,128)(2,1)S(1)} %pad_maximum_fusion.4), channel_id=1, source_target_pairs={{0,16},{8,24},{16,0},{24,8},{1,17},{9,25},{17,1},{25,9},{2,18},{10... | collective-permute-start | bytes 393224 | tf_op jit(solution)/shard_map/ppermute | solution.py:501
  95.1 9.4 %collective-permute-start.5 = (bf16[1,4,128,256]{3,2,1,0:T(8,128)(2,1)S(1)}, bf16[1,4,128,256]{3,2,1,0:T(8,128)(2,1)S(1)}, u32[]{:S(2)}, u32[]{:S(2)}) collective-permute-start(bf16[1,4,128,256]{3,2,1,0:T(8,128)(2,1)S(1)} %pad_maximum_fusion.3), channel_id=1, source_target_pairs={{0,4},{1,5},{2,6},{3,7},{4,0},{5,1},{6,2},{7,3},{8,12},{9,13},{10,... | collective-permute-start | bytes 786440 | tf_op jit(solution)/shard_map/ppermute | solution.py:504
  104.5 3.6 collective-permute-start.8
  108.1 19.0 %collective-permute-start.6 = (bf16[2,4,128,256]{3,2,1,0:T(8,128)(2,1)S(1)}, bf16[2,4,128,256]{3,2,1,0:T(8,128)(2,1)S(1)}, u32[]{:S(2)}, u32[]{:S(2)}) collective-permute-start(bf16[2,4,128,256]{3,2,1,0:T(8,128)(2,1)S(1)} %pad_maximum_fusion.2), channel_id=1, source_target_pairs={{0,2},{1,3},{2,0},{3,1},{4,6},{5,7},{6,4},{7,5},{8,10},{9,11},{10,... | collective-permute-start | bytes 1572872 | tf_op jit(solution)/shard_map/ppermute | solution.py:504
  108.1 24.7 %collective-permute-start.12 = (bf16[512,1024]{1,0:T(8,128)(2,1)}, bf16[512,1024]{1,0:T(8,128)(2,1)S(1)}, u32[]{:S(2)}, u32[]{:S(2)}) collective-permute-start(bf16[512,1024]{1,0:T(8,128)(2,1)} %collective-permute-done.11.refs_1_), channel_id=1, source_target_pairs={{2,6},{5,7},{10,14},{13,15},{18,22},{21,23},{26,30},{29,31}} | collective-permute-start | bytes 3145736 | tf_op jit(solution)/shard_map/ppermute | solution.py:471
  112.6 23.8 %collective-permute-start.16 = (bf16[512,1024]{1,0:T(8,128)(2,1)}, bf16[512,1024]{1,0:T(8,128)(2,1)}, u32[]{:S(2)}, u32[]{:S(2)}) collective-permute-start(bf16[512,1024]{1,0:T(8,128)(2,1)} %collective-permute-done.15.refs_5_), channel_id=1, source_target_pairs={{2,6},{5,7},{10,14},{13,15},{18,22},{21,23},{26,30},{29,31}} | collective-permute-start | bytes 3145736 | tf_op jit(solution)/shard_map/ppermute | solution.py:471
  117.8 29.7 %collective-permute-start.20 = (bf16[512,1024]{1,0:T(8,128)(2,1)}, bf16[512,1024]{1,0:T(8,128)(2,1)}, u32[]{:S(2)}, u32[]{:S(2)}) collective-permute-start(bf16[512,1024]{1,0:T(8,128)(2,1)} %collective-permute-done.19.refs_9_), channel_id=1, source_target_pairs={{2,6},{5,7},{10,14},{13,15},{18,22},{21,23},{26,30},{29,31}} | collective-permute-start | bytes 3145736 | tf_op jit(solution)/shard_map/ppermute | solution.py:471
  127.1 4.5 %collective-permute-start.9 = (s32[2,64]{1,0:T(2,128)S(1)}, s32[2,64]{1,0:T(2,128)S(1)}, u32[]{:S(2)}, u32[]{:S(2)}) collective-permute-start(s32[2,64]{1,0:T(2,128)S(1)} %pad_add_fusion.1), channel_id=1, source_target_pairs={{0,16},{8,24},{16,0},{24,8},{1,17},{9,25},{17,1},{25,9},{2,18},{10... | collective-permute-start | bytes 1544 | tf_op jit(solution)/shard_map/ppermute | solution.py:476
  127.1 32.6 %collective-permute-start.28 = (bf16[768,1024]{1,0:T(8,128)(2,1)}, bf16[768,1024]{1,0:T(8,128)(2,1)}, u32[]{:S(2)}, u32[]{:S(2)}) collective-permute-start(bf16[768,1024]{1,0:T(8,128)(2,1)} %collective-permute-done.27.refs_14_), channel_id=1, source_target_pairs={{6,4},{7,3},{14,12},{15,11},{22,20},{23,19},{30,28},{31,27}} | collective-permute-start | bytes 4718600 | tf_op jit(solution)/shard_map/ppermute | solution.py:471
  131.6 18.8 %collective-permute-start.7 = (bf16[4,4,128,256]{3,2,1,0:T(8,128)(2,1)}, bf16[4,4,128,256]{3,2,1,0:T(8,128)(2,1)}, u32[]{:S(2)}, u32[]{:S(2)}) collective-permute-start(bf16[4,4,128,256]{3,2,1,0:T(8,128)(2,1)} %pad_maximum_fusion.own_ref), channel_id=1, source_target_pairs={{0,1},{1,0},{2,3},{3,2},{4,5},{5,4},{6,7},{7,6},{8,9},{9,8},{10,11... | collective-permute-start | bytes 3145736 | tf_op jit(solution)/shard_map/ppermute | solution.py:504
  132.8 26.8 %copy-start.23 = (bf16[512,1024]{1,0:T(8,128)(2,1)}, bf16[512,1024]{1,0:T(8,128)(2,1)S(1)}, u32[]{:S(2)}) copy-start(bf16[512,1024]{1,0:T(8,128)(2,1)S(1)} %collective-permute-done.12.refs_2_) | copy-start | bytes 3145732
  132.8 26.8 %collective-permute-start.13 = (bf16[512,1024]{1,0:T(8,128)(2,1)S(1)}, bf16[512,1024]{1,0:T(8,128)(2,1)S(1)}, u32[]{:S(2)}, u32[]{:S(2)}) collective-permute-start(bf16[512,1024]{1,0:T(8,128)(2,1)S(1)} %collective-permute-done.12.refs_2_), channel_id=1, source_target_pairs={{6,4},{7,3},{14,12},{15,11},{22,20},{23,19},{30,28},{31,27}} | collective-permute-start | bytes 3145736 | tf_op jit(solution)/shard_map/ppermute | solution.py:471
  136.3 23.3 %collective-permute-start.17 = (bf16[512,1024]{1,0:T(8,128)(2,1)}, bf16[512,1024]{1,0:T(8,128)(2,1)S(1)}, u32[]{:S(2)}, u32[]{:S(2)}) collective-permute-start(bf16[512,1024]{1,0:T(8,128)(2,1)} %collective-permute-done.16.refs_6_), channel_id=1, source_target_pairs={{6,4},{7,3},{14,12},{15,11},{22,20},{23,19},{30,28},{31,27}} | collective-permute-start | bytes 3145736 | tf_op jit(solution)/shard_map/ppermute | solution.py:471
  147.6 12.1 %collective-permute-start.21 = (bf16[512,1024]{1,0:T(8,128)(2,1)}, bf16[512,1024]{1,0:T(8,128)(2,1)}, u32[]{:S(2)}, u32[]{:S(2)}) collective-permute-start(bf16[512,1024]{1,0:T(8,128)(2,1)} %collective-permute-done.20.refs_10_), channel_id=1, source_target_pairs={{6,4},{7,3},{14,12},{15,11},{22,20},{23,19},{30,28},{31,27}} | collective-permute-start | bytes 3145736 | tf_op jit(solution)/shard_map/ppermute | solution.py:471
  171.2 180.8 %collective-permute-start.29 = (bf16[2048,1280]{1,0:T(8,128)(2,1)}, bf16[2048,1280]{1,0:T(8,128)(2,1)}, u32[]{:S(2)}, u32[]{:S(2)}) collective-permute-start(bf16[2048,1280]{1,0:T(8,128)(2,1)} %get-tuple-element.40.mine.other), channel_id=1, source_target_pairs={{0,1},{1,0},{2,3},{3,2},{4,5},{5,4},{6,7},{7,6},{8,9},{9,8},{10,11... | collective-permute-start | bytes 15728648 | tf_op jit(solution)/shard_map/ppermute | solution.py:512
  191.7 16.9 %collective-permute-start.35 = (bf16[1024,256]{1,0:T(8,128)(2,1)}, bf16[1024,256]{1,0:T(8,128)(2,1)S(1)}, u32[]{:S(2)}, u32[]{:S(2)}) collective-permute-start(bf16[1024,256]{1,0:T(8,128)(2,1)} %get-tuple-element.49.refs_4_), channel_id=1, source_target_pairs={{0,8},{8,16},{16,24},{1,9},{9,17},{17,25},{2,10},{10,18},{18,26},{... | collective-permute-start | bytes 1572872 | tf_op jit(solution)/shard_map/ppermute | solution.py:448
  195.1 24.8 %collective-permute-start.30 = (bf16[1024,256]{1,0:T(8,128)(2,1)}, bf16[1024,256]{1,0:T(8,128)(2,1)S(1)}, u32[]{:S(2)}, u32[]{:S(2)}) collective-permute-start(bf16[1024,256]{1,0:T(8,128)(2,1)} %get-tuple-element.45.refs_0_), channel_id=1, source_target_pairs={{0,8},{8,16},{16,24},{1,9},{9,17},{17,25},{2,10},{10,18},{18,26},{... | collective-permute-start | bytes 1572872 | tf_op jit(solution)/shard_map/ppermute | solution.py:448
  199.6 31.5 %copy-start.32 = (bf16[1024,256]{1,0:T(8,128)(2,1)S(1)}, bf16[1024,256]{1,0:T(8,128)(2,1)}, u32[]{:S(2)}) copy-start(bf16[1024,256]{1,0:T(8,128)(2,1)} %get-tuple-element.47) | copy-start | bytes 1572868
  208.6 22.5 %copy-start.14 = (bf16[1024,256]{1,0:T(8,128)(2,1)}, bf16[1024,256]{1,0:T(8,128)(2,1)S(1)}, u32[]{:S(2)}) copy-start(bf16[1024,256]{1,0:T(8,128)(2,1)S(1)} %collective-permute-done.35.refs_5_) | copy-start | bytes 1572868
  208.6 33.7 %copy-start.31 = (bf16[1024,256]{1,0:T(8,128)(2,1)S(1)}, bf16[1024,256]{1,0:T(8,128)(2,1)}, u32[]{:S(2)}) copy-start(bf16[1024,256]{1,0:T(8,128)(2,1)} %get-tuple-element.43) | copy-start | bytes 1572868
  208.7 33.7 %copy-start.16 = (bf16[1024,256]{1,0:T(8,128)(2,1)}, bf16[1024,256]{1,0:T(8,128)(2,1)S(1)}, u32[]{:S(2)}) copy-start(bf16[1024,256]{1,0:T(8,128)(2,1)S(1)} %broadcast_select_fusion.6.refs_12_) | copy-start | bytes 1572868
  208.7 22.4 %collective-permute-start.36 = (bf16[1024,256]{1,0:T(8,128)(2,1)S(1)}, bf16[1024,256]{1,0:T(8,128)(2,1)S(1)}, u32[]{:S(2)}, u32[]{:S(2)}) collective-permute-start(bf16[1024,256]{1,0:T(8,128)(2,1)S(1)} %broadcast_select_fusion.6.refs_12_), channel_id=1, source_target_pairs={{0,8},{8,16},{16,24},{1,9},{9,17},{17,25},{2,10},{10,18},{18,26},{... | collective-permute-start | bytes 1572872 | tf_op jit(solution)/shard_map/ppermute | solution.py:448
  219.9 33.7 %copy-start.30 = (bf16[1024,256]{1,0:T(8,128)(2,1)S(1)}, bf16[1024,256]{1,0:T(8,128)(2,1)}, u32[]{:S(2)}) copy-start(bf16[1024,256]{1,0:T(8,128)(2,1)} %get-tuple-element.50) | copy-start | bytes 1572868
  219.9 33.7 %copy-start.18 = (bf16[1024,256]{1,0:T(8,128)(2,1)}, bf16[1024,256]{1,0:T(8,128)(2,1)S(1)}, u32[]{:S(2)}) copy-start(bf16[1024,256]{1,0:T(8,128)(2,1)S(1)} %broadcast_select_fusion.9.refs_8_) | copy-start | bytes 1572868
  219.9 22.4 %collective-permute-start.31 = (bf16[1024,256]{1,0:T(8,128)(2,1)S(1)}, bf16[1024,256]{1,0:T(8,128)(2,1)S(1)}, u32[]{:S(2)}, u32[]{:S(2)}) collective-permute-start(bf16[1024,256]{1,0:T(8,128)(2,1)S(1)} %broadcast_select_fusion.9.refs_8_), channel_id=1, source_target_pairs={{0,8},{8,16},{16,24},{1,9},{9,17},{17,25},{2,10},{10,18},{18,26},{... | collective-permute-start | bytes 1572872 | tf_op jit(solution)/shard_map/ppermute | solution.py:448
  231.1 22.5 %copy-start.7 = (bf16[1024,256]{1,0:T(8,128)(2,1)}, bf16[1024,256]{1,0:T(8,128)(2,1)S(1)}, u32[]{:S(2)}) copy-start(bf16[1024,256]{1,0:T(8,128)(2,1)S(1)} %collective-permute-done.36.refs_6_.refs_13_) | copy-start | bytes 1572868
  231.1 33.7 %copy-start.29 = (bf16[1024,256]{1,0:T(8,128)(2,1)S(1)}, bf16[1024,256]{1,0:T(8,128)(2,1)}, u32[]{:S(2)}) copy-start(bf16[1024,256]{1,0:T(8,128)(2,1)} %get-tuple-element.46) | copy-start | bytes 1572868
  231.2 33.6 %copy-start.17 = (bf16[1024,256]{1,0:T(8,128)(2,1)}, bf16[1024,256]{1,0:T(8,128)(2,1)S(1)}, u32[]{:S(2)}) copy-start(bf16[1024,256]{1,0:T(8,128)(2,1)S(1)} %broadcast_select_fusion.5.refs_4_) | copy-start | bytes 1572868
  231.2 22.4 %collective-permute-start.37 = (bf16[1024,256]{1,0:T(8,128)(2,1)S(1)}, bf16[1024,256]{1,0:T(8,128)(2,1)S(1)}, u32[]{:S(2)}, u32[]{:S(2)}) collective-permute-start(bf16[1024,256]{1,0:T(8,128)(2,1)S(1)} %broadcast_select_fusion.5.refs_4_), channel_id=1, source_target_pairs={{0,8},{8,16},{16,24},{1,9},{9,17},{17,25},{2,10},{10,18},{18,26},{... | collective-permute-start | bytes 1572872 | tf_op jit(solution)/shard_map/ppermute | solution.py:448
  242.3 22.5 %copy-start.8 = (bf16[1024,256]{1,0:T(8,128)(2,1)}, bf16[1024,256]{1,0:T(8,128)(2,1)S(1)}, u32[]{:S(2)}) copy-start(bf16[1024,256]{1,0:T(8,128)(2,1)S(1)} %collective-permute-done.31.refs_2_.refs_9_) | copy-start | bytes 1572868
  242.4 67.3 %copy-start.19 = (bf16[1024,256]{1,0:T(8,128)(2,1)}, bf16[1024,256]{1,0:T(8,128)(2,1)S(1)}, u32[]{:S(2)}) copy-start(bf16[1024,256]{1,0:T(8,128)(2,1)S(1)} %broadcast_select_fusion.8.refs_0_) | copy-start | bytes 1572868
  242.4 22.4 %collective-permute-start.32 = (bf16[1024,256]{1,0:T(8,128)(2,1)S(1)}, bf16[1024,256]{1,0:T(8,128)(2,1)S(1)}, u32[]{:S(2)}, u32[]{:S(2)}) collective-permute-start(bf16[1024,256]{1,0:T(8,128)(2,1)S(1)} %broadcast_select_fusion.8.refs_0_), channel_id=1, source_target_pairs={{0,8},{8,16},{16,24},{1,9},{9,17},{17,25},{2,10},{10,18},{18,26},{... | collective-permute-start | bytes 1572872 | tf_op jit(solution)/shard_map/ppermute | solution.py:448
  253.6 59.5 %copy-start.2 = (bf16[1024,256]{1,0:T(8,128)(2,1)}, bf16[1024,256]{1,0:T(8,128)(2,1)S(1)}, u32[]{:S(2)}) copy-start(bf16[1024,256]{1,0:T(8,128)(2,1)S(1)} %collective-permute-done.37.refs_5_.refs_7_.refs_14_) | copy-start | bytes 1572868
  253.6 59.4 %copy-start.20 = (bf16[1024,256]{1,0:T(8,128)(2,1)}, bf16[1024,256]{1,0:T(8,128)(2,1)S(1)}, u32[]{:S(2)}) copy-start(bf16[1024,256]{1,0:T(8,128)(2,1)S(1)} %broadcast_select_fusion.4.refs_12_) | copy-start | bytes 1572868
  253.7 22.4 %collective-permute-start.38 = (bf16[1024,256]{1,0:T(8,128)(2,1)S(1)}, bf16[1024,256]{1,0:T(8,128)(2,1)S(1)}, u32[]{:S(2)}, u32[]{:S(2)}) collective-permute-start(bf16[1024,256]{1,0:T(8,128)(2,1)S(1)} %broadcast_select_fusion.4.refs_12_), channel_id=1, source_target_pairs={{0,8},{8,16},{16,24},{1,9},{9,17},{17,25},{2,10},{10,18},{18,26},{... | collective-permute-start | bytes 1572872 | tf_op jit(solution)/shard_map/ppermute | solution.py:448
  264.8 48.3 %copy-start.3 = (bf16[1024,256]{1,0:T(8,128)(2,1)}, bf16[1024,256]{1,0:T(8,128)(2,1)S(1)}, u32[]{:S(2)}) copy-start(bf16[1024,256]{1,0:T(8,128)(2,1)S(1)} %collective-permute-done.32.refs_1_.refs_3_.refs_10_) | copy-start | bytes 1572868
  264.9 48.2 %copy-start.21 = (bf16[1024,256]{1,0:T(8,128)(2,1)}, bf16[1024,256]{1,0:T(8,128)(2,1)S(1)}, u32[]{:S(2)}) copy-start(bf16[1024,256]{1,0:T(8,128)(2,1)S(1)} %broadcast_select_fusion.7.refs_8_) | copy-start | bytes 1572868
  264.9 22.4 %collective-permute-start.33 = (bf16[1024,256]{1,0:T(8,128)(2,1)S(1)}, bf16[1024,256]{1,0:T(8,128)(2,1)S(1)}, u32[]{:S(2)}, u32[]{:S(2)}) collective-permute-start(bf16[1024,256]{1,0:T(8,128)(2,1)S(1)} %broadcast_select_fusion.7.refs_8_), channel_id=1, source_target_pairs={{0,8},{8,16},{16,24},{1,9},{9,17},{17,25},{2,10},{10,18},{18,26},{... | collective-permute-start | bytes 1572872 | tf_op jit(solution)/shard_map/ppermute | solution.py:448
  276.0 37.1 %copy-start.5 = (bf16[1024,256]{1,0:T(8,128)(2,1)}, bf16[1024,256]{1,0:T(8,128)(2,1)S(1)}, u32[]{:S(2)}) copy-start(bf16[1024,256]{1,0:T(8,128)(2,1)S(1)} %collective-permute-done.38.refs_6_.refs_13_.refs_15_) | copy-start | bytes 1572868
  276.0 22.5 %collective-permute-start.39 = (bf16[1024,256]{1,0:T(8,128)(2,1)S(1)}, bf16[1024,256]{1,0:T(8,128)(2,1)S(1)}, u32[]{:S(2)}, u32[]{:S(2)}) collective-permute-start(bf16[1024,256]{1,0:T(8,128)(2,1)S(1)} %collective-permute-done.38.refs_6_.refs_13_.refs_15_), channel_id=1, source_target_pairs={{0,8},{8,16},{16,24},{1,9},{9,17},{17,25},{2,10},{10,18},{18,26},{... | collective-permute-start | bytes 1572872 | tf_op jit(solution)/shard_map/ppermute | solution.py:448
  287.3 25.9 %copy-start.6 = (bf16[1024,256]{1,0:T(8,128)(2,1)}, bf16[1024,256]{1,0:T(8,128)(2,1)S(1)}, u32[]{:S(2)}) copy-start(bf16[1024,256]{1,0:T(8,128)(2,1)S(1)} %collective-permute-done.33.refs_2_.refs_9_.refs_11_) | copy-start | bytes 1572868
  287.3 22.5 %collective-permute-start.34 = (bf16[1024,256]{1,0:T(8,128)(2,1)S(1)}, bf16[1024,256]{1,0:T(8,128)(2,1)S(1)}, u32[]{:S(2)}, u32[]{:S(2)}) collective-permute-start(bf16[1024,256]{1,0:T(8,128)(2,1)S(1)} %collective-permute-done.33.refs_2_.refs_9_.refs_11_), channel_id=1, source_target_pairs={{0,8},{8,16},{16,24},{1,9},{9,17},{17,25},{2,10},{10,18},{18,26},{... | collective-permute-start | bytes 1572872 | tf_op jit(solution)/shard_map/ppermute | solution.py:448
  298.5 22.6 %collective-permute-start.41 = (bf16[1024,256]{1,0:T(8,128)(2,1)S(1)}, bf16[1024,256]{1,0:T(8,128)(2,1)}, u32[]{:S(2)}, u32[]{:S(2)}) collective-permute-start(bf16[1024,256]{1,0:T(8,128)(2,1)S(1)} %collective-permute-done.39.refs_7_.refs_14_), channel_id=1, source_target_pairs={{0,8},{8,16},{16,24},{1,9},{9,17},{17,25},{2,10},{10,18},{18,26},{... | collective-permute-start | bytes 1572872 | tf_op jit(solution)/shard_map/ppermute | solution.py:448
  309.7 21.9 %collective-permute-start.40 = (bf16[1024,256]{1,0:T(8,128)(2,1)S(1)}, bf16[1024,256]{1,0:T(8,128)(2,1)}, u32[]{:S(2)}, u32[]{:S(2)}) collective-permute-start(bf16[1024,256]{1,0:T(8,128)(2,1)S(1)} %collective-permute-done.34.refs_3_.refs_10_), channel_id=1, source_target_pairs={{0,8},{8,16},{16,24},{1,9},{9,17},{17,25},{2,10},{10,18},{18,26},{... | collective-permute-start | bytes 1572872 | tf_op jit(solution)/shard_map/ppermute | solution.py:448
  (14 other events, 111.1 us)

commit v2 on v1

--- a/solution.py
+++ b/solution.py
@@ -14,7 +14,10 @@
 LINE_CHUNKS = 8
 CHAINS = 2
 CALLS = ((0, 1, 2, 3), (4, 5, 6, 7))
-SPLITS = (((0,), (1,)), ((0, 1),))
+UPDATES = (((0,), (0,)), ((1,), (0,)), ((0, 1), (1,)))
+PIVOT_CHUNK = 2
+PLANE_GROUPS = ((0,), (1, 3), (2,))
+LINE_GROUPS = ((0, 1), (2, 3), (4, 5, 6, 7))
 ROW_BLOCK = 512
 
 
@@ -26,26 +29,28 @@
     return lax.dot_general(a, b, (contract, ((), ())), preferred_element_type=F32)
 
 
-def grads_kernel(
-    sizes, info, own_ref, recv_ref, start_ref, end_ref, row_ref, col_ref, panel_ref, err_t
-):
-    half_pieces, piece, width, col_bits = sizes
+def grads_kernel(sizes, info, own_ref, recv_ref, row_ref, col_ref, panel_ref, err_t):
+    half_pieces, piece, width, col_bits, captions = sizes
     tokens = 2 * half_pieces * piece
     acts = []
     for index in range(2 * half_pieces):
         source = own_ref if index < half_pieces else recv_ref
-        both = source[index % half_pieces, 0]
+        both = source[index % half_pieces, 0, :piece]
         acts.append(both[:, :width])
         err_t[:, index * piece : (index + 1) * piece] = both[:, width:].astype(F32).T
     act = jnp.concatenate(acts, axis=0)
+    lengths = own_ref[0, 0, piece:, :captions]
+    first = lax.broadcasted_iota(jnp.int32, (captions, captions), 0)
+    second = lax.broadcasted_iota(jnp.int32, (captions, captions), 1)
+    start = dot((second < first).astype(BF16), lengths, ((1,), (1,)))[:, :1].astype(jnp.int32)
+    end = dot((second <= first).astype(BF16), lengths, ((1,), (1,)))[:, :1].astype(jnp.int32)
     lane = lax.broadcasted_iota(jnp.int32, (1, tokens), 1)
     place = lane // piece
     position = lane % piece
     for k in range(col_bits):
         mine = (info[2] >> (col_bits - 1 - k)) & 1
         position = position + (mine ^ ((place >> k) & 1)) * (tokens >> (col_bits - k))
-    member = (position >= start_ref[0]) & (position < end_ref[0])
-    captions = member.shape[0]
+    member = (position >= start) & (position < end)
 
     def fill(out_ref, first):
         for group in range(out_ref.shape[1] // (8 * width)):
@@ -68,12 +73,10 @@
     fill(panel_ref, 0)
 
 
-def all_grads(info, own, recv, starts, ends, half_rows, tile_cols, stop, width, col_bits):
-    half_pieces, groups, piece, both = own.shape
-    captions = starts.shape[1]
-    sizes = (half_pieces, piece, width, col_bits)
-    pieces = pl.BlockSpec((half_pieces, 1, piece, both), lambda a, info: (0, a, 0, 0))
-    bounds = pl.BlockSpec((1, captions, 1), lambda a, info: (a, 0, 0))
+def all_grads(info, own, recv, captions, piece, half_rows, tile_cols, stop, width, col_bits):
+    half_pieces, groups, rows, both = own.shape
+    sizes = (half_pieces, piece, width, col_bits, captions)
+    pieces = pl.BlockSpec((half_pieces, 1, rows, both), lambda a, info: (0, a, 0, 0))
     outs = [half_rows, tile_cols, stop]
     total = sum(outs) // width
     return pl.pallas_call(
@@ -81,7 +84,7 @@
         grid_spec=pltpu.PrefetchScalarGridSpec(
             num_scalar_prefetch=1,
             grid=(groups,),
-            in_specs=[pieces, pieces, bounds, bounds],
+            in_specs=[pieces, pieces],
             out_specs=[pl.BlockSpec((captions, n), lambda a, info: (a, 0)) for n in outs],
             scratch_shapes=[pltpu.VMEM((width, 2 * half_pieces * piece), F32)],
         ),
@@ -92,48 +95,77 @@
             transcendentals=0,
         ),
         name="grads",
-    )(info, own, recv, starts, ends)
-
-
-def row_panel_kernel(sizes, info, inverse_ref, panel_grads, row_grads, *refs):
-    chunks, options, rows, pivot_rows, scale = sizes
+    )(info, own, recv)
+
+
+def pivot_kernel(options, scale, info, inverse_ref, panel_grads, *refs):
+    sources = refs[:options]
+    pivot_ref, short_ref, held, sem = refs[options:]
+    width = inverse_ref.shape[1]
+    tail = held.shape[0]
+    rows = sources[0].shape[0] - tail
+    for option, source in enumerate(sources):
+
+        @pl.when(info[3] == option)
+        def _():
+            pltpu.make_async_copy(source.at[pl.ds(rows, tail)], held, sem).start()
+
+    short_ref[...] = inverse_ref[...].astype(BF16)
+    grads = panel_grads[...]
+    gram = dot(grads[:, width:], grads[:, :width], ((0,), (0,)))
+    pltpu.make_async_copy(sources[0].at[pl.ds(rows, tail)], held, sem).wait()
+    pivot = jnp.concatenate([held[:, :width], held[:, width:]], axis=0).astype(F32)
+    pivot = (pivot + scale * gram).astype(BF16)
+    pivot_ref[...] = dot(pivot, short_ref[0], ((1,), (1,))).astype(BF16)
+
+
+def pivot_panel(info, inverse, panel_grads, pieces, scale):
+    stop = panel_grads.shape[1]
+    width = stop // 2
+    whole = pl.BlockSpec(memory_space=pltpu.VMEM)
+    return pl.pallas_call(
+        functools.partial(pivot_kernel, len(pieces), scale),
+        in_specs=[pl.BlockSpec(memory_space=pltpu.SMEM), whole, whole]
+        + [pl.BlockSpec(memory_space=pl.ANY)] * len(pieces),
+        out_specs=[whole, whole],
+        out_shape=[
+            jax.ShapeDtypeStruct((width, width), BF16),
+            jax.ShapeDtypeStruct((2, width, width), BF16),
+        ],
+        scratch_shapes=[pltpu.VMEM((width // 2, stop), BF16), pltpu.SemaphoreType.DMA],
+        cost_estimate=pl.CostEstimate(
+            flops=4 * width**3, bytes_accessed=16 * width * width, transcendentals=0
+        ),
+        name="pivot",
+    )(info, inverse, panel_grads, *pieces)
+
+
+def row_panel_kernel(sizes, info, inverse_ref, pivot_ref, panel_grads, row_grads, *refs):
+    chunks, options, scale = sizes
     sources = refs[: chunks * options]
-    out_ref, pivot_ref, held, sem = refs[chunks * options :]
+    out_ref, held, sem = refs[chunks * options :]
     width = inverse_ref.shape[1]
-    step = rows // chunks
+    step = held.shape[0] // chunks
     turn = pl.program_id(0)
 
-    def target(chunk):
-        extra = pivot_rows if chunk == chunks - 1 else 0
-        return held.at[pl.ds(chunk * step, step + extra)]
-
-    def wait(chunk):
-        pltpu.make_async_copy(sources[chunk * options], target(chunk), sem.at[chunk]).wait()
+    def copy(chunk, option):
+        source = sources[chunk * options + option].at[pl.ds(0, step)]
+        return pltpu.make_async_copy(source, held.at[pl.ds(chunk * step, step)], sem.at[chunk])
 
     @pl.when(turn == 0)
     def _():
-        for chunk in reversed(range(chunks)):
+        for chunk in range(chunks):
             for option in range(options):
 
                 @pl.when(info[3] == option)
                 def _():
-                    pltpu.make_async_copy(
-                        sources[chunk * options + option], target(chunk), sem.at[chunk]
-                    ).start()
-
-        wait(chunks - 1)
-        grads = panel_grads[...]
-        packed = held[rows : rows + pivot_rows, :]
-        pivot = jnp.concatenate([packed[:, :width], packed[:, width:]], axis=0).astype(F32)
-        pivot = pivot + scale * dot(grads[:, width:], grads[:, :width], ((0,), (0,)))
-        pivot = dot(pivot.astype(BF16), inverse_ref[0], ((1,), (1,))).astype(BF16)
-        pivot_ref[...] = pivot
-
-    for chunk in range(chunks - 1):
+                    copy(chunk, option).start()
+
+    for chunk in range(chunks):
 
         @pl.when(turn == chunk)
         def _():
-            wait(chunk)
+            copy(chunk, 0).wait()
 
     at = pl.multiple_of(turn * step, step)
     mine = row_grads[...].T
@@ -148,43 +180,34 @@
     out_ref[:, 2 * width :] = mine
 
 
-def row_panel(info, inverse, panel_grads, row_grads, pieces, scale):
+def row_panel(info, inverse, pivot, panel_grads, row_grads, pieces, scale):
     chunks, options = len(pieces), len(pieces[0])
     captions, rows = row_grads.shape
     stop = panel_grads.shape[1]
     width = stop // 2
     step = rows // chunks
-    pivot_rows = pieces[-1][0].shape[0] - pieces[0][0].shape[0]
     whole = pl.BlockSpec(memory_space=pltpu.VMEM)
     return pl.pallas_call(
-        functools.partial(row_panel_kernel, (chunks, options, rows, pivot_rows, scale)),
+        functools.partial(row_panel_kernel, (chunks, options, scale)),
         grid=(chunks,),
         in_specs=[
             pl.BlockSpec(memory_space=pltpu.SMEM),
             whole,
             whole,
+            whole,
             pl.BlockSpec((captions, step), lambda s: (0, s)),
         ]
         + [pl.BlockSpec(memory_space=pl.ANY)] * (chunks * options),
-        out_specs=[
-            pl.BlockSpec((step, stop + captions), lambda s: (s, 0)),
-            pl.BlockSpec((width, width), lambda s: (0, 0)),
-        ],
-        out_shape=[
-            jax.ShapeDtypeStruct((rows, stop + captions), BF16),
-            jax.ShapeDtypeStruct((width, width), BF16),
-        ],
-        scratch_shapes=[
-            pltpu.VMEM((rows + pivot_rows, stop), BF16),
-            pltpu.SemaphoreType.DMA((chunks,)),
-        ],
+        out_specs=pl.BlockSpec((step, stop + captions), lambda s: (s, 0)),
+        out_shape=jax.ShapeDtypeStruct((rows, stop + captions), BF16),
+        scratch_shapes=[pltpu.VMEM((rows, stop), BF16), pltpu.SemaphoreType.DMA((chunks,))],
         cost_estimate=pl.CostEstimate(
             flops=2 * rows * (stop * captions + 3 * width * width),
             bytes_accessed=4 * rows * stop + 2 * captions * (rows + stop),
             transcendentals=0,
         ),
         name="row_panel",
-    )(info, inverse, panel_grads, row_grads, *[p for piece in pieces for p in piece])
+    )(info, inverse, pivot, panel_grads, row_grads, *[p for piece in pieces for p in piece])
 
 
 def col_panel_kernel(sizes, info, inverse_ref, pivot_ref, panel_grads, col_grads, *refs):
@@ -250,29 +273,40 @@
     )(info, inverse, pivot, panel_grads, col_grads, *[p for piece in pieces for p in piece])
 
 
-def update_kernel(sizes, info, mine, other, right, ridge_ref, *refs):
-    first_col, stop, base, blocks = sizes
-    out_ref = refs[-1]
+def update_kernel(sizes, info, mine, other, *refs):
+    parts, stop, base, blocks, first_col = sizes
+    rights = refs[:parts]
+    ridge_ref, out_ref = refs[parts], refs[-1]
     step = pl.program_id(0) + base
-    block, columns = out_ref.shape
-    inside = max(0, min(columns, stop - first_col))
+    block = out_ref.shape[0]
 
     def write(left):
         which = step // blocks
         row = info[7] + ((info[0] ^ which) * blocks + step - which * blocks) * block
-        panel_part = jnp.logical_and(info[2] == 0, inside > 0)
-
-        @pl.when(jnp.logical_and(row >= stop, jnp.logical_not(panel_part & (inside == columns))))
-        def _():
-            out_ref[...] = ridge_ref[...] + dot(left[...], right[...], ((1,), (0,)))
+        holds = info[2] == 0
 
         @pl.when(row < stop)
         def _():
             out_ref[...] = jnp.zeros_like(out_ref)
 
-        if inside:
-
-            @pl.when(panel_part)
+        at = 0
+        for right in rights:
+            until = at + right.shape[1]
+            busy = row >= stop
+            if first_col + until <= stop:
+                busy = busy & jnp.logical_not(holds)
+
+            @pl.when(busy)
+            def _():
+                product = dot(left[...], right[...], ((1,), (0,)))
+                out_ref[:, at:until] = ridge_ref[:, at:until] + product
+
+            at = until
+
+        inside = min(stop - first_col, out_ref.shape[1])
+        if inside > 0:
+
+            @pl.when(holds)
             def _():
                 out_ref[:, :inside] = left[:, first_col : first_col + inside].astype(F32)
 
@@ -285,14 +319,14 @@
         write(other)
 
 
-def update(info, out, mine, other, right, ridge, first_col, stop, halves):
-    depth, columns = right.shape
+def update(info, out, mine, other, rights, ridge, stop, halves, first_col):
+    depth = mine.shape[1]
+    columns = sum(right.shape[1] for right in rights)
+    at = first_col // columns
     half_rows = mine.shape[0]
     block = min(ROW_BLOCK, half_rows)
     blocks = half_rows // block
-    at = first_col // columns
-    assert at * columns == first_col and stop % block == 0
-
+    assert stop % block == 0 and at * columns == first_col
     base = halves[0] * blocks
 
     def rows_of(step, info):
@@ -303,10 +337,10 @@
     specs = [
         pl.BlockSpec((block, depth), lambda s, i: (jnp.minimum(s + base, blocks - 1), 0)),
         pl.BlockSpec((block, depth), lambda s, i: (jnp.maximum(s + base - blocks, 0), 0)),
-        pl.BlockSpec((depth, columns), lambda s, i: (0, 0)),
-        tile,
     ]
-    operands = [mine, other, right, ridge]
+    specs += [pl.BlockSpec(right.shape, lambda s, i: (0, 0)) for right in rights]
+    specs.append(tile)
+    operands = [mine, other, *rights, ridge]
     aliases = {}
     if out is not None:
         specs.append(pl.BlockSpec(memory_space=pl.ANY))
@@ -314,9 +348,12 @@
         aliases = {len(operands): 0}
     rows = len(halves) * half_rows
     return pl.pallas_call(
-        functools.partial(update_kernel, (first_col, stop, base, blocks)),
+        functools.partial(update_kernel, (len(rights), stop, base, blocks, first_col)),
         grid_spec=pltpu.PrefetchScalarGridSpec(
-            num_scalar_prefetch=1, grid=(len(halves) * blocks,), in_specs=specs, out_specs=tile
+            num_scalar_prefetch=1,
+            grid=(len(halves) * blocks,),
+            in_specs=specs,
+            out_specs=tile,
         ),
         out_shape=jax.ShapeDtypeStruct(ridge.shape, F32),
         input_output_aliases=aliases,
@@ -329,24 +366,42 @@
     )(info, *operands)
 
 
-def chunk_kernel(boxes, who, info, ridge_ref, *refs):
+def chunk_kernel(boxes, who, dead, choices, info, ridge_ref, *refs):
     count = len(boxes)
     wide, narrow, in_sem, out_sem = refs[-4:]
     outs = refs[-4 - count : -4]
-    extra = refs[0] if len(refs) > count + 4 else None
+    extras = refs[: len(refs) - count - 4]
+    extras = [extras[k : k + choices] for k in range(0, len(extras), choices)]
     rows, columns = wide.shape[1:]
 
-    @pl.when(info[who] == 0)
+    idle = jnp.logical_and(info[2] == 0, dead)
+
+    @pl.when((info[who] == 0) & jnp.logical_not(idle))
     def _():
         loads, stores = [], []
         for k, (row, column) in enumerate(boxes):
             source = ridge_ref.at[pl.ds(row, rows), pl.ds(column, columns)]
             loads.append([pltpu.make_async_copy(source, wide.at[k], in_sem.at[k])])
-            if extra is not None:
-                target = narrow.at[k, pl.ds(rows, outs[k].shape[0] - rows)]
-                loads[k].append(pltpu.make_async_copy(extra, target, in_sem.at[count + k]))
-            for load in loads[k]:
-                load.start()
+            loads[k][0].start()
+            tail = outs[k].shape[0] - rows
+            part = extras[0][0].shape[1] if extras else 0
+            for index, options in enumerate(extras):
+                for side in range(2):
+                    target = narrow.at[
+                        k,
+                        pl.ds(rows, tail),
+                        pl.ds(side * columns // 2 + index * part, part),
+                    ]
+                    sem = in_sem.at[count + (2 * index + side) * count + k]
+                    for z, option in enumerate(options):
+                        source = option.at[pl.ds(side * tail, tail)]
+                        load = pltpu.make_async_copy(source, target, sem)
+
+                        @pl.when(info[1] == z)
+                        def _():
+                            load.start()
+
+                    loads[k].append(load)
         for k in range(count):
             for load in loads[k]:
                 load.wait()
@@ -357,21 +412,22 @@
             store.wait()
 
 
-def chunks_of(info, ridge, boxes, shape, who, extra=None):
+def chunks_of(info, ridge, boxes, shape, who, extras=(), dead=False):
     count = len(boxes)
     rows, columns = shape
-    total = rows + (0 if extra is None else extra.shape[0])
+    total = rows + (columns // 4 if extras else 0)
+    choices = len(extras[0]) if extras else 1
     place = pl.BlockSpec(memory_space=pl.ANY)
-    operands = [ridge] if extra is None else [ridge, extra]
+    operands = [ridge, *[piece for options in extras for piece in options]]
     return pl.pallas_call(
-        functools.partial(chunk_kernel, boxes, who),
+        functools.partial(chunk_kernel, boxes, who, dead, choices),
         in_specs=[pl.BlockSpec(memory_space=pltpu.SMEM)] + [place] * len(operands),
         out_specs=[place] * count,
         out_shape=[jax.ShapeDtypeStruct((total, columns), BF16)] * count,
         scratch_shapes=[
             pltpu.VMEM((count, rows, columns), F32),
             pltpu.VMEM((count, total, columns), BF16),
-            pltpu.SemaphoreType.DMA((2 * count,)),
+            pltpu.SemaphoreType.DMA(((1 + 2 * len(extras)) * count,)),
             pltpu.SemaphoreType.DMA((count,)),
         ],
         cost_estimate=pl.CostEstimate(
@@ -397,7 +453,6 @@
     proj_width = act_proj.shape[1]
     captions = lengths.shape[1]
     scale = 1.0 / (captions * row_count)
-    inverse = pivot_inverse.astype(BF16)
 
     pairs = col_count // 2
     orders = gray_order(pairs)
@@ -423,20 +478,17 @@
     for k, fact in enumerate(facts):
         info = jnp.where(slot == k, fact, info)
 
-    boxes = [(width, 0), (width + width // 2, 0)]
-    pivot = chunks_of(info, ridge, boxes, (width // 2, width), 2)
-    pivot = jnp.concatenate(pivot, axis=1)
-    sent = []
+    pivots = list(chunks_of(info, ridge, [(width, 0)], (width, width), 2))
     for z in range(1, row_count):
-        sent.append(lax.ppermute(pivot, ("row", "col"), [(0, z * col_count)]))
-    pivot = jnp.where(row_idx == 0, pivot, functools.reduce(jnp.add, sent))
+        pivots.append(lax.ppermute(pivots[0], ("row", "col"), [(0, z * col_count)]))
 
     line_step = tile_cols // LINE_CHUNKS
     steps = LINE_CHUNKS + CHAINS * (row_count - 2)
     arrived, source, first = [], [], []
-    for ns in (range(CHAINS), range(CHAINS, LINE_CHUNKS)):
-        boxes = [(0, n * line_step) for n in ns]
-        first += chunks_of(info, ridge, boxes, (stop, line_step), 1)
+    for ks in LINE_GROUPS:
+        boxes = [(0, k * line_step) for k in ks]
+        dead = (max(ks) + 1) * line_step <= stop
+        first += chunks_of(info, ridge, boxes, (stop, line_step), 1, (), dead)
     for k in range(steps):
         if k >= LINE_CHUNKS:
             piece = arrived[k - CHAINS]
@@ -452,14 +504,12 @@
     ]
 
     plane_step = half_rows // PLANE_CHUNKS
-    plane = []
-    last = PLANE_CHUNKS - 1
-    made = {}
-    for name, ns in (("a", (0,)), ("b", tuple(range(1, last))), ("c", (last,))):
+    plane, made = [], {}
+    for ns in PLANE_GROUPS:
         boxes = [(half_rows + n * plane_step, 0) for n in ns]
         boxes += [(n * plane_step, 0) for n in ns]
-        extra = pivot if name == "c" else None
-        got = chunks_of(info, ridge, boxes, (plane_step, stop), 2, extra)
+        extras = [pivots] if PIVOT_CHUNK in ns else ()
+        got = chunks_of(info, ridge, boxes, (plane_step, stop), 2, extras)
         for k, n in enumerate(ns):
             made[n] = (got[k], got[len(ns) + k])
     for n in range(PLANE_CHUNKS):
@@ -470,15 +520,6 @@
             perm = [(2 * o[d - 1] + c, 2 * o[d] + c) for c, o in enumerate(orders)]
             hops.append(lax.ppermute(hops[-1], "col", perm))
         plane.append(hops)
-
-    all_lengths = lengths
-    for k in range(row_count.bit_length() - 1):
-        got = lax.ppermute(all_lengths, "row", xor_pairs(row_count, 1 << k))
-        all_lengths = jnp.concatenate([all_lengths, got], axis=0)
-    before = jnp.arange(captions)[:, None] < jnp.arange(captions)[None, :]
-    starts = jnp.sum(jnp.where(before[None], all_lengths[:, :, None], 0), axis=1)
-    ends = (starts + all_lengths)[:, :, None]
-    starts = starts[:, :, None]
 
     total = jnp.concatenate(
         [
@@ -496,7 +537,9 @@
         keep = jnp.where(upper, high, low)
         got = lax.ppermute(send, "col", xor_pairs(col_count, 1 << k))
         total = keep + got
-    held = total.astype(BF16)[None, None]
+    piece = total.shape[0]
+    counts = jnp.pad(lengths.astype(F32), ((0, 15), (0, total.shape[1] - captions)))
+    held = jnp.concatenate([total, counts], axis=0).astype(BF16)[None, None]
     for k in range(row_count.bit_length() - 1):
         got = lax.ppermute(held, "row", xor_pairs(row_count, 1 << k))
         held = jnp.concatenate([held, got], axis=1)
@@ -506,28 +549,28 @@
             held = jnp.concatenate([held, got], axis=0)
 
     row_grads, col_grads, panel_grads = all_grads(
-        info, held, got, starts, ends, half_rows, tile_cols, stop, proj_width, col_bits
+        info, held, got, captions, piece, half_rows, tile_cols, stop, proj_width, col_bits
     )
-    mine, pivot_panel = row_panel(info, inverse, panel_grads, row_grads, plane, scale)
+    pivot, inverse = pivot_panel(
+        info, pivot_inverse, panel_grads, plane[PIVOT_CHUNK], scale
+    )
+    mine = row_panel(info, inverse, pivot, panel_grads, row_grads, plane, scale)
     other = lax.ppermute(mine, "col", xor_pairs(col_count, 1))
-
+    rights = []
+    for call in CALLS:
+        pieces = [line[n] for n in call]
+        first_col = call[0] * line_step
+        rights.append(
+            col_panel(
+                info, inverse, pivot, panel_grads, col_grads, pieces, first_col, scale
+            )
+        )
     out = None
-    for index, call in enumerate(CALLS):
-        first_col = call[0] * line_step
-        pieces = [line[n] for n in call]
-        right = col_panel(
-            info,
-            inverse,
-            pivot_panel,
-            panel_grads,
-            col_grads,
-            pieces,
-            first_col,
-            scale,
-        )
-        for halves in SPLITS[index]:
-            rest = other if 1 in halves else mine
-            out = update(info, out, mine, rest, right, ridge, first_col, stop, halves)
+    for halves, parts in UPDATES:
+        rest = other if 1 in halves else mine
+        used = [rights[part] for part in parts]
+        first_col = CALLS[parts[0]][0] * line_step
+        out = update(info, out, mine, rest, used, ridge, stop, halves, first_col)
     return out
 
 

time: 389 us -> 393 us (1.010)
  the two profiles are of different devices: /device:TPU:10 before, /device:TPU:13 now
where the time goes in v2:
time: 393 us; the launch traced here: 391 us
  waiting for transfers between devices  193 us (49%)
  starting transfers between devices  99.6 us (25%)
  Pallas kernels  90.9 us (23%)
    ppermute x12, waiting for transfers between devices, per_device(): lax.ppermute(piece, 'row', [(z - 1, z) for z in range(1, row_count)])  107 us
    pallas_call x3, Pallas kernels, update(): pl.pallas_call(functools.partial(update_kernel, (len(rights), stop, base,...  48.6 us
    ppermute x3, waiting for transfers between devices, per_device(): got = lax.ppermute(held, 'col', xor_pairs(col_count, 1 << k))  34.5 us
    ppermute x3, starting transfers between devices, per_device(): got = lax.ppermute(send, 'col', xor_pairs(col_count, 1 << k))  27.5 us
    ppermute x12, waiting for transfers between devices, per_device(): hops.append(lax.ppermute(hops[-1], 'col', perm))  26 us
    ppermute x12, starting transfers between devices, per_device(): lax.ppermute(piece, 'row', [(z - 1, z) for z in range(1, row_count)])  24.5 us
    ppermute x12, starting transfers between devices, per_device(): hops.append(lax.ppermute(hops[-1], 'col', perm))  22.6 us
    ppermute x3, waiting for transfers between devices, per_device(): got = lax.ppermute(send, 'col', xor_pairs(col_count, 1 << k))  21.9 us
  transfers between devices with their start and end apart: 40, of which 19 were waited for; matrix products, arithmetic and copies ran while one was open for 1% of the time, Pallas kernels for 11%

profile of v2, /device:TPU:13, one launch (start us, length us, event | category | flops | bytes accessed | tf_op | source)
XLA Modules:
  0.0 391.5 jit_solution(11318179788723688412)
XLA Ops:
  2.1 1.5 collective-permute-start.9
  3.5 1.4 collective-permute-start.8
  5.7 0.9 copy-done.24
  6.6 1.6 fusion.3
  9.8 1.8 collective-permute-start.11
  12.4 1.5 collective-permute-done
  14.1 1.3 collective-permute-start.1
  16.1 1.7 collective-permute-start.15
  18.5 1.6 collective-permute-start.19
  20.2 1.7 collective-permute-start.23
  21.9 1.7 broadcast_select_fusion.refs_0_.refs_8_
  23.6 1.3 collective-permute-start.12
  25.0 25.5 %collective-permute-start.2 = (f32[128,256]{1,0:T(8,128)S(1)}, f32[128,256]{1,0:T(8,128)S(1)}, u32[]{:S(2)}, u32[]{:S(2)}) collective-permute-start(f32[128,256]{1,0:T(8,128)S(1)} %slice_select_fusion.1), channel_id=1, source_target_pairs={{0,4},{1,5},{2,6},{3,7},{4,0},{5,1},{6,2},{7,3},{8,12},{9,13},{10,... | collective-permute-start | bytes 393224 | tf_op jit(solution)/shard_map/ppermute | solution.py:538
  50.5 20.4 %collective-permute-done.2 = f32[128,256]{1,0:T(8,128)S(1)} collective-permute-done((f32[128,256]{1,0:T(8,128)S(1)}, f32[128,256]{1,0:T(8,128)S(1)}, u32[]{:S(2)}, u32[]{:S(2)}) %collective-permute-start.2) | collective-permute-done | bytes 131104 | tf_op jit(solution)/shard_map/ppermute | solution.py:538
  71.0 3.5 collective-permute-done.3
  74.8 1.4 collective-permute-start.16
  76.3 1.3 collective-permute-start.20
  77.7 1.4 collective-permute-start.13
  79.2 1.3 collective-permute-start.24
  80.6 4.1 %collective-permute-start.5 = (bf16[1,4,144,256]{3,2,1,0:T(8,128)(2,1)S(1)}, bf16[1,4,144,256]{3,2,1,0:T(8,128)(2,1)S(1)}, u32[]{:S(2)}, u32[]{:S(2)}) collective-permute-start(bf16[1,4,144,256]{3,2,1,0:T(8,128)(2,1)S(1)} %pad_maximum_fusion.3), channel_id=1, source_target_pairs={{0,4},{1,5},{2,6},{3,7},{4,0},{5,1},{6,2},{7,3},{8,12},{9,13},{10,... | collective-permute-start | bytes 884744 | tf_op jit(solution)/shard_map/ppermute | solution.py:547
  84.7 34.5 %collective-permute-done.5 = bf16[1,4,144,256]{3,2,1,0:T(8,128)(2,1)S(1)} collective-permute-done((bf16[1,4,144,256]{3,2,1,0:T(8,128)(2,1)S(1)}, bf16[1,4,144,256]{3,2,1,0:T(8,128)(2,1)S(1)}, u32[]{:S(2)}, u32[]{:S(2)}) %collective-permute-start.5) | collective-permute-done | bytes 294944 | tf_op jit(solution)/shard_map/ppermute | solution.py:547
  119.4 4.3 %collective-permute-start.17 = (bf16[512,1024]{1,0:T(8,128)(2,1)S(1)}, bf16[512,1024]{1,0:T(8,128)(2,1)}, u32[]{:S(2)}, u32[]{:S(2)}) collective-permute-start(bf16[512,1024]{1,0:T(8,128)(2,1)S(1)} %collective-permute-done.16.refs_1_), channel_id=1, source_target_pairs={{2,6},{5,7},{10,14},{13,15},{18,22},{21,23},{26,30},{29,31}} | collective-permute-start | bytes 3145736 | tf_op jit(solution)/shard_map/ppermute | solution.py:521
  123.7 2.3 collective-permute-start.21
  126.0 2.3 collective-permute-start.25
  128.5 2.0 collective-permute-start.14
  130.5 7.0 %collective-permute-done.17.refs_2_ = bf16[512,1024]{1,0:T(8,128)(2,1)} collective-permute-done((bf16[512,1024]{1,0:T(8,128)(2,1)S(1)}, bf16[512,1024]{1,0:T(8,128)(2,1)}, u32[]{:S(2)}, u32[]{:S(2)}) %collective-permute-start.17) | collective-permute-done | bytes 1048608 | tf_op jit(solution)/shard_map/ppermute | solution.py:521
  137.4 1.7 collective-permute-start.18
  139.1 9.5 %collective-permute-done.21.refs_6_ = bf16[512,1024]{1,0:T(8,128)(2,1)} collective-permute-done((bf16[512,1024]{1,0:T(8,128)(2,1)S(1)}, bf16[512,1024]{1,0:T(8,128)(2,1)}, u32[]{:S(2)}, u32[]{:S(2)}) %collective-permute-start.21) | collective-permute-done | bytes 1048608 | tf_op jit(solution)/shard_map/ppermute | solution.py:521
  148.7 1.7 collective-permute-start.22
  150.4 9.5 %collective-permute-done.25.refs_14_ = bf16[512,1024]{1,0:T(8,128)(2,1)} collective-permute-done((bf16[512,1024]{1,0:T(8,128)(2,1)S(1)}, bf16[512,1024]{1,0:T(8,128)(2,1)}, u32[]{:S(2)}, u32[]{:S(2)}) %collective-permute-start.25) | collective-permute-done | bytes 1048608 | tf_op jit(solution)/shard_map/ppermute | solution.py:521
  159.9 1.7 collective-permute-start.26
  161.5 9.4 %grads.1 = (bf16[256,2048]{1,0:T(8,128)(2,1)}, bf16[256,2048]{1,0:T(8,128)(2,1)}, bf16[256,1024]{1,0:T(8,128)(2,1)}) custom-call(s32[8]{0:T(128)} %compare_select_fusion.7.info, bf16[4,4,144,256]{3,2,1,0:T(8,128)(2,1)} %copy-done.25, bf16[4,4,144,256]{3,2,1,0:T(8,128)(2,1)} %collective-permute-done.7.recv_ref), custom_call_target="tpu_custom_call" | custom-call | flops 5368709120 | bytes 4980736 | tf_op jit(solution)/shard_map/grads/pallas_call | solution.py:82
  171.0 4.0 %pivot.1 = (bf16[512,512]{1,0:T(8,128)(2,1)}, bf16[2,512,512]{2,1,0:T(8,128)(2,1)}) custom-call(s32[8]{0:T(128)} %compare_select_fusion.7.info, f32[2,512,512]{2,1,0:T(8,128)} %inverse_ref.1, bf16[256,1024]{1,0:T(8,128)(2,1)} %get-tuple-element.26.panel_grads, bf16[768,1024]{1,0:T(8,128)(2,1)} %copy-done.2, bf16[768,1024]{1,0:T(8,128)(2,1)} %copy-done.5, ...), custom_call_target="tpu_custom_call" | custom-call | flops 536870912 | bytes 4194304 | tf_op jit(solution)/shard_map/pivot/pallas_call | solution.py:126
  175.0 9.4 %row_panel.1.mine.other = bf16[2048,1280]{1,0:T(8,128)(2,1)} custom-call(s32[8]{0:T(128)} %compare_select_fusion.7.info, bf16[2,512,512]{2,1,0:T(8,128)(2,1)} %get-tuple-element.29.inverse_ref, bf16[512,512]{1,0:T(8,128)(2,1)} %get-tuple-element.30.pivot_ref, bf16[256,1024]{1,0:T(8,128)(2,1)} %get-tuple-element.26.panel_grads, ...), custom_call_target="tpu_custom_call" | custom-call | flops 4294967296 | bytes 9961472 | tf_op jit(solution)/shard_map/row_panel/pallas_call | solution.py:190
  184.4 10.1 %collective-permute-start.27 = (bf16[2048,1280]{1,0:T(8,128)(2,1)}, bf16[2048,1280]{1,0:T(8,128)(2,1)}, u32[]{:S(2)}, u32[]{:S(2)}) collective-permute-start(bf16[2048,1280]{1,0:T(8,128)(2,1)} %row_panel.1.mine.other), channel_id=1, source_target_pairs={{0,1},{1,0},{2,3},{3,2},{4,5},{5,4},{6,7},{7,6},{8,9},{9,8},{10,11... | collective-permute-start | bytes 15728648 | tf_op jit(solution)/shard_map/ppermute | solution.py:558
  195.2 3.1 collective-permute-start.33
  198.3 1.9 collective-permute-start.28
  200.9 11.1 %collective-permute-done.33.refs_5_ = bf16[1024,256]{1,0:T(8,128)(2,1)S(1)} collective-permute-done((bf16[1024,256]{1,0:T(8,128)(2,1)}, bf16[1024,256]{1,0:T(8,128)(2,1)S(1)}, u32[]{:S(2)}, u32[]{:S(2)}) %collective-permute-start.33) | collective-permute-done | bytes 524320 | tf_op jit(solution)/shard_map/ppermute | solution.py:500
  212.1 1.9 collective-permute-start.34
  214.1 9.2 %collective-permute-done.28.refs_1_ = bf16[1024,256]{1,0:T(8,128)(2,1)S(1)} collective-permute-done((bf16[1024,256]{1,0:T(8,128)(2,1)}, bf16[1024,256]{1,0:T(8,128)(2,1)S(1)}, u32[]{:S(2)}, u32[]{:S(2)}) %collective-permute-start.28) | collective-permute-done | bytes 524320 | tf_op jit(solution)/shard_map/ppermute | solution.py:500
  223.4 1.9 collective-permute-start.29
  226.1 8.4 %collective-permute-done.34.refs_6_.refs_13_ = bf16[1024,256]{1,0:T(8,128)(2,1)S(1)} collective-permute-done((bf16[1024,256]{1,0:T(8,128)(2,1)S(1)}, bf16[1024,256]{1,0:T(8,128)(2,1)S(1)}, u32[]{:S(2)}, u32[]{:S(2)}) %collective-permute-start.34) | collective-permute-done | bytes 524320 | tf_op jit(solution)/shard_map/ppermute | solution.py:500
  234.6 2.1 collective-permute-start.35
  236.7 9.1 %collective-permute-done.29.refs_2_.refs_9_ = bf16[1024,256]{1,0:T(8,128)(2,1)S(1)} collective-permute-done((bf16[1024,256]{1,0:T(8,128)(2,1)S(1)}, bf16[1024,256]{1,0:T(8,128)(2,1)S(1)}, u32[]{:S(2)}, u32[]{:S(2)}) %collective-permute-start.29) | collective-permute-done | bytes 524320 | tf_op jit(solution)/shard_map/ppermute | solution.py:500
  245.8 1.9 collective-permute-start.30
  247.8 9.2 %collective-permute-done.35.refs_5_.refs_7_.refs_14_ = bf16[1024,256]{1,0:T(8,128)(2,1)S(1)} collective-permute-done((bf16[1024,256]{1,0:T(8,128)(2,1)S(1)}, bf16[1024,256]{1,0:T(8,128)(2,1)S(1)}, u32[]{:S(2)}, u32[]{:S(2)}) %collective-permute-start.35) | collective-permute-done | bytes 524320 | tf_op jit(solution)/shard_map/ppermute | solution.py:500
  257.1 1.9 collective-permute-start.36
  259.0 9.2 %collective-permute-done.30.refs_1_.refs_3_.refs_10_ = bf16[1024,256]{1,0:T(8,128)(2,1)S(1)} collective-permute-done((bf16[1024,256]{1,0:T(8,128)(2,1)S(1)}, bf16[1024,256]{1,0:T(8,128)(2,1)S(1)}, u32[]{:S(2)}, u32[]{:S(2)}) %collective-permute-start.30) | collective-permute-done | bytes 524320 | tf_op jit(solution)/shard_map/ppermute | solution.py:500
  268.3 2.1 collective-permute-start.31
  270.4 9.0 %collective-permute-done.36.refs_6_.refs_13_.refs_15_ = bf16[1024,256]{1,0:T(8,128)(2,1)S(1)} collective-permute-done((bf16[1024,256]{1,0:T(8,128)(2,1)S(1)}, bf16[1024,256]{1,0:T(8,128)(2,1)S(1)}, u32[]{:S(2)}, u32[]{:S(2)}) %collective-permute-start.36) | collective-permute-done | bytes 524320 | tf_op jit(solution)/shard_map/ppermute | solution.py:500
  279.5 1.9 collective-permute-start.37
  281.4 9.3 %collective-permute-done.31.refs_2_.refs_9_.refs_11_ = bf16[1024,256]{1,0:T(8,128)(2,1)S(1)} collective-permute-done((bf16[1024,256]{1,0:T(8,128)(2,1)S(1)}, bf16[1024,256]{1,0:T(8,128)(2,1)S(1)}, u32[]{:S(2)}, u32[]{:S(2)}) %collective-permute-start.31) | collective-permute-done | bytes 524320 | tf_op jit(solution)/shard_map/ppermute | solution.py:500
  290.7 1.9 collective-permute-start.32
  292.6 9.3 %collective-permute-done.37.refs_7_.refs_14_ = bf16[1024,256]{1,0:T(8,128)(2,1)S(1)} collective-permute-done((bf16[1024,256]{1,0:T(8,128)(2,1)S(1)}, bf16[1024,256]{1,0:T(8,128)(2,1)S(1)}, u32[]{:S(2)}, u32[]{:S(2)}) %collective-permute-start.37) | collective-permute-done | bytes 524320 | tf_op jit(solution)/shard_map/ppermute | solution.py:500
  302.0 1.9 collective-permute-start.39
  303.9 9.3 %collective-permute-done.32.refs_3_.refs_10_ = bf16[1024,256]{1,0:T(8,128)(2,1)S(1)} collective-permute-done((bf16[1024,256]{1,0:T(8,128)(2,1)S(1)}, bf16[1024,256]{1,0:T(8,128)(2,1)S(1)}, u32[]{:S(2)}, u32[]{:S(2)}) %collective-permute-start.32) | collective-permute-done | bytes 524320 | tf_op jit(solution)/shard_map/ppermute | solution.py:500
  313.2 1.9 collective-permute-start.38
  315.2 7.3 %col_panel.3.refs_0_ = bf16[1280,1024]{1,0:T(8,128)(2,1)} custom-call(s32[8]{0:T(128)} %compare_select_fusion.7.info, bf16[2,512,512]{2,1,0:T(8,128)(2,1)} %get-tuple-element.29.inverse_ref, bf16[512,512]{1,0:T(8,128)(2,1)} %get-tuple-element.30.pivot_ref, bf16[256,1024]{1,0:T(8,128)(2,1)} %get-tuple-element.26.panel_grads, ...), custom_call_target="tpu_custom_call" | custom-call | flops 2147483648 | bytes 5242880 | tf_op jit(solution)/shard_map/col_panel/pallas_call | solution.py:254
  322.4 2.1 collective-permute-done.39.refs_15_
  324.5 11.2 %collective-permute-done.38.refs_11_ = bf16[1024,256]{1,0:T(8,128)(2,1)} collective-permute-done((bf16[1024,256]{1,0:T(8,128)(2,1)S(1)}, bf16[1024,256]{1,0:T(8,128)(2,1)}, u32[]{:S(2)}, u32[]{:S(2)}) %collective-permute-start.38) | collective-permute-done | bytes 524320 | tf_op jit(solution)/shard_map/ppermute | solution.py:500
  335.8 7.1 %col_panel.2.refs_0_ = bf16[1280,1024]{1,0:T(8,128)(2,1)} custom-call(s32[8]{0:T(128)} %compare_select_fusion.7.info, bf16[2,512,512]{2,1,0:T(8,128)(2,1)} %get-tuple-element.29.inverse_ref, bf16[512,512]{1,0:T(8,128)(2,1)} %get-tuple-element.30.pivot_ref, bf16[256,1024]{1,0:T(8,128)(2,1)} %get-tuple-element.26.panel_grads, ...), custom_call_target="tpu_custom_call" | custom-call | flops 2147483648 | bytes 5242880 | tf_op jit(solution)/shard_map/col_panel/pallas_call | solution.py:254
  342.9 13.1 %update.3.refs_2_ = f32[4096,2048]{1,0:T(8,128)} custom-call(s32[8]{0:T(128)} %compare_select_fusion.7.info, bf16[2048,1280]{1,0:T(8,128)(2,1)} %row_panel.1.mine.other, bf16[2048,1280]{1,0:T(8,128)(2,1)} %row_panel.1.mine.other, bf16[1280,1024]{1,0:T(8,128)(2,1)} %col_panel.3.refs_0_, f32[4096,2048]{1,0:T(8,128)} %refs_1_.5), custom_call_target="tpu_custom_call" | custom-call | flops 5368709120 | bytes 24641536 | tf_op jit(solution)/shard_map/update/pallas_call | solution.py:350
  355.9 13.4 %update.4.refs_2_ = f32[4096,2048]{1,0:T(8,128)} custom-call(s32[8]{0:T(128)} %compare_select_fusion.7.info, bf16[2048,1280]{1,0:T(8,128)(2,1)} %row_panel.1.mine.other, bf16[2048,1280]{1,0:T(8,128)(2,1)} %collective-permute-done.27.other, bf16[1280,1024]{1,0:T(8,128)(2,1)} %col_panel.3.refs_0_, ...), custom_call_target="tpu_custom_call", output_to_operand_aliasing={{}: (5, {})} | custom-call | flops 5368709120 | bytes 24641536 | tf_op jit(solution)/shard_map/update/pallas_call | solution.py:350
  369.4 22.1 %update.5 = f32[4096,2048]{1,0:T(8,128)} custom-call(s32[8]{0:T(128)} %compare_select_fusion.7.info, bf16[2048,1280]{1,0:T(8,128)(2,1)} %row_panel.1.mine.other, bf16[2048,1280]{1,0:T(8,128)(2,1)} %collective-permute-done.27.other, bf16[1280,1024]{1,0:T(8,128)(2,1)} %col_panel.2.refs_0_, f32[4096,2048]{1,0:T(8,128)} %refs_1_.5, ...), custom_call_target="tpu_custom_call", output_to_operand_aliasing={{}: (5, {})} | custom-call | flops 10737418240 | bytes 46661632 | tf_op jit(solution)/shard_map/update/pallas_call | solution.py:350
  (131 shorter events, 10.3 us)
Async XLA Ops:
  1.4 6.9 %collective-permute-start.10 = (bf16[512,512]{1,0:T(8,128)(2,1)}, bf16[512,512]{1,0:T(8,128)(2,1)S(1)}, u32[]{:S(2)}, u32[]{:S(2)}) collective-permute-start(bf16[512,512]{1,0:T(8,128)(2,1)} %chunks.7.refs_0_), channel_id=1, source_target_pairs={{0,24}} | collective-permute-start | bytes 1572872 | tf_op jit(solution)/shard_map/ppermute | solution.py:483
  2.1 6.2 %collective-permute-start.9 = (bf16[512,512]{1,0:T(8,128)(2,1)}, bf16[512,512]{1,0:T(8,128)(2,1)}, u32[]{:S(2)}, u32[]{:S(2)}) collective-permute-start(bf16[512,512]{1,0:T(8,128)(2,1)} %chunks.7.refs_0_), channel_id=1, source_target_pairs={{0,16}} | collective-permute-start | bytes 1572872 | tf_op jit(solution)/shard_map/ppermute | solution.py:483
  3.5 4.7 %collective-permute-start.8 = (bf16[512,512]{1,0:T(8,128)(2,1)}, bf16[512,512]{1,0:T(8,128)(2,1)}, u32[]{:S(2)}, u32[]{:S(2)}) collective-permute-start(bf16[512,512]{1,0:T(8,128)(2,1)} %chunks.7.refs_0_), channel_id=1, source_target_pairs={{0,8}} | collective-permute-start | bytes 1572872 | tf_op jit(solution)/shard_map/ppermute | solution.py:483
  9.8 12.1 %collective-permute-start.11 = (bf16[768,1024]{1,0:T(8,128)(2,1)}, bf16[768,1024]{1,0:T(8,128)(2,1)}, u32[]{:S(2)}, u32[]{:S(2)}) collective-permute-start(bf16[768,1024]{1,0:T(8,128)(2,1)} %get-tuple-element.27), channel_id=1, source_target_pairs={{0,1},{8,9},{16,17},{24,25}} | collective-permute-start | bytes 4718600 | tf_op jit(solution)/shard_map/ppermute | solution.py:517
  11.7 2.3 collective-permute-start
  14.1 7.8 %collective-permute-start.1 = (f32[256,256]{1,0:T(8,128)S(1)}, f32[256,256]{1,0:T(8,128)S(1)}, u32[]{:S(2)}, u32[]{:S(2)}) collective-permute-start(f32[256,256]{1,0:T(8,128)S(1)} %slice_select_fusion), channel_id=1, source_target_pairs={{0,2},{1,3},{2,0},{3,1},{4,6},{5,7},{6,4},{7,5},{8,10},{9,11},{10,... | collective-permute-start | bytes 786440 | tf_op jit(solution)/shard_map/ppermute | solution.py:538
  16.1 58.5 %collective-permute-start.15 = (bf16[512,1024]{1,0:T(8,128)(2,1)}, bf16[512,1024]{1,0:T(8,128)(2,1)}, u32[]{:S(2)}, u32[]{:S(2)}) collective-permute-start(bf16[512,1024]{1,0:T(8,128)(2,1)} %get-tuple-element.32), channel_id=1, source_target_pairs={{0,1},{8,9},{16,17},{24,25}} | collective-permute-start | bytes 3145736 | tf_op jit(solution)/shard_map/ppermute | solution.py:517
  18.5 57.7 %collective-permute-start.19 = (bf16[512,1024]{1,0:T(8,128)(2,1)}, bf16[512,1024]{1,0:T(8,128)(2,1)}, u32[]{:S(2)}, u32[]{:S(2)}) collective-permute-start(bf16[512,1024]{1,0:T(8,128)(2,1)} %get-tuple-element.34), channel_id=1, source_target_pairs={{0,1},{8,9},{16,17},{24,25}} | collective-permute-start | bytes 3145736 | tf_op jit(solution)/shard_map/ppermute | solution.py:517
  20.2 58.9 %collective-permute-start.23 = (bf16[512,1024]{1,0:T(8,128)(2,1)}, bf16[512,1024]{1,0:T(8,128)(2,1)}, u32[]{:S(2)}, u32[]{:S(2)}) collective-permute-start(bf16[512,1024]{1,0:T(8,128)(2,1)} %get-tuple-element.36), channel_id=1, source_target_pairs={{0,1},{8,9},{16,17},{24,25}} | collective-permute-start | bytes 3145736 | tf_op jit(solution)/shard_map/ppermute | solution.py:517
  21.9 28.5 %copy-start.36 = (s32[1,64]{1,0:T(1,128)S(1)}, s32[1,64]{1,0:T(1,128)}, u32[]{:S(2)}) copy-start(s32[1,64]{1,0:T(1,128)} %param.11) | copy-start | bytes 772
  21.9 52.6 %copy-start.31 = (bf16[512,1024]{1,0:T(8,128)(2,1)S(1)}, bf16[512,1024]{1,0:T(8,128)(2,1)}, u32[]{:S(2)}) copy-start(bf16[512,1024]{1,0:T(8,128)(2,1)} %get-tuple-element.33) | copy-start | bytes 3145732
  23.6 51.1 %copy-start.2 = (bf16[768,1024]{1,0:T(8,128)(2,1)}, bf16[768,1024]{1,0:T(8,128)(2,1)S(1)}, u32[]{:S(2)}) copy-start(bf16[768,1024]{1,0:T(8,128)(2,1)S(1)} %broadcast_select_fusion.refs_0_.refs_8_) | copy-start | bytes 4718596
  23.6 54.0 %collective-permute-start.12 = (bf16[768,1024]{1,0:T(8,128)(2,1)S(1)}, bf16[768,1024]{1,0:T(8,128)(2,1)S(1)}, u32[]{:S(2)}, u32[]{:S(2)}) collective-permute-start(bf16[768,1024]{1,0:T(8,128)(2,1)S(1)} %broadcast_select_fusion.refs_0_.refs_8_), channel_id=1, source_target_pairs={{0,2},{1,5},{8,10},{9,13},{16,18},{17,21},{24,26},{25,29}} | collective-permute-start | bytes 4718600 | tf_op jit(solution)/shard_map/ppermute | solution.py:521
  25.0 51.2 %copy-start.30 = (bf16[512,1024]{1,0:T(8,128)(2,1)S(1)}, bf16[512,1024]{1,0:T(8,128)(2,1)}, u32[]{:S(2)}) copy-start(bf16[512,1024]{1,0:T(8,128)(2,1)} %get-tuple-element.35) | copy-start | bytes 3145732
  25.0 45.9 %collective-permute-start.2 = (f32[128,256]{1,0:T(8,128)S(1)}, f32[128,256]{1,0:T(8,128)S(1)}, u32[]{:S(2)}, u32[]{:S(2)}) collective-permute-start(f32[128,256]{1,0:T(8,128)S(1)} %slice_select_fusion.1), channel_id=1, source_target_pairs={{0,4},{1,5},{2,6},{3,7},{4,0},{5,1},{6,2},{7,3},{8,12},{9,13},{10,... | collective-permute-start | bytes 393224 | tf_op jit(solution)/shard_map/ppermute | solution.py:538
  70.9 3.6 collective-permute-start.3
  74.5 6.1 %collective-permute-start.4 = (bf16[1,2,144,256]{3,2,1,0:T(8,128)(2,1)S(1)}, bf16[1,2,144,256]{3,2,1,0:T(8,128)(2,1)S(1)}, u32[]{:S(2)}, u32[]{:S(2)}) collective-permute-start(bf16[1,2,144,256]{3,2,1,0:T(8,128)(2,1)S(1)} %pad_maximum_fusion.4), channel_id=1, source_target_pairs={{0,16},{8,24},{16,0},{24,8},{1,17},{9,25},{17,1},{25,9},{2,18},{10... | collective-permute-start | bytes 442376 | tf_op jit(solution)/shard_map/ppermute | solution.py:544
  74.8 44.6 %collective-permute-start.16 = (bf16[512,1024]{1,0:T(8,128)(2,1)S(1)}, bf16[512,1024]{1,0:T(8,128)(2,1)S(1)}, u32[]{:S(2)}, u32[]{:S(2)}) collective-permute-start(bf16[512,1024]{1,0:T(8,128)(2,1)S(1)} %broadcast_select_fusion.3.refs_0_), channel_id=1, source_target_pairs={{0,2},{1,5},{8,10},{9,13},{16,18},{17,21},{24,26},{25,29}} | collective-permute-start | bytes 3145736 | tf_op jit(solution)/shard_map/ppermute | solution.py:521
  76.3 42.9 %copy-start.12 = (bf16[512,1024]{1,0:T(8,128)(2,1)}, bf16[512,1024]{1,0:T(8,128)(2,1)S(1)}, u32[]{:S(2)}) copy-start(bf16[512,1024]{1,0:T(8,128)(2,1)S(1)} %broadcast_select_fusion.2.refs_4_) | copy-start | bytes 3145732
  76.3 47.4 %collective-permute-start.20 = (bf16[512,1024]{1,0:T(8,128)(2,1)S(1)}, bf16[512,1024]{1,0:T(8,128)(2,1)S(1)}, u32[]{:S(2)}, u32[]{:S(2)}) collective-permute-start(bf16[512,1024]{1,0:T(8,128)(2,1)S(1)} %broadcast_select_fusion.2.refs_4_), channel_id=1, source_target_pairs={{0,2},{1,5},{8,10},{9,13},{16,18},{17,21},{24,26},{25,29}} | collective-permute-start | bytes 3145736 | tf_op jit(solution)/shard_map/ppermute | solution.py:521
  77.7 41.6 %copy-start.5 = (bf16[768,1024]{1,0:T(8,128)(2,1)}, bf16[768,1024]{1,0:T(8,128)(2,1)S(1)}, u32[]{:S(2)}) copy-start(bf16[768,1024]{1,0:T(8,128)(2,1)S(1)} %collective-permute-done.12.refs_1_.refs_9_) | copy-start | bytes 4718596
  77.7 50.8 %collective-permute-start.13 = (bf16[768,1024]{1,0:T(8,128)(2,1)S(1)}, bf16[768,1024]{1,0:T(8,128)(2,1)S(1)}, u32[]{:S(2)}, u32[]{:S(2)}) collective-permute-start(bf16[768,1024]{1,0:T(8,128)(2,1)S(1)} %collective-permute-done.12.refs_1_.refs_9_), channel_id=1, source_target_pairs={{2,6},{5,7},{10,14},{13,15},{18,22},{21,23},{26,30},{29,31}} | collective-permute-start | bytes 4718600 | tf_op jit(solution)/shard_map/ppermute | solution.py:521
  79.2 49.2 %copy-start.13 = (bf16[512,1024]{1,0:T(8,128)(2,1)}, bf16[512,1024]{1,0:T(8,128)(2,1)S(1)}, u32[]{:S(2)}) copy-start(bf16[512,1024]{1,0:T(8,128)(2,1)S(1)} %broadcast_select_fusion.1.refs_12_) | copy-start | bytes 3145732
  79.2 46.7 %collective-permute-start.24 = (bf16[512,1024]{1,0:T(8,128)(2,1)S(1)}, bf16[512,1024]{1,0:T(8,128)(2,1)S(1)}, u32[]{:S(2)}, u32[]{:S(2)}) collective-permute-start(bf16[512,1024]{1,0:T(8,128)(2,1)S(1)} %broadcast_select_fusion.1.refs_12_), channel_id=1, source_target_pairs={{0,2},{1,5},{8,10},{9,13},{16,18},{17,21},{24,26},{25,29}} | collective-permute-start | bytes 3145736 | tf_op jit(solution)/shard_map/ppermute | solution.py:521
  80.6 38.6 %collective-permute-start.5 = (bf16[1,4,144,256]{3,2,1,0:T(8,128)(2,1)S(1)}, bf16[1,4,144,256]{3,2,1,0:T(8,128)(2,1)S(1)}, u32[]{:S(2)}, u32[]{:S(2)}) collective-permute-start(bf16[1,4,144,256]{3,2,1,0:T(8,128)(2,1)S(1)} %pad_maximum_fusion.3), channel_id=1, source_target_pairs={{0,4},{1,5},{2,6},{3,7},{4,0},{5,1},{6,2},{7,3},{8,12},{9,13},{10,... | collective-permute-start | bytes 884744 | tf_op jit(solution)/shard_map/ppermute | solution.py:547
  119.3 9.0 %collective-permute-start.6 = (bf16[2,4,144,256]{3,2,1,0:T(8,128)(2,1)S(1)}, bf16[2,4,144,256]{3,2,1,0:T(8,128)(2,1)S(1)}, u32[]{:S(2)}, u32[]{:S(2)}) collective-permute-start(bf16[2,4,144,256]{3,2,1,0:T(8,128)(2,1)S(1)} %pad_maximum_fusion.1), channel_id=1, source_target_pairs={{0,2},{1,3},{2,0},{3,1},{4,6},{5,7},{6,4},{7,5},{8,10},{9,11},{10,... | collective-permute-start | bytes 1769480 | tf_op jit(solution)/shard_map/ppermute | solution.py:547
  119.4 18.0 %collective-permute-start.17 = (bf16[512,1024]{1,0:T(8,128)(2,1)S(1)}, bf16[512,1024]{1,0:T(8,128)(2,1)}, u32[]{:S(2)}, u32[]{:S(2)}) collective-permute-start(bf16[512,1024]{1,0:T(8,128)(2,1)S(1)} %collective-permute-done.16.refs_1_), channel_id=1, source_target_pairs={{2,6},{5,7},{10,14},{13,15},{18,22},{21,23},{26,30},{29,31}} | collective-permute-start | bytes 3145736 | tf_op jit(solution)/shard_map/ppermute | solution.py:521
  123.7 24.9 %collective-permute-start.21 = (bf16[512,1024]{1,0:T(8,128)(2,1)S(1)}, bf16[512,1024]{1,0:T(8,128)(2,1)}, u32[]{:S(2)}, u32[]{:S(2)}) collective-permute-start(bf16[512,1024]{1,0:T(8,128)(2,1)S(1)} %collective-permute-done.20.refs_5_), channel_id=1, source_target_pairs={{2,6},{5,7},{10,14},{13,15},{18,22},{21,23},{26,30},{29,31}} | collective-permute-start | bytes 3145736 | tf_op jit(solution)/shard_map/ppermute | solution.py:521
  126.0 22.7 %copy-start.28 = (bf16[512,1024]{1,0:T(8,128)(2,1)}, bf16[512,1024]{1,0:T(8,128)(2,1)S(1)}, u32[]{:S(2)}) copy-start(bf16[512,1024]{1,0:T(8,128)(2,1)S(1)} %collective-permute-done.24.refs_13_) | copy-start | bytes 3145732
  126.0 33.9 %collective-permute-start.25 = (bf16[512,1024]{1,0:T(8,128)(2,1)S(1)}, bf16[512,1024]{1,0:T(8,128)(2,1)}, u32[]{:S(2)}, u32[]{:S(2)}) collective-permute-start(bf16[512,1024]{1,0:T(8,128)(2,1)S(1)} %collective-permute-done.24.refs_13_), channel_id=1, source_target_pairs={{2,6},{5,7},{10,14},{13,15},{18,22},{21,23},{26,30},{29,31}} | collective-permute-start | bytes 3145736 | tf_op jit(solution)/shard_map/ppermute | solution.py:521
  128.4 33.2 %copy-start.25 = (bf16[4,4,144,256]{3,2,1,0:T(8,128)(2,1)}, bf16[4,4,144,256]{3,2,1,0:T(8,128)(2,1)S(1)}, u32[]{:S(2)}) copy-start(bf16[4,4,144,256]{3,2,1,0:T(8,128)(2,1)S(1)} %pad_maximum_fusion.own_ref) | copy-start | bytes 3538948
  128.4 33.2 %collective-permute-start.7 = (bf16[4,4,144,256]{3,2,1,0:T(8,128)(2,1)S(1)}, bf16[4,4,144,256]{3,2,1,0:T(8,128)(2,1)}, u32[]{:S(2)}, u32[]{:S(2)}) collective-permute-start(bf16[4,4,144,256]{3,2,1,0:T(8,128)(2,1)S(1)} %pad_maximum_fusion.own_ref), channel_id=1, source_target_pairs={{0,1},{1,0},{2,3},{3,2},{4,5},{5,4},{6,7},{7,6},{8,9},{9,8},{10,11... | collective-permute-start | bytes 3538952 | tf_op jit(solution)/shard_map/ppermute | solution.py:547
  128.5 42.5 %copy-start.6 = (bf16[768,1024]{1,0:T(8,128)(2,1)}, bf16[768,1024]{1,0:T(8,128)(2,1)S(1)}, u32[]{:S(2)}) copy-start(bf16[768,1024]{1,0:T(8,128)(2,1)S(1)} %collective-permute-done.13.refs_2_.refs_10_) | copy-start | bytes 4718596
  128.5 42.5 %collective-permute-start.14 = (bf16[768,1024]{1,0:T(8,128)(2,1)S(1)}, bf16[768,1024]{1,0:T(8,128)(2,1)}, u32[]{:S(2)}, u32[]{:S(2)}) collective-permute-start(bf16[768,1024]{1,0:T(8,128)(2,1)S(1)} %collective-permute-done.13.refs_2_.refs_10_), channel_id=1, source_target_pairs={{6,4},{7,3},{14,12},{15,11},{22,20},{23,19},{30,28},{31,27}} | collective-permute-start | bytes 4718600 | tf_op jit(solution)/shard_map/ppermute | solution.py:521
  137.4 37.6 %collective-permute-start.18 = (bf16[512,1024]{1,0:T(8,128)(2,1)}, bf16[512,1024]{1,0:T(8,128)(2,1)}, u32[]{:S(2)}, u32[]{:S(2)}) collective-permute-start(bf16[512,1024]{1,0:T(8,128)(2,1)} %collective-permute-done.17.refs_2_), channel_id=1, source_target_pairs={{6,4},{7,3},{14,12},{15,11},{22,20},{23,19},{30,28},{31,27}} | collective-permute-start | bytes 3145736 | tf_op jit(solution)/shard_map/ppermute | solution.py:521
  148.7 26.4 %collective-permute-start.22 = (bf16[512,1024]{1,0:T(8,128)(2,1)}, bf16[512,1024]{1,0:T(8,128)(2,1)}, u32[]{:S(2)}, u32[]{:S(2)}) collective-permute-start(bf16[512,1024]{1,0:T(8,128)(2,1)} %collective-permute-done.21.refs_6_), channel_id=1, source_target_pairs={{6,4},{7,3},{14,12},{15,11},{22,20},{23,19},{30,28},{31,27}} | collective-permute-start | bytes 3145736 | tf_op jit(solution)/shard_map/ppermute | solution.py:521
  159.9 15.1 %collective-permute-start.26 = (bf16[512,1024]{1,0:T(8,128)(2,1)}, bf16[512,1024]{1,0:T(8,128)(2,1)}, u32[]{:S(2)}, u32[]{:S(2)}) collective-permute-start(bf16[512,1024]{1,0:T(8,128)(2,1)} %collective-permute-done.25.refs_14_), channel_id=1, source_target_pairs={{6,4},{7,3},{14,12},{15,11},{22,20},{23,19},{30,28},{31,27}} | collective-permute-start | bytes 3145736 | tf_op jit(solution)/shard_map/ppermute | solution.py:521
  184.4 171.5 %collective-permute-start.27 = (bf16[2048,1280]{1,0:T(8,128)(2,1)}, bf16[2048,1280]{1,0:T(8,128)(2,1)}, u32[]{:S(2)}, u32[]{:S(2)}) collective-permute-start(bf16[2048,1280]{1,0:T(8,128)(2,1)} %row_panel.1.mine.other), channel_id=1, source_target_pairs={{0,1},{1,0},{2,3},{3,2},{4,5},{5,4},{6,7},{7,6},{8,9},{9,8},{10,11... | collective-permute-start | bytes 15728648 | tf_op jit(solution)/shard_map/ppermute | solution.py:558
  195.2 16.9 %collective-permute-start.33 = (bf16[1024,256]{1,0:T(8,128)(2,1)}, bf16[1024,256]{1,0:T(8,128)(2,1)S(1)}, u32[]{:S(2)}, u32[]{:S(2)}) collective-permute-start(bf16[1024,256]{1,0:T(8,128)(2,1)} %get-tuple-element.45.refs_4_), channel_id=1, source_target_pairs={{0,8},{8,16},{16,24},{1,9},{9,17},{17,25},{2,10},{10,18},{18,26},{... | collective-permute-start | bytes 1572872 | tf_op jit(solution)/shard_map/ppermute | solution.py:500
  198.3 25.0 %collective-permute-start.28 = (bf16[1024,256]{1,0:T(8,128)(2,1)}, bf16[1024,256]{1,0:T(8,128)(2,1)S(1)}, u32[]{:S(2)}, u32[]{:S(2)}) collective-permute-start(bf16[1024,256]{1,0:T(8,128)(2,1)} %get-tuple-element.41.refs_0_), channel_id=1, source_target_pairs={{0,8},{8,16},{16,24},{1,9},{9,17},{17,25},{2,10},{10,18},{18,26},{... | collective-permute-start | bytes 1572872 | tf_op jit(solution)/shard_map/ppermute | solution.py:500
  212.1 22.4 %collective-permute-start.34 = (bf16[1024,256]{1,0:T(8,128)(2,1)S(1)}, bf16[1024,256]{1,0:T(8,128)(2,1)S(1)}, u32[]{:S(2)}, u32[]{:S(2)}) collective-permute-start(bf16[1024,256]{1,0:T(8,128)(2,1)S(1)} %broadcast_select_fusion.6.refs_12_), channel_id=1, source_target_pairs={{0,8},{8,16},{16,24},{1,9},{9,17},{17,25},{2,10},{10,18},{18,26},{... | collective-permute-start | bytes 1572872 | tf_op jit(solution)/shard_map/ppermute | solution.py:500
  223.4 22.4 %collective-permute-start.29 = (bf16[1024,256]{1,0:T(8,128)(2,1)S(1)}, bf16[1024,256]{1,0:T(8,128)(2,1)S(1)}, u32[]{:S(2)}, u32[]{:S(2)}) collective-permute-start(bf16[1024,256]{1,0:T(8,128)(2,1)S(1)} %broadcast_select_fusion.9.refs_8_), channel_id=1, source_target_pairs={{0,8},{8,16},{16,24},{1,9},{9,17},{17,25},{2,10},{10,18},{18,26},{... | collective-permute-start | bytes 1572872 | tf_op jit(solution)/shard_map/ppermute | solution.py:500
  226.1 30.9 %copy-start.34 = (bf16[1024,256]{1,0:T(8,128)(2,1)S(1)}, bf16[1024,256]{1,0:T(8,128)(2,1)}, u32[]{:S(2)}) copy-start(bf16[1024,256]{1,0:T(8,128)(2,1)} %get-tuple-element.46) | copy-start | bytes 1572868
  234.5 22.5 %copy-start.9 = (bf16[1024,256]{1,0:T(8,128)(2,1)}, bf16[1024,256]{1,0:T(8,128)(2,1)S(1)}, u32[]{:S(2)}) copy-start(bf16[1024,256]{1,0:T(8,128)(2,1)S(1)} %collective-permute-done.34.refs_6_.refs_13_) | copy-start | bytes 1572868
  234.5 33.7 %copy-start.33 = (bf16[1024,256]{1,0:T(8,128)(2,1)S(1)}, bf16[1024,256]{1,0:T(8,128)(2,1)}, u32[]{:S(2)}) copy-start(bf16[1024,256]{1,0:T(8,128)(2,1)} %get-tuple-element.42) | copy-start | bytes 1572868
  234.6 22.4 %copy-start.20 = (bf16[1024,256]{1,0:T(8,128)(2,1)}, bf16[1024,256]{1,0:T(8,128)(2,1)S(1)}, u32[]{:S(2)}) copy-start(bf16[1024,256]{1,0:T(8,128)(2,1)S(1)} %broadcast_select_fusion.5.refs_4_) | copy-start | bytes 1572868
  234.6 22.4 %collective-permute-start.35 = (bf16[1024,256]{1,0:T(8,128)(2,1)S(1)}, bf16[1024,256]{1,0:T(8,128)(2,1)S(1)}, u32[]{:S(2)}, u32[]{:S(2)}) collective-permute-start(bf16[1024,256]{1,0:T(8,128)(2,1)S(1)} %broadcast_select_fusion.5.refs_4_), channel_id=1, source_target_pairs={{0,8},{8,16},{16,24},{1,9},{9,17},{17,25},{2,10},{10,18},{18,26},{... | collective-permute-start | bytes 1572872 | tf_op jit(solution)/shard_map/ppermute | solution.py:500
  245.8 22.5 %copy-start.10 = (bf16[1024,256]{1,0:T(8,128)(2,1)}, bf16[1024,256]{1,0:T(8,128)(2,1)S(1)}, u32[]{:S(2)}) copy-start(bf16[1024,256]{1,0:T(8,128)(2,1)S(1)} %collective-permute-done.29.refs_2_.refs_9_) | copy-start | bytes 1572868
  245.8 22.4 %copy-start.21 = (bf16[1024,256]{1,0:T(8,128)(2,1)}, bf16[1024,256]{1,0:T(8,128)(2,1)S(1)}, u32[]{:S(2)}) copy-start(bf16[1024,256]{1,0:T(8,128)(2,1)S(1)} %broadcast_select_fusion.8.refs_0_) | copy-start | bytes 1572868
  245.8 22.4 %collective-permute-start.30 = (bf16[1024,256]{1,0:T(8,128)(2,1)S(1)}, bf16[1024,256]{1,0:T(8,128)(2,1)S(1)}, u32[]{:S(2)}, u32[]{:S(2)}) collective-permute-start(bf16[1024,256]{1,0:T(8,128)(2,1)S(1)} %broadcast_select_fusion.8.refs_0_), channel_id=1, source_target_pairs={{0,8},{8,16},{16,24},{1,9},{9,17},{17,25},{2,10},{10,18},{18,26},{... | collective-permute-start | bytes 1572872 | tf_op jit(solution)/shard_map/ppermute | solution.py:500
  257.0 58.1 %copy-start.3 = (bf16[1024,256]{1,0:T(8,128)(2,1)}, bf16[1024,256]{1,0:T(8,128)(2,1)S(1)}, u32[]{:S(2)}) copy-start(bf16[1024,256]{1,0:T(8,128)(2,1)S(1)} %collective-permute-done.35.refs_5_.refs_7_.refs_14_) | copy-start | bytes 1572868
  257.1 56.1 %copy-start.22 = (bf16[1024,256]{1,0:T(8,128)(2,1)}, bf16[1024,256]{1,0:T(8,128)(2,1)S(1)}, u32[]{:S(2)}) copy-start(bf16[1024,256]{1,0:T(8,128)(2,1)S(1)} %broadcast_select_fusion.4.refs_12_) | copy-start | bytes 1572868
  257.1 22.4 %collective-permute-start.36 = (bf16[1024,256]{1,0:T(8,128)(2,1)S(1)}, bf16[1024,256]{1,0:T(8,128)(2,1)S(1)}, u32[]{:S(2)}, u32[]{:S(2)}) collective-permute-start(bf16[1024,256]{1,0:T(8,128)(2,1)S(1)} %broadcast_select_fusion.4.refs_12_), channel_id=1, source_target_pairs={{0,8},{8,16},{16,24},{1,9},{9,17},{17,25},{2,10},{10,18},{18,26},{... | collective-permute-start | bytes 1572872 | tf_op jit(solution)/shard_map/ppermute | solution.py:500
  268.2 46.9 %copy-start.4 = (bf16[1024,256]{1,0:T(8,128)(2,1)}, bf16[1024,256]{1,0:T(8,128)(2,1)S(1)}, u32[]{:S(2)}) copy-start(bf16[1024,256]{1,0:T(8,128)(2,1)S(1)} %collective-permute-done.30.refs_1_.refs_3_.refs_10_) | copy-start | bytes 1572868
  268.3 46.8 %copy-start.23 = (bf16[1024,256]{1,0:T(8,128)(2,1)}, bf16[1024,256]{1,0:T(8,128)(2,1)S(1)}, u32[]{:S(2)}) copy-start(bf16[1024,256]{1,0:T(8,128)(2,1)S(1)} %broadcast_select_fusion.7.refs_8_) | copy-start | bytes 1572868
  268.3 22.4 %collective-permute-start.31 = (bf16[1024,256]{1,0:T(8,128)(2,1)S(1)}, bf16[1024,256]{1,0:T(8,128)(2,1)S(1)}, u32[]{:S(2)}, u32[]{:S(2)}) collective-permute-start(bf16[1024,256]{1,0:T(8,128)(2,1)S(1)} %broadcast_select_fusion.7.refs_8_), channel_id=1, source_target_pairs={{0,8},{8,16},{16,24},{1,9},{9,17},{17,25},{2,10},{10,18},{18,26},{... | collective-permute-start | bytes 1572872 | tf_op jit(solution)/shard_map/ppermute | solution.py:500
  279.5 35.7 %copy-start.7 = (bf16[1024,256]{1,0:T(8,128)(2,1)}, bf16[1024,256]{1,0:T(8,128)(2,1)S(1)}, u32[]{:S(2)}) copy-start(bf16[1024,256]{1,0:T(8,128)(2,1)S(1)} %collective-permute-done.36.refs_6_.refs_13_.refs_15_) | copy-start | bytes 1572868
  279.5 22.5 %collective-permute-start.37 = (bf16[1024,256]{1,0:T(8,128)(2,1)S(1)}, bf16[1024,256]{1,0:T(8,128)(2,1)S(1)}, u32[]{:S(2)}, u32[]{:S(2)}) collective-permute-start(bf16[1024,256]{1,0:T(8,128)(2,1)S(1)} %collective-permute-done.36.refs_6_.refs_13_.refs_15_), channel_id=1, source_target_pairs={{0,8},{8,16},{16,24},{1,9},{9,17},{17,25},{2,10},{10,18},{18,26},{... | collective-permute-start | bytes 1572872 | tf_op jit(solution)/shard_map/ppermute | solution.py:500
  290.7 24.4 %copy-start.8 = (bf16[1024,256]{1,0:T(8,128)(2,1)}, bf16[1024,256]{1,0:T(8,128)(2,1)S(1)}, u32[]{:S(2)}) copy-start(bf16[1024,256]{1,0:T(8,128)(2,1)S(1)} %collective-permute-done.31.refs_2_.refs_9_.refs_11_) | copy-start | bytes 1572868
  290.7 22.5 %collective-permute-start.32 = (bf16[1024,256]{1,0:T(8,128)(2,1)S(1)}, bf16[1024,256]{1,0:T(8,128)(2,1)S(1)}, u32[]{:S(2)}, u32[]{:S(2)}) collective-permute-start(bf16[1024,256]{1,0:T(8,128)(2,1)S(1)} %collective-permute-done.31.refs_2_.refs_9_.refs_11_), channel_id=1, source_target_pairs={{0,8},{8,16},{16,24},{1,9},{9,17},{17,25},{2,10},{10,18},{18,26},{... | collective-permute-start | bytes 1572872 | tf_op jit(solution)/shard_map/ppermute | solution.py:500
  301.9 20.5 %copy-start.14 = (bf16[1024,256]{1,0:T(8,128)(2,1)}, bf16[1024,256]{1,0:T(8,128)(2,1)S(1)}, u32[]{:S(2)}) copy-start(bf16[1024,256]{1,0:T(8,128)(2,1)S(1)} %collective-permute-done.37.refs_7_.refs_14_) | copy-start | bytes 1572868
  302.0 22.6 %collective-permute-start.39 = (bf16[1024,256]{1,0:T(8,128)(2,1)S(1)}, bf16[1024,256]{1,0:T(8,128)(2,1)}, u32[]{:S(2)}, u32[]{:S(2)}) collective-permute-start(bf16[1024,256]{1,0:T(8,128)(2,1)S(1)} %collective-permute-done.37.refs_7_.refs_14_), channel_id=1, source_target_pairs={{0,8},{8,16},{16,24},{1,9},{9,17},{17,25},{2,10},{10,18},{18,26},{... | collective-permute-start | bytes 1572872 | tf_op jit(solution)/shard_map/ppermute | solution.py:500
  313.2 22.6 %collective-permute-start.38 = (bf16[1024,256]{1,0:T(8,128)(2,1)S(1)}, bf16[1024,256]{1,0:T(8,128)(2,1)}, u32[]{:S(2)}, u32[]{:S(2)}) collective-permute-start(bf16[1024,256]{1,0:T(8,128)(2,1)S(1)} %collective-permute-done.32.refs_3_.refs_10_), channel_id=1, source_target_pairs={{0,8},{8,16},{16,24},{1,9},{9,17},{17,25},{2,10},{10,18},{18,26},{... | collective-permute-start | bytes 1572872 | tf_op jit(solution)/shard_map/ppermute | solution.py:500
  369.4 22.1 %copy-start.1 = (bf16[1024,1024]{1,0:T(8,128)(2,1)S(1)}, bf16[1024,1024]{1,0:T(8,128)(2,1)}, u32[]{:S(2)}) copy-start(bf16[1024,1024]{1,0:T(8,128)(2,1)} %param.7) | copy-start | bytes 6291460
  (13 other events, 88.1 us)

commit v3 on v2

--- a/solution.py
+++ b/solution.py
@@ -14,9 +14,9 @@
 LINE_CHUNKS = 8
 CHAINS = 2
 CALLS = ((0, 1, 2, 3), (4, 5, 6, 7))
-UPDATES = (((0,), (0,)), ((1,), (0,)), ((0, 1), (1,)))
-PIVOT_CHUNK = 2
-PLANE_GROUPS = ((0,), (1, 3), (2,))
+UPDATES = (((0, 0),), ((1, 0), (0, 1), (1, 1)))
+PIVOT_CHUNK = 3
+PLANE_GROUPS = ((0,), (1, 2), (3,))
 LINE_GROUPS = ((0, 1), (2, 3), (4, 5, 6, 7))
 ROW_BLOCK = 512
 
@@ -273,87 +273,82 @@
     )(info, inverse, pivot, panel_grads, col_grads, *[p for piece in pieces for p in piece])
 
 
+def pick(step, values):
+    value = jnp.int32(values[0])
+    for k in range(1, len(values)):
+        value = jnp.where(step == k, values[k], value)
+    return value
+
+
 def update_kernel(sizes, info, mine, other, *refs):
-    parts, stop, base, blocks, first_col = sizes
-    rights = refs[:parts]
-    ridge_ref, out_ref = refs[parts], refs[-1]
-    step = pl.program_id(0) + base
-    block = out_ref.shape[0]
-
-    def write(left):
-        which = step // blocks
-        row = info[7] + ((info[0] ^ which) * blocks + step - which * blocks) * block
-        holds = info[2] == 0
-
-        @pl.when(row < stop)
+    work, parts, stop, blocks = sizes
+    rights = refs[: len(parts)]
+    ridge_ref, out_ref = refs[len(parts)], refs[-1]
+    step = pl.program_id(0)
+    block, columns = out_ref.shape
+    segment = step // blocks
+    holds = info[2] == 0
+
+    for place, (half, part) in enumerate(work):
+        left, right = (mine, other)[half], rights[parts.index(part)]
+        first_col = part * columns
+        inside = max(0, min(stop - first_col, columns))
+        row = info[7] + ((info[0] ^ half) * blocks + step - place * blocks) * block
+        now = segment == place
+        busy = now & (row >= stop)
+        if inside == columns:
+            busy = busy & jnp.logical_not(holds)
+
+        @pl.when(busy)
+        def _():
+            out_ref[...] = ridge_ref[...] + dot(left[...], right[...], ((1,), (0,)))
+
+        @pl.when(now & (row < stop))
         def _():
             out_ref[...] = jnp.zeros_like(out_ref)
 
-        at = 0
-        for right in rights:
-            until = at + right.shape[1]
-            busy = row >= stop
-            if first_col + until <= stop:
-                busy = busy & jnp.logical_not(holds)
-
-            @pl.when(busy)
-            def _():
-                product = dot(left[...], right[...], ((1,), (0,)))
-                out_ref[:, at:until] = ridge_ref[:, at:until] + product
-
-            at = until
-
-        inside = min(stop - first_col, out_ref.shape[1])
-        if inside > 0:
-
-            @pl.when(holds)
+        if inside:
+
+            @pl.when(now & holds)
             def _():
                 out_ref[:, :inside] = left[:, first_col : first_col + inside].astype(F32)
 
-    @pl.when(step < blocks)
-    def _():
-        write(mine)
-
-    @pl.when(step >= blocks)
-    def _():
-        write(other)
-
-
-def update(info, out, mine, other, rights, ridge, stop, halves, first_col):
-    depth = mine.shape[1]
-    columns = sum(right.shape[1] for right in rights)
-    at = first_col // columns
+
+def update(info, out, mine, other, rights, ridge, stop, work):
+    parts = sorted({part for _, part in work})
+    depth, columns = rights[parts[0]].shape
     half_rows = mine.shape[0]
     block = min(ROW_BLOCK, half_rows)
     blocks = half_rows // block
-    assert stop % block == 0 and at * columns == first_col
-    base = halves[0] * blocks
-
-    def rows_of(step, info):
-        which = (step + base) // blocks
-        return (info[0] ^ which) * blocks + step + base - which * blocks
-
-    tile = pl.BlockSpec((block, columns), lambda s, i: (rows_of(s, i), at))
-    specs = [
-        pl.BlockSpec((block, depth), lambda s, i: (jnp.minimum(s + base, blocks - 1), 0)),
-        pl.BlockSpec((block, depth), lambda s, i: (jnp.maximum(s + base - blocks, 0), 0)),
-    ]
-    specs += [pl.BlockSpec(right.shape, lambda s, i: (0, 0)) for right in rights]
-    specs.append(tile)
-    operands = [mine, other, *rights, ridge]
+    assert stop % block == 0
+
+    def half_of(step):
+        return pick(step // blocks, [half for half, _ in work])
+
+    def tile_of(step, info):
+        part = pick(step // blocks, [part for _, part in work])
+        return (info[0] ^ half_of(step)) * blocks + step % blocks, part
+
+    def left_of(half):
+        return lambda step, info: (jnp.where(half_of(step) == half, step % blocks, 0), 0)
+
+    specs = [pl.BlockSpec((block, depth), left_of(half)) for half in range(2)]
+    specs += [pl.BlockSpec((depth, columns), lambda s, i: (0, 0)) for _ in parts]
+    specs.append(pl.BlockSpec((block, columns), tile_of))
+    operands = [mine, other, *[rights[part] for part in parts], ridge]
     aliases = {}
     if out is not None:
         specs.append(pl.BlockSpec(memory_space=pl.ANY))
         operands.append(out)
         aliases = {len(operands): 0}
-    rows = len(halves) * half_rows
+    rows = len(work) * half_rows
     return pl.pallas_call(
-        functools.partial(update_kernel, (len(rights), stop, base, blocks, first_col)),
+        functools.partial(update_kernel, (work, parts, stop, blocks)),
         grid_spec=pltpu.PrefetchScalarGridSpec(
             num_scalar_prefetch=1,
-            grid=(len(halves) * blocks,),
+            grid=(len(work) * blocks,),
             in_specs=specs,
-            out_specs=tile,
+            out_specs=pl.BlockSpec((block, columns), tile_of),
         ),
         out_shape=jax.ShapeDtypeStruct(ridge.shape, F32),
         input_output_aliases=aliases,
@@ -374,9 +369,13 @@
     extras = [extras[k : k + choices] for k in range(0, len(extras), choices)]
     rows, columns = wide.shape[1:]
 
-    idle = jnp.logical_and(info[2] == 0, dead)
-
-    @pl.when((info[who] == 0) & jnp.logical_not(idle))
+    ready = info[who[0]] == 0
+    for place in who[1:]:
+        ready = ready & (info[place] == 0)
+    if dead:
+        ready = ready & (info[2] != 0)
+
+    @pl.when(ready)
     def _():
         loads, stores = [], []
         for k, (row, column) in enumerate(boxes):
@@ -478,7 +477,7 @@
     for k, fact in enumerate(facts):
         info = jnp.where(slot == k, fact, info)
 
-    pivots = list(chunks_of(info, ridge, [(width, 0)], (width, width), 2))
+    pivots = list(chunks_of(info, ridge, [(width, 0)], (width, width), (1, 2)))
     for z in range(1, row_count):
         pivots.append(lax.ppermute(pivots[0], ("row", "col"), [(0, z * col_count)]))
 
@@ -488,7 +487,7 @@
     for ks in LINE_GROUPS:
         boxes = [(0, k * line_step) for k in ks]
         dead = (max(ks) + 1) * line_step <= stop
-        first += chunks_of(info, ridge, boxes, (stop, line_step), 1, (), dead)
+        first += chunks_of(info, ridge, boxes, (stop, line_step), (1,), (), dead)
     for k in range(steps):
         if k >= LINE_CHUNKS:
             piece = arrived[k - CHAINS]
@@ -509,7 +508,7 @@
         boxes = [(half_rows + n * plane_step, 0) for n in ns]
         boxes += [(n * plane_step, 0) for n in ns]
         extras = [pivots] if PIVOT_CHUNK in ns else ()
-        got = chunks_of(info, ridge, boxes, (plane_step, stop), 2, extras)
+        got = chunks_of(info, ridge, boxes, (plane_step, stop), (2,), extras)
         for k, n in enumerate(ns):
             made[n] = (got[k], got[len(ns) + k])
     for n in range(PLANE_CHUNKS):
@@ -566,11 +565,9 @@
             )
         )
     out = None
-    for halves, parts in UPDATES:
-        rest = other if 1 in halves else mine
-        used = [rights[part] for part in parts]
-        first_col = CALLS[parts[0]][0] * line_step
-        out = update(info, out, mine, rest, used, ridge, stop, halves, first_col)
+    for work in UPDATES:
+        rest = other if any(half for half, _ in work) else mine
+        out = update(info, out, mine, rest, rights, ridge, stop, work)
     return out
 
 

time: 393 us -> 388 us (0.987)
    pallas_call x3 -> x2, Pallas kernels: 48.6 us -> 46.2 us  [update(): pl.pallas_call(functools.partial(update_kernel, (work, parts, stop, block...]
  transfers between devices with their start and end apart: 40 -> 40, of which waited for: 19 -> 19; matrix products, arithmetic and copies ran while one was open for 1% -> 1% of each run, Pallas kernels for 11% -> 12%
where the time goes in v3:
time: 388 us; the launch traced here: 387 us
  waiting for transfers between devices  192 us (49%)
  starting transfers between devices  97.9 us (25%)
  Pallas kernels  88.5 us (23%)
    ppermute x12, waiting for transfers between devices, per_device(): lax.ppermute(piece, 'row', [(z - 1, z) for z in range(1, row_count)])  106 us
    pallas_call x2, Pallas kernels, update(): pl.pallas_call(functools.partial(update_kernel, (work, parts, stop, block...  46.2 us
    ppermute x3, waiting for transfers between devices, per_device(): got = lax.ppermute(held, 'col', xor_pairs(col_count, 1 << k))  34.4 us
    ppermute x12, waiting for transfers between devices, per_device(): hops.append(lax.ppermute(hops[-1], 'col', perm))  26 us
    ppermute x3, starting transfers between devices, per_device(): got = lax.ppermute(send, 'col', xor_pairs(col_count, 1 << k))  25.2 us
    ppermute x12, starting transfers between devices, per_device(): lax.ppermute(piece, 'row', [(z - 1, z) for z in range(1, row_count)])  24.7 us
    ppermute x12, starting transfers between devices, per_device(): hops.append(lax.ppermute(hops[-1], 'col', perm))  23 us
    ppermute x3, waiting for transfers between devices, per_device(): got = lax.ppermute(send, 'col', xor_pairs(col_count, 1 << k))  21.9 us
  transfers between devices with their start and end apart: 40, of which 19 were waited for; matrix products, arithmetic and copies ran while one was open for 1% of the time, Pallas kernels for 12%

profile of v3, /device:TPU:13, one launch (start us, length us, event | category | flops | bytes accessed | tf_op | source)
XLA Modules:
  0.0 387.0 jit_solution(9166037086988076820)
XLA Ops:
  0.5 0.8 chunks.7.refs_0_
  2.1 1.5 collective-permute-start.9
  3.5 1.4 collective-permute-start.8
  5.7 0.9 copy-done.24
  6.6 1.6 fusion.3
  9.8 1.8 collective-permute-start.11
  12.4 1.5 collective-permute-done
  14.1 1.3 collective-permute-start.1
  16.1 1.7 collective-permute-start.15
  18.6 1.6 collective-permute-start.19
  20.2 1.7 collective-permute-start.23
  22.0 1.6 broadcast_select_fusion.refs_0_.refs_12_
  23.6 1.6 collective-permute-start.12
  25.2 23.2 %collective-permute-start.2 = (f32[128,256]{1,0:T(8,128)S(1)}, f32[128,256]{1,0:T(8,128)S(1)}, u32[]{:S(2)}, u32[]{:S(2)}) collective-permute-start(f32[128,256]{1,0:T(8,128)S(1)} %slice_select_fusion.1), channel_id=1, source_target_pairs={{0,4},{1,5},{2,6},{3,7},{4,0},{5,1},{6,2},{7,3},{8,12},{9,13},{10,... | collective-permute-start | bytes 393224 | tf_op jit(solution)/shard_map/ppermute | solution.py:537
  48.4 20.4 %collective-permute-done.2 = f32[128,256]{1,0:T(8,128)S(1)} collective-permute-done((f32[128,256]{1,0:T(8,128)S(1)}, f32[128,256]{1,0:T(8,128)S(1)}, u32[]{:S(2)}, u32[]{:S(2)}) %collective-permute-start.2) | collective-permute-done | bytes 131104 | tf_op jit(solution)/shard_map/ppermute | solution.py:537
  68.9 3.5 collective-permute-done.3
  72.6 1.4 collective-permute-start.16
  74.3 1.4 collective-permute-start.20
  75.7 1.4 collective-permute-start.13
  77.3 1.3 collective-permute-start.24
  78.6 4.1 %collective-permute-start.5 = (bf16[1,4,144,256]{3,2,1,0:T(8,128)(2,1)S(1)}, bf16[1,4,144,256]{3,2,1,0:T(8,128)(2,1)S(1)}, u32[]{:S(2)}, u32[]{:S(2)}) collective-permute-start(bf16[1,4,144,256]{3,2,1,0:T(8,128)(2,1)S(1)} %pad_maximum_fusion.3), channel_id=1, source_target_pairs={{0,4},{1,5},{2,6},{3,7},{4,0},{5,1},{6,2},{7,3},{8,12},{9,13},{10,... | collective-permute-start | bytes 884744 | tf_op jit(solution)/shard_map/ppermute | solution.py:546
  82.7 34.4 %collective-permute-done.5 = bf16[1,4,144,256]{3,2,1,0:T(8,128)(2,1)S(1)} collective-permute-done((bf16[1,4,144,256]{3,2,1,0:T(8,128)(2,1)S(1)}, bf16[1,4,144,256]{3,2,1,0:T(8,128)(2,1)S(1)}, u32[]{:S(2)}, u32[]{:S(2)}) %collective-permute-start.5) | collective-permute-done | bytes 294944 | tf_op jit(solution)/shard_map/ppermute | solution.py:546
  117.3 4.3 %collective-permute-start.17 = (bf16[512,1024]{1,0:T(8,128)(2,1)S(1)}, bf16[512,1024]{1,0:T(8,128)(2,1)}, u32[]{:S(2)}, u32[]{:S(2)}) collective-permute-start(bf16[512,1024]{1,0:T(8,128)(2,1)S(1)} %collective-permute-done.16.refs_1_), channel_id=1, source_target_pairs={{2,6},{5,7},{10,14},{13,15},{18,22},{21,23},{26,30},{29,31}} | collective-permute-start | bytes 3145736 | tf_op jit(solution)/shard_map/ppermute | solution.py:520
  121.6 2.3 collective-permute-start.21
  123.9 2.3 collective-permute-start.25
  126.4 2.0 collective-permute-start.14
  128.4 6.9 %collective-permute-done.17.refs_2_ = bf16[512,1024]{1,0:T(8,128)(2,1)} collective-permute-done((bf16[512,1024]{1,0:T(8,128)(2,1)S(1)}, bf16[512,1024]{1,0:T(8,128)(2,1)}, u32[]{:S(2)}, u32[]{:S(2)}) %collective-permute-start.17) | collective-permute-done | bytes 1048608 | tf_op jit(solution)/shard_map/ppermute | solution.py:520
  135.3 1.7 collective-permute-start.18
  137.0 9.5 %collective-permute-done.21.refs_6_ = bf16[512,1024]{1,0:T(8,128)(2,1)} collective-permute-done((bf16[512,1024]{1,0:T(8,128)(2,1)S(1)}, bf16[512,1024]{1,0:T(8,128)(2,1)}, u32[]{:S(2)}, u32[]{:S(2)}) %collective-permute-start.21) | collective-permute-done | bytes 1048608 | tf_op jit(solution)/shard_map/ppermute | solution.py:520
  146.5 1.7 collective-permute-start.22
  148.2 9.5 %collective-permute-done.25.refs_10_ = bf16[512,1024]{1,0:T(8,128)(2,1)} collective-permute-done((bf16[512,1024]{1,0:T(8,128)(2,1)S(1)}, bf16[512,1024]{1,0:T(8,128)(2,1)}, u32[]{:S(2)}, u32[]{:S(2)}) %collective-permute-start.25) | collective-permute-done | bytes 1048608 | tf_op jit(solution)/shard_map/ppermute | solution.py:520
  157.8 1.6 collective-permute-start.26
  159.4 9.4 %grads.1 = (bf16[256,2048]{1,0:T(8,128)(2,1)}, bf16[256,2048]{1,0:T(8,128)(2,1)}, bf16[256,1024]{1,0:T(8,128)(2,1)}) custom-call(s32[8]{0:T(128)} %compare_select_fusion.7.info, bf16[4,4,144,256]{3,2,1,0:T(8,128)(2,1)} %copy-done.25, bf16[4,4,144,256]{3,2,1,0:T(8,128)(2,1)} %collective-permute-done.7.recv_ref), custom_call_target="tpu_custom_call" | custom-call | flops 5368709120 | bytes 4980736 | tf_op jit(solution)/shard_map/grads/pallas_call | solution.py:82
  168.9 4.0 %pivot.1 = (bf16[512,512]{1,0:T(8,128)(2,1)}, bf16[2,512,512]{2,1,0:T(8,128)(2,1)}) custom-call(s32[8]{0:T(128)} %compare_select_fusion.7.info, f32[2,512,512]{2,1,0:T(8,128)} %inverse_ref.1, bf16[256,1024]{1,0:T(8,128)(2,1)} %get-tuple-element.26.panel_grads, bf16[768,1024]{1,0:T(8,128)(2,1)} %copy-done.2, bf16[768,1024]{1,0:T(8,128)(2,1)} %copy-done.5, ...), custom_call_target="tpu_custom_call" | custom-call | flops 536870912 | bytes 4194304 | tf_op jit(solution)/shard_map/pivot/pallas_call | solution.py:126
  172.9 9.4 %row_panel.1.mine.other = bf16[2048,1280]{1,0:T(8,128)(2,1)} custom-call(s32[8]{0:T(128)} %compare_select_fusion.7.info, bf16[2,512,512]{2,1,0:T(8,128)(2,1)} %get-tuple-element.29.inverse_ref, bf16[512,512]{1,0:T(8,128)(2,1)} %get-tuple-element.30.pivot_ref, bf16[256,1024]{1,0:T(8,128)(2,1)} %get-tuple-element.26.panel_grads, ...), custom_call_target="tpu_custom_call" | custom-call | flops 4294967296 | bytes 9961472 | tf_op jit(solution)/shard_map/row_panel/pallas_call | solution.py:190
  182.3 10.1 %collective-permute-start.27 = (bf16[2048,1280]{1,0:T(8,128)(2,1)}, bf16[2048,1280]{1,0:T(8,128)(2,1)}, u32[]{:S(2)}, u32[]{:S(2)}) collective-permute-start(bf16[2048,1280]{1,0:T(8,128)(2,1)} %row_panel.1.mine.other), channel_id=1, source_target_pairs={{0,1},{1,0},{2,3},{3,2},{4,5},{5,4},{6,7},{7,6},{8,9},{9,8},{10,11... | collective-permute-start | bytes 15728648 | tf_op jit(solution)/shard_map/ppermute | solution.py:557
  193.1 3.2 collective-permute-start.31
  196.2 1.9 collective-permute-start.28
  198.9 11.1 %collective-permute-done.31.refs_5_ = bf16[1024,256]{1,0:T(8,128)(2,1)S(1)} collective-permute-done((bf16[1024,256]{1,0:T(8,128)(2,1)}, bf16[1024,256]{1,0:T(8,128)(2,1)S(1)}, u32[]{:S(2)}, u32[]{:S(2)}) %collective-permute-start.31) | collective-permute-done | bytes 524320 | tf_op jit(solution)/shard_map/ppermute | solution.py:499
  210.1 1.9 collective-permute-start.32
  212.0 9.2 %collective-permute-done.28.refs_1_ = bf16[1024,256]{1,0:T(8,128)(2,1)S(1)} collective-permute-done((bf16[1024,256]{1,0:T(8,128)(2,1)}, bf16[1024,256]{1,0:T(8,128)(2,1)S(1)}, u32[]{:S(2)}, u32[]{:S(2)}) %collective-permute-start.28) | collective-permute-done | bytes 524320 | tf_op jit(solution)/shard_map/ppermute | solution.py:499
  221.3 1.9 collective-permute-start.29
  224.0 8.4 %collective-permute-done.32.refs_6_.refs_13_ = bf16[1024,256]{1,0:T(8,128)(2,1)S(1)} collective-permute-done((bf16[1024,256]{1,0:T(8,128)(2,1)S(1)}, bf16[1024,256]{1,0:T(8,128)(2,1)S(1)}, u32[]{:S(2)}, u32[]{:S(2)}) %collective-permute-start.32) | collective-permute-done | bytes 524320 | tf_op jit(solution)/shard_map/ppermute | solution.py:499
  232.5 2.1 collective-permute-start.33
  234.6 9.1 %collective-permute-done.29.refs_2_.refs_9_ = bf16[1024,256]{1,0:T(8,128)(2,1)S(1)} collective-permute-done((bf16[1024,256]{1,0:T(8,128)(2,1)S(1)}, bf16[1024,256]{1,0:T(8,128)(2,1)S(1)}, u32[]{:S(2)}, u32[]{:S(2)}) %collective-permute-start.29) | collective-permute-done | bytes 524320 | tf_op jit(solution)/shard_map/ppermute | solution.py:499
  243.8 2.1 collective-permute-start.30
  245.8 9.1 %collective-permute-done.33.refs_7_.refs_14_.refs_5_ = bf16[1024,256]{1,0:T(8,128)(2,1)S(1)} collective-permute-done((bf16[1024,256]{1,0:T(8,128)(2,1)S(1)}, bf16[1024,256]{1,0:T(8,128)(2,1)S(1)}, u32[]{:S(2)}, u32[]{:S(2)}) %collective-permute-start.33) | collective-permute-done | bytes 524320 | tf_op jit(solution)/shard_map/ppermute | solution.py:499
  255.0 1.9 collective-permute-start.35
  256.9 9.2 %collective-permute-done.30.refs_3_.refs_10_.refs_1_ = bf16[1024,256]{1,0:T(8,128)(2,1)S(1)} collective-permute-done((bf16[1024,256]{1,0:T(8,128)(2,1)S(1)}, bf16[1024,256]{1,0:T(8,128)(2,1)S(1)}, u32[]{:S(2)}, u32[]{:S(2)}) %collective-permute-start.30) | collective-permute-done | bytes 524320 | tf_op jit(solution)/shard_map/ppermute | solution.py:499
  266.2 2.1 collective-permute-start.34
  268.4 9.0 %collective-permute-done.35.refs_15_.refs_6_.refs_13_ = bf16[1024,256]{1,0:T(8,128)(2,1)S(1)} collective-permute-done((bf16[1024,256]{1,0:T(8,128)(2,1)S(1)}, bf16[1024,256]{1,0:T(8,128)(2,1)S(1)}, u32[]{:S(2)}, u32[]{:S(2)}) %collective-permute-start.35) | collective-permute-done | bytes 524320 | tf_op jit(solution)/shard_map/ppermute | solution.py:499
  277.4 1.9 collective-permute-start.37
  279.3 9.3 %collective-permute-done.34.refs_11_.refs_2_.refs_9_ = bf16[1024,256]{1,0:T(8,128)(2,1)S(1)} collective-permute-done((bf16[1024,256]{1,0:T(8,128)(2,1)S(1)}, bf16[1024,256]{1,0:T(8,128)(2,1)S(1)}, u32[]{:S(2)}, u32[]{:S(2)}) %collective-permute-start.34) | collective-permute-done | bytes 524320 | tf_op jit(solution)/shard_map/ppermute | solution.py:499
  288.6 1.9 collective-permute-start.36
  290.5 9.3 %collective-permute-done.37.refs_7_.refs_14_ = bf16[1024,256]{1,0:T(8,128)(2,1)S(1)} collective-permute-done((bf16[1024,256]{1,0:T(8,128)(2,1)S(1)}, bf16[1024,256]{1,0:T(8,128)(2,1)S(1)}, u32[]{:S(2)}, u32[]{:S(2)}) %collective-permute-start.37) | collective-permute-done | bytes 524320 | tf_op jit(solution)/shard_map/ppermute | solution.py:499
  299.9 1.9 collective-permute-start.39
  301.8 9.3 %collective-permute-done.36.refs_3_.refs_10_ = bf16[1024,256]{1,0:T(8,128)(2,1)S(1)} collective-permute-done((bf16[1024,256]{1,0:T(8,128)(2,1)S(1)}, bf16[1024,256]{1,0:T(8,128)(2,1)S(1)}, u32[]{:S(2)}, u32[]{:S(2)}) %collective-permute-start.36) | collective-permute-done | bytes 524320 | tf_op jit(solution)/shard_map/ppermute | solution.py:499
  311.1 1.9 collective-permute-start.38
  313.1 7.2 %col_panel.2.refs_0_ = bf16[1280,1024]{1,0:T(8,128)(2,1)} custom-call(s32[8]{0:T(128)} %compare_select_fusion.7.info, bf16[2,512,512]{2,1,0:T(8,128)(2,1)} %get-tuple-element.29.inverse_ref, bf16[512,512]{1,0:T(8,128)(2,1)} %get-tuple-element.30.pivot_ref, bf16[256,1024]{1,0:T(8,128)(2,1)} %get-tuple-element.26.panel_grads, ...), custom_call_target="tpu_custom_call" | custom-call | flops 2147483648 | bytes 5242880 | tf_op jit(solution)/shard_map/col_panel/pallas_call | solution.py:254
  320.3 2.1 collective-permute-done.39.refs_15_
  322.4 11.2 %collective-permute-done.38.refs_11_ = bf16[1024,256]{1,0:T(8,128)(2,1)} collective-permute-done((bf16[1024,256]{1,0:T(8,128)(2,1)S(1)}, bf16[1024,256]{1,0:T(8,128)(2,1)}, u32[]{:S(2)}, u32[]{:S(2)}) %collective-permute-start.38) | collective-permute-done | bytes 524320 | tf_op jit(solution)/shard_map/ppermute | solution.py:499
  333.7 7.1 %col_panel.3.refs_1_ = bf16[1280,1024]{1,0:T(8,128)(2,1)} custom-call(s32[8]{0:T(128)} %compare_select_fusion.7.info, bf16[2,512,512]{2,1,0:T(8,128)(2,1)} %get-tuple-element.29.inverse_ref, bf16[512,512]{1,0:T(8,128)(2,1)} %get-tuple-element.30.pivot_ref, bf16[256,1024]{1,0:T(8,128)(2,1)} %get-tuple-element.26.panel_grads, ...), custom_call_target="tpu_custom_call" | custom-call | flops 2147483648 | bytes 5242880 | tf_op jit(solution)/shard_map/col_panel/pallas_call | solution.py:254
  340.8 13.5 %update.2.refs_3_ = f32[4096,2048]{1,0:T(8,128)} custom-call(s32[8]{0:T(128)} %compare_select_fusion.7.info, bf16[2048,1280]{1,0:T(8,128)(2,1)} %row_panel.1.mine.other, bf16[2048,1280]{1,0:T(8,128)(2,1)} %row_panel.1.mine.other, bf16[1280,1024]{1,0:T(8,128)(2,1)} %col_panel.2.refs_0_, f32[4096,2048]{1,0:T(8,128)} %refs_2_.1), custom_call_target="tpu_custom_call" | custom-call | flops 5368709120 | bytes 24641536 | tf_op jit(solution)/shard_map/update/pallas_call | solution.py:345
  354.3 32.7 %update.3 = f32[4096,2048]{1,0:T(8,128)} custom-call(s32[8]{0:T(128)} %compare_select_fusion.7.info, bf16[2048,1280]{1,0:T(8,128)(2,1)} %row_panel.1.mine.other, bf16[2048,1280]{1,0:T(8,128)(2,1)} %collective-permute-done.27.other, bf16[1280,1024]{1,0:T(8,128)(2,1)} %col_panel.2.refs_0_, ...), custom_call_target="tpu_custom_call", output_to_operand_aliasing={{}: (6, {})} | custom-call | flops 16106127360 | bytes 68681728 | tf_op jit(solution)/shard_map/update/pallas_call | solution.py:345
  (134 shorter events, 9.4 us)
Async XLA Ops:
  1.4 6.9 %collective-permute-start.10 = (bf16[512,512]{1,0:T(8,128)(2,1)}, bf16[512,512]{1,0:T(8,128)(2,1)S(1)}, u32[]{:S(2)}, u32[]{:S(2)}) collective-permute-start(bf16[512,512]{1,0:T(8,128)(2,1)} %chunks.7.refs_0_), channel_id=1, source_target_pairs={{0,24}} | collective-permute-start | bytes 1572872 | tf_op jit(solution)/shard_map/ppermute | solution.py:482
  2.1 6.2 %collective-permute-start.9 = (bf16[512,512]{1,0:T(8,128)(2,1)}, bf16[512,512]{1,0:T(8,128)(2,1)}, u32[]{:S(2)}, u32[]{:S(2)}) collective-permute-start(bf16[512,512]{1,0:T(8,128)(2,1)} %chunks.7.refs_0_), channel_id=1, source_target_pairs={{0,16}} | collective-permute-start | bytes 1572872 | tf_op jit(solution)/shard_map/ppermute | solution.py:482
  3.5 4.7 %collective-permute-start.8 = (bf16[512,512]{1,0:T(8,128)(2,1)}, bf16[512,512]{1,0:T(8,128)(2,1)}, u32[]{:S(2)}, u32[]{:S(2)}) collective-permute-start(bf16[512,512]{1,0:T(8,128)(2,1)} %chunks.7.refs_0_), channel_id=1, source_target_pairs={{0,8}} | collective-permute-start | bytes 1572872 | tf_op jit(solution)/shard_map/ppermute | solution.py:482
  9.8 12.1 %collective-permute-start.11 = (bf16[768,1024]{1,0:T(8,128)(2,1)}, bf16[768,1024]{1,0:T(8,128)(2,1)}, u32[]{:S(2)}, u32[]{:S(2)}) collective-permute-start(bf16[768,1024]{1,0:T(8,128)(2,1)} %get-tuple-element.27), channel_id=1, source_target_pairs={{0,1},{8,9},{16,17},{24,25}} | collective-permute-start | bytes 4718600 | tf_op jit(solution)/shard_map/ppermute | solution.py:516
  11.7 2.3 collective-permute-start
  14.1 7.8 %collective-permute-start.1 = (f32[256,256]{1,0:T(8,128)S(1)}, f32[256,256]{1,0:T(8,128)S(1)}, u32[]{:S(2)}, u32[]{:S(2)}) collective-permute-start(f32[256,256]{1,0:T(8,128)S(1)} %slice_select_fusion), channel_id=1, source_target_pairs={{0,2},{1,3},{2,0},{3,1},{4,6},{5,7},{6,4},{7,5},{8,10},{9,11},{10,... | collective-permute-start | bytes 786440 | tf_op jit(solution)/shard_map/ppermute | solution.py:537
  16.1 56.4 %collective-permute-start.15 = (bf16[512,1024]{1,0:T(8,128)(2,1)}, bf16[512,1024]{1,0:T(8,128)(2,1)}, u32[]{:S(2)}, u32[]{:S(2)}) collective-permute-start(bf16[512,1024]{1,0:T(8,128)(2,1)} %get-tuple-element.32), channel_id=1, source_target_pairs={{0,1},{8,9},{16,17},{24,25}} | collective-permute-start | bytes 3145736 | tf_op jit(solution)/shard_map/ppermute | solution.py:516
  18.6 55.5 %collective-permute-start.19 = (bf16[512,1024]{1,0:T(8,128)(2,1)}, bf16[512,1024]{1,0:T(8,128)(2,1)}, u32[]{:S(2)}, u32[]{:S(2)}) collective-permute-start(bf16[512,1024]{1,0:T(8,128)(2,1)} %get-tuple-element.34), channel_id=1, source_target_pairs={{0,1},{8,9},{16,17},{24,25}} | collective-permute-start | bytes 3145736 | tf_op jit(solution)/shard_map/ppermute | solution.py:516
  20.2 56.9 %collective-permute-start.23 = (bf16[512,1024]{1,0:T(8,128)(2,1)}, bf16[512,1024]{1,0:T(8,128)(2,1)}, u32[]{:S(2)}, u32[]{:S(2)}) collective-permute-start(bf16[512,1024]{1,0:T(8,128)(2,1)} %get-tuple-element.36), channel_id=1, source_target_pairs={{0,1},{8,9},{16,17},{24,25}} | collective-permute-start | bytes 3145736 | tf_op jit(solution)/shard_map/ppermute | solution.py:516
  22.0 26.4 %copy-start.38 = (s32[1,64]{1,0:T(1,128)S(1)}, s32[1,64]{1,0:T(1,128)}, u32[]{:S(2)}) copy-start(s32[1,64]{1,0:T(1,128)} %param.11) | copy-start | bytes 772
  23.6 49.1 %copy-start.2 = (bf16[768,1024]{1,0:T(8,128)(2,1)}, bf16[768,1024]{1,0:T(8,128)(2,1)S(1)}, u32[]{:S(2)}) copy-start(bf16[768,1024]{1,0:T(8,128)(2,1)S(1)} %broadcast_select_fusion.refs_0_.refs_12_) | copy-start | bytes 4718596
  23.6 48.9 %copy-start.31 = (bf16[512,1024]{1,0:T(8,128)(2,1)S(1)}, bf16[512,1024]{1,0:T(8,128)(2,1)}, u32[]{:S(2)}) copy-start(bf16[512,1024]{1,0:T(8,128)(2,1)} %get-tuple-element.33) | copy-start | bytes 3145732
  23.6 52.1 %collective-permute-start.12 = (bf16[768,1024]{1,0:T(8,128)(2,1)S(1)}, bf16[768,1024]{1,0:T(8,128)(2,1)S(1)}, u32[]{:S(2)}, u32[]{:S(2)}) collective-permute-start(bf16[768,1024]{1,0:T(8,128)(2,1)S(1)} %broadcast_select_fusion.refs_0_.refs_12_), channel_id=1, source_target_pairs={{0,2},{1,5},{8,10},{9,13},{16,18},{17,21},{24,26},{25,29}} | collective-permute-start | bytes 4718600 | tf_op jit(solution)/shard_map/ppermute | solution.py:520
  25.2 43.6 %collective-permute-start.2 = (f32[128,256]{1,0:T(8,128)S(1)}, f32[128,256]{1,0:T(8,128)S(1)}, u32[]{:S(2)}, u32[]{:S(2)}) collective-permute-start(f32[128,256]{1,0:T(8,128)S(1)} %slice_select_fusion.1), channel_id=1, source_target_pairs={{0,4},{1,5},{2,6},{3,7},{4,0},{5,1},{6,2},{7,3},{8,12},{9,13},{10,... | collective-permute-start | bytes 393224 | tf_op jit(solution)/shard_map/ppermute | solution.py:537
  68.8 3.6 collective-permute-start.3
  72.4 6.2 %collective-permute-start.4 = (bf16[1,2,144,256]{3,2,1,0:T(8,128)(2,1)S(1)}, bf16[1,2,144,256]{3,2,1,0:T(8,128)(2,1)S(1)}, u32[]{:S(2)}, u32[]{:S(2)}) collective-permute-start(bf16[1,2,144,256]{3,2,1,0:T(8,128)(2,1)S(1)} %pad_maximum_fusion.4), channel_id=1, source_target_pairs={{0,16},{8,24},{16,0},{24,8},{1,17},{9,25},{17,1},{25,9},{2,18},{10... | collective-permute-start | bytes 442376 | tf_op jit(solution)/shard_map/ppermute | solution.py:543
  72.6 44.6 %collective-permute-start.16 = (bf16[512,1024]{1,0:T(8,128)(2,1)S(1)}, bf16[512,1024]{1,0:T(8,128)(2,1)S(1)}, u32[]{:S(2)}, u32[]{:S(2)}) collective-permute-start(bf16[512,1024]{1,0:T(8,128)(2,1)S(1)} %broadcast_select_fusion.3.refs_0_), channel_id=1, source_target_pairs={{0,2},{1,5},{8,10},{9,13},{16,18},{17,21},{24,26},{25,29}} | collective-permute-start | bytes 3145736 | tf_op jit(solution)/shard_map/ppermute | solution.py:520
  74.3 47.3 %collective-permute-start.20 = (bf16[512,1024]{1,0:T(8,128)(2,1)S(1)}, bf16[512,1024]{1,0:T(8,128)(2,1)S(1)}, u32[]{:S(2)}, u32[]{:S(2)}) collective-permute-start(bf16[512,1024]{1,0:T(8,128)(2,1)S(1)} %broadcast_select_fusion.2.refs_4_), channel_id=1, source_target_pairs={{0,2},{1,5},{8,10},{9,13},{16,18},{17,21},{24,26},{25,29}} | collective-permute-start | bytes 3145736 | tf_op jit(solution)/shard_map/ppermute | solution.py:520
  75.7 50.6 %collective-permute-start.13 = (bf16[768,1024]{1,0:T(8,128)(2,1)S(1)}, bf16[768,1024]{1,0:T(8,128)(2,1)S(1)}, u32[]{:S(2)}, u32[]{:S(2)}) collective-permute-start(bf16[768,1024]{1,0:T(8,128)(2,1)S(1)} %collective-permute-done.12.refs_1_.refs_13_), channel_id=1, source_target_pairs={{2,6},{5,7},{10,14},{13,15},{18,22},{21,23},{26,30},{29,31}} | collective-permute-start | bytes 4718600 | tf_op jit(solution)/shard_map/ppermute | solution.py:520
  77.3 49.0 %copy-start.13 = (bf16[512,1024]{1,0:T(8,128)(2,1)}, bf16[512,1024]{1,0:T(8,128)(2,1)S(1)}, u32[]{:S(2)}) copy-start(bf16[512,1024]{1,0:T(8,128)(2,1)S(1)} %broadcast_select_fusion.1.refs_8_) | copy-start | bytes 3145732
  77.3 46.6 %collective-permute-start.24 = (bf16[512,1024]{1,0:T(8,128)(2,1)S(1)}, bf16[512,1024]{1,0:T(8,128)(2,1)S(1)}, u32[]{:S(2)}, u32[]{:S(2)}) collective-permute-start(bf16[512,1024]{1,0:T(8,128)(2,1)S(1)} %broadcast_select_fusion.1.refs_8_), channel_id=1, source_target_pairs={{0,2},{1,5},{8,10},{9,13},{16,18},{17,21},{24,26},{25,29}} | collective-permute-start | bytes 3145736 | tf_op jit(solution)/shard_map/ppermute | solution.py:520
  78.6 38.5 %collective-permute-start.5 = (bf16[1,4,144,256]{3,2,1,0:T(8,128)(2,1)S(1)}, bf16[1,4,144,256]{3,2,1,0:T(8,128)(2,1)S(1)}, u32[]{:S(2)}, u32[]{:S(2)}) collective-permute-start(bf16[1,4,144,256]{3,2,1,0:T(8,128)(2,1)S(1)} %pad_maximum_fusion.3), channel_id=1, source_target_pairs={{0,4},{1,5},{2,6},{3,7},{4,0},{5,1},{6,2},{7,3},{8,12},{9,13},{10,... | collective-permute-start | bytes 884744 | tf_op jit(solution)/shard_map/ppermute | solution.py:546
  117.2 9.0 %collective-permute-start.6 = (bf16[2,4,144,256]{3,2,1,0:T(8,128)(2,1)S(1)}, bf16[2,4,144,256]{3,2,1,0:T(8,128)(2,1)S(1)}, u32[]{:S(2)}, u32[]{:S(2)}) collective-permute-start(bf16[2,4,144,256]{3,2,1,0:T(8,128)(2,1)S(1)} %pad_maximum_fusion.1), channel_id=1, source_target_pairs={{0,2},{1,3},{2,0},{3,1},{4,6},{5,7},{6,4},{7,5},{8,10},{9,11},{10,... | collective-permute-start | bytes 1769480 | tf_op jit(solution)/shard_map/ppermute | solution.py:546
  117.3 18.0 %collective-permute-start.17 = (bf16[512,1024]{1,0:T(8,128)(2,1)S(1)}, bf16[512,1024]{1,0:T(8,128)(2,1)}, u32[]{:S(2)}, u32[]{:S(2)}) collective-permute-start(bf16[512,1024]{1,0:T(8,128)(2,1)S(1)} %collective-permute-done.16.refs_1_), channel_id=1, source_target_pairs={{2,6},{5,7},{10,14},{13,15},{18,22},{21,23},{26,30},{29,31}} | collective-permute-start | bytes 3145736 | tf_op jit(solution)/shard_map/ppermute | solution.py:520
  121.6 13.7 %copy-start.27 = (bf16[512,1024]{1,0:T(8,128)(2,1)}, bf16[512,1024]{1,0:T(8,128)(2,1)S(1)}, u32[]{:S(2)}) copy-start(bf16[512,1024]{1,0:T(8,128)(2,1)S(1)} %collective-permute-done.20.refs_5_) | copy-start | bytes 3145732
  121.6 25.0 %collective-permute-start.21 = (bf16[512,1024]{1,0:T(8,128)(2,1)S(1)}, bf16[512,1024]{1,0:T(8,128)(2,1)}, u32[]{:S(2)}, u32[]{:S(2)}) collective-permute-start(bf16[512,1024]{1,0:T(8,128)(2,1)S(1)} %collective-permute-done.20.refs_5_), channel_id=1, source_target_pairs={{2,6},{5,7},{10,14},{13,15},{18,22},{21,23},{26,30},{29,31}} | collective-permute-start | bytes 3145736 | tf_op jit(solution)/shard_map/ppermute | solution.py:520
  123.9 22.7 %copy-start.28 = (bf16[512,1024]{1,0:T(8,128)(2,1)}, bf16[512,1024]{1,0:T(8,128)(2,1)S(1)}, u32[]{:S(2)}) copy-start(bf16[512,1024]{1,0:T(8,128)(2,1)S(1)} %collective-permute-done.24.refs_9_) | copy-start | bytes 3145732
  123.9 33.9 %collective-permute-start.25 = (bf16[512,1024]{1,0:T(8,128)(2,1)S(1)}, bf16[512,1024]{1,0:T(8,128)(2,1)}, u32[]{:S(2)}, u32[]{:S(2)}) collective-permute-start(bf16[512,1024]{1,0:T(8,128)(2,1)S(1)} %collective-permute-done.24.refs_9_), channel_id=1, source_target_pairs={{2,6},{5,7},{10,14},{13,15},{18,22},{21,23},{26,30},{29,31}} | collective-permute-start | bytes 3145736 | tf_op jit(solution)/shard_map/ppermute | solution.py:520
  126.2 33.2 %copy-start.25 = (bf16[4,4,144,256]{3,2,1,0:T(8,128)(2,1)}, bf16[4,4,144,256]{3,2,1,0:T(8,128)(2,1)S(1)}, u32[]{:S(2)}) copy-start(bf16[4,4,144,256]{3,2,1,0:T(8,128)(2,1)S(1)} %pad_maximum_fusion.own_ref) | copy-start | bytes 3538948
  126.3 33.2 %collective-permute-start.7 = (bf16[4,4,144,256]{3,2,1,0:T(8,128)(2,1)S(1)}, bf16[4,4,144,256]{3,2,1,0:T(8,128)(2,1)}, u32[]{:S(2)}, u32[]{:S(2)}) collective-permute-start(bf16[4,4,144,256]{3,2,1,0:T(8,128)(2,1)S(1)} %pad_maximum_fusion.own_ref), channel_id=1, source_target_pairs={{0,1},{1,0},{2,3},{3,2},{4,5},{5,4},{6,7},{7,6},{8,9},{9,8},{10,11... | collective-permute-start | bytes 3538952 | tf_op jit(solution)/shard_map/ppermute | solution.py:546
  126.4 42.5 %copy-start.6 = (bf16[768,1024]{1,0:T(8,128)(2,1)}, bf16[768,1024]{1,0:T(8,128)(2,1)S(1)}, u32[]{:S(2)}) copy-start(bf16[768,1024]{1,0:T(8,128)(2,1)S(1)} %collective-permute-done.13.refs_2_.refs_14_) | copy-start | bytes 4718596
  126.4 42.5 %collective-permute-start.14 = (bf16[768,1024]{1,0:T(8,128)(2,1)S(1)}, bf16[768,1024]{1,0:T(8,128)(2,1)}, u32[]{:S(2)}, u32[]{:S(2)}) collective-permute-start(bf16[768,1024]{1,0:T(8,128)(2,1)S(1)} %collective-permute-done.13.refs_2_.refs_14_), channel_id=1, source_target_pairs={{6,4},{7,3},{14,12},{15,11},{22,20},{23,19},{30,28},{31,27}} | collective-permute-start | bytes 4718600 | tf_op jit(solution)/shard_map/ppermute | solution.py:520
  135.3 37.6 %collective-permute-start.18 = (bf16[512,1024]{1,0:T(8,128)(2,1)}, bf16[512,1024]{1,0:T(8,128)(2,1)}, u32[]{:S(2)}, u32[]{:S(2)}) collective-permute-start(bf16[512,1024]{1,0:T(8,128)(2,1)} %collective-permute-done.17.refs_2_), channel_id=1, source_target_pairs={{6,4},{7,3},{14,12},{15,11},{22,20},{23,19},{30,28},{31,27}} | collective-permute-start | bytes 3145736 | tf_op jit(solution)/shard_map/ppermute | solution.py:520
  146.5 26.4 %collective-permute-start.22 = (bf16[512,1024]{1,0:T(8,128)(2,1)}, bf16[512,1024]{1,0:T(8,128)(2,1)}, u32[]{:S(2)}, u32[]{:S(2)}) collective-permute-start(bf16[512,1024]{1,0:T(8,128)(2,1)} %collective-permute-done.21.refs_6_), channel_id=1, source_target_pairs={{6,4},{7,3},{14,12},{15,11},{22,20},{23,19},{30,28},{31,27}} | collective-permute-start | bytes 3145736 | tf_op jit(solution)/shard_map/ppermute | solution.py:520
  157.8 15.1 %collective-permute-start.26 = (bf16[512,1024]{1,0:T(8,128)(2,1)}, bf16[512,1024]{1,0:T(8,128)(2,1)}, u32[]{:S(2)}, u32[]{:S(2)}) collective-permute-start(bf16[512,1024]{1,0:T(8,128)(2,1)} %collective-permute-done.25.refs_10_), channel_id=1, source_target_pairs={{6,4},{7,3},{14,12},{15,11},{22,20},{23,19},{30,28},{31,27}} | collective-permute-start | bytes 3145736 | tf_op jit(solution)/shard_map/ppermute | solution.py:520
  182.3 172.0 %collective-permute-start.27 = (bf16[2048,1280]{1,0:T(8,128)(2,1)}, bf16[2048,1280]{1,0:T(8,128)(2,1)}, u32[]{:S(2)}, u32[]{:S(2)}) collective-permute-start(bf16[2048,1280]{1,0:T(8,128)(2,1)} %row_panel.1.mine.other), channel_id=1, source_target_pairs={{0,1},{1,0},{2,3},{3,2},{4,5},{5,4},{6,7},{7,6},{8,9},{9,8},{10,11... | collective-permute-start | bytes 15728648 | tf_op jit(solution)/shard_map/ppermute | solution.py:557
  193.1 16.9 %collective-permute-start.31 = (bf16[1024,256]{1,0:T(8,128)(2,1)}, bf16[1024,256]{1,0:T(8,128)(2,1)S(1)}, u32[]{:S(2)}, u32[]{:S(2)}) collective-permute-start(bf16[1024,256]{1,0:T(8,128)(2,1)} %get-tuple-element.42.refs_4_), channel_id=1, source_target_pairs={{0,8},{8,16},{16,24},{1,9},{9,17},{17,25},{2,10},{10,18},{18,26},{... | collective-permute-start | bytes 1572872 | tf_op jit(solution)/shard_map/ppermute | solution.py:499
  196.2 25.0 %collective-permute-start.28 = (bf16[1024,256]{1,0:T(8,128)(2,1)}, bf16[1024,256]{1,0:T(8,128)(2,1)S(1)}, u32[]{:S(2)}, u32[]{:S(2)}) collective-permute-start(bf16[1024,256]{1,0:T(8,128)(2,1)} %get-tuple-element.39.refs_0_), channel_id=1, source_target_pairs={{0,8},{8,16},{16,24},{1,9},{9,17},{17,25},{2,10},{10,18},{18,26},{... | collective-permute-start | bytes 1572872 | tf_op jit(solution)/shard_map/ppermute | solution.py:499
  198.9 22.3 %copy-start.36 = (bf16[1024,256]{1,0:T(8,128)(2,1)S(1)}, bf16[1024,256]{1,0:T(8,128)(2,1)}, u32[]{:S(2)}) copy-start(bf16[1024,256]{1,0:T(8,128)(2,1)} %get-tuple-element.40) | copy-start | bytes 1572868
  210.0 13.9 %copy-start.18 = (bf16[1024,256]{1,0:T(8,128)(2,1)}, bf16[1024,256]{1,0:T(8,128)(2,1)S(1)}, u32[]{:S(2)}) copy-start(bf16[1024,256]{1,0:T(8,128)(2,1)S(1)} %broadcast_select_fusion.7.refs_12_) | copy-start | bytes 1572868
  210.1 22.4 %collective-permute-start.32 = (bf16[1024,256]{1,0:T(8,128)(2,1)S(1)}, bf16[1024,256]{1,0:T(8,128)(2,1)S(1)}, u32[]{:S(2)}, u32[]{:S(2)}) collective-permute-start(bf16[1024,256]{1,0:T(8,128)(2,1)S(1)} %broadcast_select_fusion.7.refs_12_), channel_id=1, source_target_pairs={{0,8},{8,16},{16,24},{1,9},{9,17},{17,25},{2,10},{10,18},{18,26},{... | collective-permute-start | bytes 1572872 | tf_op jit(solution)/shard_map/ppermute | solution.py:499
  221.3 22.4 %collective-permute-start.29 = (bf16[1024,256]{1,0:T(8,128)(2,1)S(1)}, bf16[1024,256]{1,0:T(8,128)(2,1)S(1)}, u32[]{:S(2)}, u32[]{:S(2)}) collective-permute-start(bf16[1024,256]{1,0:T(8,128)(2,1)S(1)} %broadcast_select_fusion.9.refs_8_), channel_id=1, source_target_pairs={{0,8},{8,16},{16,24},{1,9},{9,17},{17,25},{2,10},{10,18},{18,26},{... | collective-permute-start | bytes 1572872 | tf_op jit(solution)/shard_map/ppermute | solution.py:499
  224.0 19.7 %copy-start.35 = (bf16[1024,256]{1,0:T(8,128)(2,1)S(1)}, bf16[1024,256]{1,0:T(8,128)(2,1)}, u32[]{:S(2)}) copy-start(bf16[1024,256]{1,0:T(8,128)(2,1)} %get-tuple-element.41) | copy-start | bytes 1572868
  232.5 22.5 %copy-start.34 = (bf16[1024,256]{1,0:T(8,128)(2,1)S(1)}, bf16[1024,256]{1,0:T(8,128)(2,1)}, u32[]{:S(2)}) copy-start(bf16[1024,256]{1,0:T(8,128)(2,1)} %get-tuple-element.46) | copy-start | bytes 1572868
  232.5 22.4 %copy-start.20 = (bf16[1024,256]{1,0:T(8,128)(2,1)}, bf16[1024,256]{1,0:T(8,128)(2,1)S(1)}, u32[]{:S(2)}) copy-start(bf16[1024,256]{1,0:T(8,128)(2,1)S(1)} %broadcast_select_fusion.6.refs_4_) | copy-start | bytes 1572868
  232.5 22.4 %collective-permute-start.33 = (bf16[1024,256]{1,0:T(8,128)(2,1)S(1)}, bf16[1024,256]{1,0:T(8,128)(2,1)S(1)}, u32[]{:S(2)}, u32[]{:S(2)}) collective-permute-start(bf16[1024,256]{1,0:T(8,128)(2,1)S(1)} %broadcast_select_fusion.6.refs_4_), channel_id=1, source_target_pairs={{0,8},{8,16},{16,24},{1,9},{9,17},{17,25},{2,10},{10,18},{18,26},{... | collective-permute-start | bytes 1572872 | tf_op jit(solution)/shard_map/ppermute | solution.py:499
  243.7 11.3 %copy-start.10 = (bf16[1024,256]{1,0:T(8,128)(2,1)}, bf16[1024,256]{1,0:T(8,128)(2,1)S(1)}, u32[]{:S(2)}) copy-start(bf16[1024,256]{1,0:T(8,128)(2,1)S(1)} %collective-permute-done.29.refs_2_.refs_9_) | copy-start | bytes 1572868
  243.7 22.5 %copy-start.33 = (bf16[1024,256]{1,0:T(8,128)(2,1)S(1)}, bf16[1024,256]{1,0:T(8,128)(2,1)}, u32[]{:S(2)}) copy-start(bf16[1024,256]{1,0:T(8,128)(2,1)} %get-tuple-element.45) | copy-start | bytes 1572868
  243.8 22.4 %copy-start.21 = (bf16[1024,256]{1,0:T(8,128)(2,1)}, bf16[1024,256]{1,0:T(8,128)(2,1)S(1)}, u32[]{:S(2)}) copy-start(bf16[1024,256]{1,0:T(8,128)(2,1)S(1)} %broadcast_select_fusion.8.refs_0_) | copy-start | bytes 1572868
  243.8 22.4 %collective-permute-start.30 = (bf16[1024,256]{1,0:T(8,128)(2,1)S(1)}, bf16[1024,256]{1,0:T(8,128)(2,1)S(1)}, u32[]{:S(2)}, u32[]{:S(2)}) collective-permute-start(bf16[1024,256]{1,0:T(8,128)(2,1)S(1)} %broadcast_select_fusion.8.refs_0_), channel_id=1, source_target_pairs={{0,8},{8,16},{16,24},{1,9},{9,17},{17,25},{2,10},{10,18},{18,26},{... | collective-permute-start | bytes 1572872 | tf_op jit(solution)/shard_map/ppermute | solution.py:499
  254.9 11.3 %copy-start.3 = (bf16[1024,256]{1,0:T(8,128)(2,1)}, bf16[1024,256]{1,0:T(8,128)(2,1)S(1)}, u32[]{:S(2)}) copy-start(bf16[1024,256]{1,0:T(8,128)(2,1)S(1)} %collective-permute-done.33.refs_7_.refs_14_.refs_5_) | copy-start | bytes 1572868
  255.0 56.1 %copy-start.22 = (bf16[1024,256]{1,0:T(8,128)(2,1)}, bf16[1024,256]{1,0:T(8,128)(2,1)S(1)}, u32[]{:S(2)}) copy-start(bf16[1024,256]{1,0:T(8,128)(2,1)S(1)} %broadcast_select_fusion.4.refs_12_) | copy-start | bytes 1572868
  255.0 22.4 %collective-permute-start.35 = (bf16[1024,256]{1,0:T(8,128)(2,1)S(1)}, bf16[1024,256]{1,0:T(8,128)(2,1)S(1)}, u32[]{:S(2)}, u32[]{:S(2)}) collective-permute-start(bf16[1024,256]{1,0:T(8,128)(2,1)S(1)} %broadcast_select_fusion.4.refs_12_), channel_id=1, source_target_pairs={{0,8},{8,16},{16,24},{1,9},{9,17},{17,25},{2,10},{10,18},{18,26},{... | collective-permute-start | bytes 1572872 | tf_op jit(solution)/shard_map/ppermute | solution.py:499
  266.2 46.9 %copy-start.4 = (bf16[1024,256]{1,0:T(8,128)(2,1)}, bf16[1024,256]{1,0:T(8,128)(2,1)S(1)}, u32[]{:S(2)}) copy-start(bf16[1024,256]{1,0:T(8,128)(2,1)S(1)} %collective-permute-done.30.refs_3_.refs_10_.refs_1_) | copy-start | bytes 1572868
  266.2 54.1 %copy-start.23 = (bf16[1024,256]{1,0:T(8,128)(2,1)}, bf16[1024,256]{1,0:T(8,128)(2,1)S(1)}, u32[]{:S(2)}) copy-start(bf16[1024,256]{1,0:T(8,128)(2,1)S(1)} %broadcast_select_fusion.5.refs_8_) | copy-start | bytes 1572868
  266.2 22.4 %collective-permute-start.34 = (bf16[1024,256]{1,0:T(8,128)(2,1)S(1)}, bf16[1024,256]{1,0:T(8,128)(2,1)S(1)}, u32[]{:S(2)}, u32[]{:S(2)}) collective-permute-start(bf16[1024,256]{1,0:T(8,128)(2,1)S(1)} %broadcast_select_fusion.5.refs_8_), channel_id=1, source_target_pairs={{0,8},{8,16},{16,24},{1,9},{9,17},{17,25},{2,10},{10,18},{18,26},{... | collective-permute-start | bytes 1572872 | tf_op jit(solution)/shard_map/ppermute | solution.py:499
  277.4 35.6 %copy-start.7 = (bf16[1024,256]{1,0:T(8,128)(2,1)}, bf16[1024,256]{1,0:T(8,128)(2,1)S(1)}, u32[]{:S(2)}) copy-start(bf16[1024,256]{1,0:T(8,128)(2,1)S(1)} %collective-permute-done.35.refs_15_.refs_6_.refs_13_) | copy-start | bytes 1572868
  277.4 22.5 %collective-permute-start.37 = (bf16[1024,256]{1,0:T(8,128)(2,1)S(1)}, bf16[1024,256]{1,0:T(8,128)(2,1)S(1)}, u32[]{:S(2)}, u32[]{:S(2)}) collective-permute-start(bf16[1024,256]{1,0:T(8,128)(2,1)S(1)} %collective-permute-done.35.refs_15_.refs_6_.refs_13_), channel_id=1, source_target_pairs={{0,8},{8,16},{16,24},{1,9},{9,17},{17,25},{2,10},{10,18},{18,26},{... | collective-permute-start | bytes 1572872 | tf_op jit(solution)/shard_map/ppermute | solution.py:499
  288.6 24.4 %copy-start.8 = (bf16[1024,256]{1,0:T(8,128)(2,1)}, bf16[1024,256]{1,0:T(8,128)(2,1)S(1)}, u32[]{:S(2)}) copy-start(bf16[1024,256]{1,0:T(8,128)(2,1)S(1)} %collective-permute-done.34.refs_11_.refs_2_.refs_9_) | copy-start | bytes 1572868
  288.6 22.5 %collective-permute-start.36 = (bf16[1024,256]{1,0:T(8,128)(2,1)S(1)}, bf16[1024,256]{1,0:T(8,128)(2,1)S(1)}, u32[]{:S(2)}, u32[]{:S(2)}) collective-permute-start(bf16[1024,256]{1,0:T(8,128)(2,1)S(1)} %collective-permute-done.34.refs_11_.refs_2_.refs_9_), channel_id=1, source_target_pairs={{0,8},{8,16},{16,24},{1,9},{9,17},{17,25},{2,10},{10,18},{18,26},{... | collective-permute-start | bytes 1572872 | tf_op jit(solution)/shard_map/ppermute | solution.py:499
  299.9 20.4 %copy-start.14 = (bf16[1024,256]{1,0:T(8,128)(2,1)}, bf16[1024,256]{1,0:T(8,128)(2,1)S(1)}, u32[]{:S(2)}) copy-start(bf16[1024,256]{1,0:T(8,128)(2,1)S(1)} %collective-permute-done.37.refs_7_.refs_14_) | copy-start | bytes 1572868
  299.9 22.6 %collective-permute-start.39 = (bf16[1024,256]{1,0:T(8,128)(2,1)S(1)}, bf16[1024,256]{1,0:T(8,128)(2,1)}, u32[]{:S(2)}, u32[]{:S(2)}) collective-permute-start(bf16[1024,256]{1,0:T(8,128)(2,1)S(1)} %collective-permute-done.37.refs_7_.refs_14_), channel_id=1, source_target_pairs={{0,8},{8,16},{16,24},{1,9},{9,17},{17,25},{2,10},{10,18},{18,26},{... | collective-permute-start | bytes 1572872 | tf_op jit(solution)/shard_map/ppermute | solution.py:499
  311.1 22.6 %collective-permute-start.38 = (bf16[1024,256]{1,0:T(8,128)(2,1)S(1)}, bf16[1024,256]{1,0:T(8,128)(2,1)}, u32[]{:S(2)}, u32[]{:S(2)}) collective-permute-start(bf16[1024,256]{1,0:T(8,128)(2,1)S(1)} %collective-permute-done.36.refs_3_.refs_10_), channel_id=1, source_target_pairs={{0,8},{8,16},{16,24},{1,9},{9,17},{17,25},{2,10},{10,18},{18,26},{... | collective-permute-start | bytes 1572872 | tf_op jit(solution)/shard_map/ppermute | solution.py:499
  354.3 32.7 %copy-start.1 = (bf16[1024,1024]{1,0:T(8,128)(2,1)S(1)}, bf16[1024,1024]{1,0:T(8,128)(2,1)}, u32[]{:S(2)}) copy-start(bf16[1024,1024]{1,0:T(8,128)(2,1)} %param.7) | copy-start | bytes 6291460
  (15 other events, 69.1 us)

commit v4 on v3

--- a/solution.py
+++ b/solution.py
@@ -18,7 +18,8 @@
 PIVOT_CHUNK = 3
 PLANE_GROUPS = ((0,), (1, 2), (3,))
 LINE_GROUPS = ((0, 1), (2, 3), (4, 5, 6, 7))
-ROW_BLOCK = 512
+ROW_BLOCK = 1024
+SLABS = 4
 
 
 def xor_pairs(count, bit):
@@ -126,7 +127,7 @@
     return pl.pallas_call(
         functools.partial(pivot_kernel, len(pieces), scale),
         in_specs=[pl.BlockSpec(memory_space=pltpu.SMEM), whole, whole]
-        + [pl.BlockSpec(memory_space=pl.ANY)] * len(pieces),
+        + [pl.BlockSpec(memory_space=pltpu.HBM)] * len(pieces),
         out_specs=[whole, whole],
         out_shape=[
             jax.ShapeDtypeStruct((width, width), BF16),
@@ -197,7 +198,7 @@
             whole,
             pl.BlockSpec((captions, step), lambda s: (0, s)),
         ]
-        + [pl.BlockSpec(memory_space=pl.ANY)] * (chunks * options),
+        + [pl.BlockSpec(memory_space=pltpu.HBM)] * (chunks * options),
         out_specs=pl.BlockSpec((step, stop + captions), lambda s: (s, 0)),
         out_shape=jax.ShapeDtypeStruct((rows, stop + captions), BF16),
         scratch_shapes=[pltpu.VMEM((rows, stop), BF16), pltpu.SemaphoreType.DMA((chunks,))],
@@ -257,7 +258,7 @@
         in_specs=[pl.BlockSpec(memory_space=pltpu.SMEM)]
         + [whole] * 3
         + [pl.BlockSpec((captions, columns), lambda s: (0, first_col // columns))]
-        + [pl.BlockSpec(memory_space=pl.ANY)] * (chunks * options),
+        + [pl.BlockSpec(memory_space=pltpu.HBM)] * (chunks * options),
         out_specs=whole,
         out_shape=jax.ShapeDtypeStruct((stop + captions, columns), BF16),
         scratch_shapes=[
@@ -375,15 +376,21 @@
     if dead:
         ready = ready & (info[2] != 0)
 
+    slab = rows // SLABS
+
     @pl.when(ready)
     def _():
-        loads, stores = [], []
+        loads, tails, stores = [], [], []
         for k, (row, column) in enumerate(boxes):
-            source = ridge_ref.at[pl.ds(row, rows), pl.ds(column, columns)]
-            loads.append([pltpu.make_async_copy(source, wide.at[k], in_sem.at[k])])
-            loads[k][0].start()
-            tail = outs[k].shape[0] - rows
-            part = extras[0][0].shape[1] if extras else 0
+            for q in range(SLABS):
+                source = ridge_ref.at[pl.ds(row + q * slab, slab), pl.ds(column, columns)]
+                target = wide.at[k, pl.ds(q * slab, slab)]
+                loads.append(pltpu.make_async_copy(source, target, in_sem.at[k * SLABS + q]))
+                loads[-1].start()
+        tail = outs[0].shape[0] - rows
+        part = extras[0][0].shape[1] if extras else 0
+        used = count * SLABS
+        for k in range(count if extras else 0):
             for index, options in enumerate(extras):
                 for side in range(2):
                     target = narrow.at[
@@ -391,22 +398,31 @@
                         pl.ds(rows, tail),
                         pl.ds(side * columns // 2 + index * part, part),
                     ]
-                    sem = in_sem.at[count + (2 * index + side) * count + k]
                     for z, option in enumerate(options):
                         source = option.at[pl.ds(side * tail, tail)]
-                        load = pltpu.make_async_copy(source, target, sem)
+                        load = pltpu.make_async_copy(source, target, in_sem.at[used])
 
                         @pl.when(info[1] == z)
                         def _():
                             load.start()
 
-                    loads[k].append(load)
+                    tails.append(load)
+                    used = used + 1
         for k in range(count):
-            for load in loads[k]:
-                load.wait()
-            narrow[k, :rows] = wide[k].astype(BF16)
-            stores.append(pltpu.make_async_copy(narrow.at[k], outs[k], out_sem.at[k]))
-            stores[k].start()
+            for q in range(SLABS):
+                here = pl.ds(q * slab, slab)
+                loads[k * SLABS + q].wait()
+                narrow[k, q * slab : (q + 1) * slab] = wide[k, q * slab : (q + 1) * slab].astype(BF16)
+                sem = out_sem.at[k * SLABS + q]
+                stores.append(pltpu.make_async_copy(narrow.at[k, here], outs[k].at[here], sem))
+                stores[-1].start()
+        for load in tails:
+            load.wait()
+        for k in range(count if extras else 0):
+            here = pl.ds(rows, tail)
+            sem = out_sem.at[count * SLABS + k]
+            stores.append(pltpu.make_async_copy(narrow.at[k, here], outs[k].at[here], sem))
+            stores[-1].start()
         for store in stores:
             store.wait()
 
@@ -426,8 +442,8 @@
         scratch_shapes=[
             pltpu.VMEM((count, rows, columns), F32),
             pltpu.VMEM((count, total, columns), BF16),
-            pltpu.SemaphoreType.DMA(((1 + 2 * len(extras)) * count,)),
-            pltpu.SemaphoreType.DMA((count,)),
+            pltpu.SemaphoreType.DMA(((SLABS + 2 * len(extras)) * count,)),
+            pltpu.SemaphoreType.DMA(((SLABS + 1) * count,)),
         ],
         cost_estimate=pl.CostEstimate(
             flops=0, bytes_accessed=6 * count * rows * columns, transcendentals=0

time: 388 us -> 389 us (level)
  no operation moved by 1% of the time
where the time goes in v4:
time: 389 us; the launch traced here: 387 us
  waiting for transfers between devices  191 us (49%)
  starting transfers between devices  98.4 us (25%)
  Pallas kernels  90 us (23%)
    ppermute x12, waiting for transfers between devices, per_device(): lax.ppermute(piece, 'row', [(z - 1, z) for z in range(1, row_count)])  105 us
    pallas_call x2, Pallas kernels, update(): pl.pallas_call(functools.partial(update_kernel, (work, parts, stop, block...  46.7 us
    ppermute x3, waiting for transfers between devices, per_device(): got = lax.ppermute(held, 'col', xor_pairs(col_count, 1 << k))  34.4 us
    ppermute x12, waiting for transfers between devices, per_device(): hops.append(lax.ppermute(hops[-1], 'col', perm))  26 us
    ppermute x12, starting transfers between devices, per_device(): lax.ppermute(piece, 'row', [(z - 1, z) for z in range(1, row_count)])  25.7 us
    ppermute x3, starting transfers between devices, per_device(): got = lax.ppermute(send, 'col', xor_pairs(col_count, 1 << k))  24.7 us
    ppermute x12, starting transfers between devices, per_device(): hops.append(lax.ppermute(hops[-1], 'col', perm))  23 us
    ppermute x3, waiting for transfers between devices, per_device(): got = lax.ppermute(send, 'col', xor_pairs(col_count, 1 << k))  21.9 us
  transfers between devices with their start and end apart: 40, of which 19 were waited for; matrix products, arithmetic and copies ran while one was open for 1% of the time, Pallas kernels for 12%

profile of v4, /device:TPU:13, one launch (start us, length us, event | category | flops | bytes accessed | tf_op | source)
XLA Modules:
  0.0 387.5 jit_solution(2940716212477117788)
XLA Ops:
  2.1 1.5 collective-permute-start.9
  3.6 1.4 collective-permute-start.8
  6.7 1.7 fusion.3
  10.0 1.8 collective-permute-start.11
  12.6 1.5 collective-permute-done
  14.3 1.3 collective-permute-start.1
  16.4 1.7 collective-permute-start.15
  18.1 1.0 chunks.10
  19.1 1.6 collective-permute-start.19
  20.8 1.7 collective-permute-start.23
  22.5 1.6 broadcast_select_fusion.refs_0_.refs_12_
  24.1 1.6 collective-permute-start.12
  25.7 22.7 %collective-permute-start.2 = (f32[128,256]{1,0:T(8,128)S(1)}, f32[128,256]{1,0:T(8,128)S(1)}, u32[]{:S(2)}, u32[]{:S(2)}) collective-permute-start(f32[128,256]{1,0:T(8,128)S(1)} %slice_select_fusion.1), channel_id=1, source_target_pairs={{0,4},{1,5},{2,6},{3,7},{4,0},{5,1},{6,2},{7,3},{8,12},{9,13},{10,... | collective-permute-start | bytes 393224 | tf_op jit(solution)/shard_map/ppermute | solution.py:553
  48.5 20.4 %collective-permute-done.2 = f32[128,256]{1,0:T(8,128)S(1)} collective-permute-done((f32[128,256]{1,0:T(8,128)S(1)}, f32[128,256]{1,0:T(8,128)S(1)}, u32[]{:S(2)}, u32[]{:S(2)}) %collective-permute-start.2) | collective-permute-done | bytes 131104 | tf_op jit(solution)/shard_map/ppermute | solution.py:553
  69.0 3.5 collective-permute-done.3
  72.7 1.4 collective-permute-start.16
  74.3 1.4 collective-permute-start.20
  75.8 1.4 collective-permute-start.13
  77.4 1.3 collective-permute-start.24
  78.7 4.1 %collective-permute-start.5 = (bf16[1,4,144,256]{3,2,1,0:T(8,128)(2,1)S(1)}, bf16[1,4,144,256]{3,2,1,0:T(8,128)(2,1)S(1)}, u32[]{:S(2)}, u32[]{:S(2)}) collective-permute-start(bf16[1,4,144,256]{3,2,1,0:T(8,128)(2,1)S(1)} %pad_maximum_fusion.3), channel_id=1, source_target_pairs={{0,4},{1,5},{2,6},{3,7},{4,0},{5,1},{6,2},{7,3},{8,12},{9,13},{10,... | collective-permute-start | bytes 884744 | tf_op jit(solution)/shard_map/ppermute | solution.py:562
  82.8 34.4 %collective-permute-done.5 = bf16[1,4,144,256]{3,2,1,0:T(8,128)(2,1)S(1)} collective-permute-done((bf16[1,4,144,256]{3,2,1,0:T(8,128)(2,1)S(1)}, bf16[1,4,144,256]{3,2,1,0:T(8,128)(2,1)S(1)}, u32[]{:S(2)}, u32[]{:S(2)}) %collective-permute-start.5) | collective-permute-done | bytes 294944 | tf_op jit(solution)/shard_map/ppermute | solution.py:562
  117.3 4.3 %collective-permute-start.17 = (bf16[512,1024]{1,0:T(8,128)(2,1)S(1)}, bf16[512,1024]{1,0:T(8,128)(2,1)}, u32[]{:S(2)}, u32[]{:S(2)}) collective-permute-start(bf16[512,1024]{1,0:T(8,128)(2,1)S(1)} %collective-permute-done.16.refs_1_), channel_id=1, source_target_pairs={{2,6},{5,7},{10,14},{13,15},{18,22},{21,23},{26,30},{29,31}} | collective-permute-start | bytes 3145736 | tf_op jit(solution)/shard_map/ppermute | solution.py:536
  121.6 2.3 collective-permute-start.21
  123.9 2.3 collective-permute-start.25
  126.4 2.0 collective-permute-start.14
  128.4 6.9 %collective-permute-done.17.refs_2_ = bf16[512,1024]{1,0:T(8,128)(2,1)} collective-permute-done((bf16[512,1024]{1,0:T(8,128)(2,1)S(1)}, bf16[512,1024]{1,0:T(8,128)(2,1)}, u32[]{:S(2)}, u32[]{:S(2)}) %collective-permute-start.17) | collective-permute-done | bytes 1048608 | tf_op jit(solution)/shard_map/ppermute | solution.py:536
  135.4 1.7 collective-permute-start.18
  137.1 9.5 %collective-permute-done.21.refs_6_ = bf16[512,1024]{1,0:T(8,128)(2,1)} collective-permute-done((bf16[512,1024]{1,0:T(8,128)(2,1)S(1)}, bf16[512,1024]{1,0:T(8,128)(2,1)}, u32[]{:S(2)}, u32[]{:S(2)}) %collective-permute-start.21) | collective-permute-done | bytes 1048608 | tf_op jit(solution)/shard_map/ppermute | solution.py:536
  146.6 1.7 collective-permute-start.22
  148.3 9.5 %collective-permute-done.25.refs_10_ = bf16[512,1024]{1,0:T(8,128)(2,1)} collective-permute-done((bf16[512,1024]{1,0:T(8,128)(2,1)S(1)}, bf16[512,1024]{1,0:T(8,128)(2,1)}, u32[]{:S(2)}, u32[]{:S(2)}) %collective-permute-start.25) | collective-permute-done | bytes 1048608 | tf_op jit(solution)/shard_map/ppermute | solution.py:536
  157.8 1.6 collective-permute-start.26
  159.5 9.4 %grads.1 = (bf16[256,2048]{1,0:T(8,128)(2,1)}, bf16[256,2048]{1,0:T(8,128)(2,1)}, bf16[256,1024]{1,0:T(8,128)(2,1)}) custom-call(s32[8]{0:T(128)} %compare_select_fusion.7.info, bf16[4,4,144,256]{3,2,1,0:T(8,128)(2,1)} %copy-done.25, bf16[4,4,144,256]{3,2,1,0:T(8,128)(2,1)} %collective-permute-done.7.recv_ref), custom_call_target="tpu_custom_call" | custom-call | flops 5368709120 | bytes 4980736 | tf_op jit(solution)/shard_map/grads/pallas_call | solution.py:83
  168.9 4.0 %pivot.1 = (bf16[512,512]{1,0:T(8,128)(2,1)}, bf16[2,512,512]{2,1,0:T(8,128)(2,1)}) custom-call(s32[8]{0:T(128)} %compare_select_fusion.7.info, f32[2,512,512]{2,1,0:T(8,128)} %inverse_ref.1, bf16[256,1024]{1,0:T(8,128)(2,1)} %get-tuple-element.26.panel_grads, bf16[768,1024]{1,0:T(8,128)(2,1)} %copy-done.2, bf16[768,1024]{1,0:T(8,128)(2,1)} %copy-done.5, ...), custom_call_target="tpu_custom_call" | custom-call | flops 536870912 | bytes 4194304 | tf_op jit(solution)/shard_map/pivot/pallas_call | solution.py:127
  173.0 9.4 %row_panel.1.mine.other = bf16[2048,1280]{1,0:T(8,128)(2,1)} custom-call(s32[8]{0:T(128)} %compare_select_fusion.7.info, bf16[2,512,512]{2,1,0:T(8,128)(2,1)} %get-tuple-element.29.inverse_ref, bf16[512,512]{1,0:T(8,128)(2,1)} %get-tuple-element.30.pivot_ref, bf16[256,1024]{1,0:T(8,128)(2,1)} %get-tuple-element.26.panel_grads, ...), custom_call_target="tpu_custom_call" | custom-call | flops 4294967296 | bytes 9961472 | tf_op jit(solution)/shard_map/row_panel/pallas_call | solution.py:191
  182.4 10.1 %collective-permute-start.27 = (bf16[2048,1280]{1,0:T(8,128)(2,1)}, bf16[2048,1280]{1,0:T(8,128)(2,1)}, u32[]{:S(2)}, u32[]{:S(2)}) collective-permute-start(bf16[2048,1280]{1,0:T(8,128)(2,1)} %row_panel.1.mine.other), channel_id=1, source_target_pairs={{0,1},{1,0},{2,3},{3,2},{4,5},{5,4},{6,7},{7,6},{8,9},{9,8},{10,11... | collective-permute-start | bytes 15728648 | tf_op jit(solution)/shard_map/ppermute | solution.py:573
  193.3 3.2 collective-permute-start.31
  196.5 1.9 collective-permute-start.28
  199.2 10.8 %collective-permute-done.31.refs_5_ = bf16[1024,256]{1,0:T(8,128)(2,1)S(1)} collective-permute-done((bf16[1024,256]{1,0:T(8,128)(2,1)}, bf16[1024,256]{1,0:T(8,128)(2,1)S(1)}, u32[]{:S(2)}, u32[]{:S(2)}) %collective-permute-start.31) | collective-permute-done | bytes 524320 | tf_op jit(solution)/shard_map/ppermute | solution.py:515
  210.1 2.0 collective-permute-start.32
  212.1 9.1 %collective-permute-done.28.refs_1_ = bf16[1024,256]{1,0:T(8,128)(2,1)S(1)} collective-permute-done((bf16[1024,256]{1,0:T(8,128)(2,1)}, bf16[1024,256]{1,0:T(8,128)(2,1)S(1)}, u32[]{:S(2)}, u32[]{:S(2)}) %collective-permute-start.28) | collective-permute-done | bytes 524320 | tf_op jit(solution)/shard_map/ppermute | solution.py:515
  221.3 2.0 collective-permute-start.29
  223.4 1.0 chunks.13
  224.4 8.1 %collective-permute-done.32.refs_6_.refs_13_ = bf16[1024,256]{1,0:T(8,128)(2,1)S(1)} collective-permute-done((bf16[1024,256]{1,0:T(8,128)(2,1)S(1)}, bf16[1024,256]{1,0:T(8,128)(2,1)S(1)}, u32[]{:S(2)}, u32[]{:S(2)}) %collective-permute-start.32) | collective-permute-done | bytes 524320 | tf_op jit(solution)/shard_map/ppermute | solution.py:515
  232.6 2.2 collective-permute-start.33
  234.7 9.0 %collective-permute-done.29.refs_2_.refs_9_ = bf16[1024,256]{1,0:T(8,128)(2,1)S(1)} collective-permute-done((bf16[1024,256]{1,0:T(8,128)(2,1)S(1)}, bf16[1024,256]{1,0:T(8,128)(2,1)S(1)}, u32[]{:S(2)}, u32[]{:S(2)}) %collective-permute-start.29) | collective-permute-done | bytes 524320 | tf_op jit(solution)/shard_map/ppermute | solution.py:515
  243.8 2.2 collective-permute-start.30
  246.0 9.0 %collective-permute-done.33.refs_7_.refs_14_.refs_5_ = bf16[1024,256]{1,0:T(8,128)(2,1)S(1)} collective-permute-done((bf16[1024,256]{1,0:T(8,128)(2,1)S(1)}, bf16[1024,256]{1,0:T(8,128)(2,1)S(1)}, u32[]{:S(2)}, u32[]{:S(2)}) %collective-permute-start.33) | collective-permute-done | bytes 524320 | tf_op jit(solution)/shard_map/ppermute | solution.py:515
  255.0 2.0 collective-permute-start.35
  257.1 9.1 %collective-permute-done.30.refs_3_.refs_10_.refs_1_ = bf16[1024,256]{1,0:T(8,128)(2,1)S(1)} collective-permute-done((bf16[1024,256]{1,0:T(8,128)(2,1)S(1)}, bf16[1024,256]{1,0:T(8,128)(2,1)S(1)}, u32[]{:S(2)}, u32[]{:S(2)}) %collective-permute-start.30) | collective-permute-done | bytes 524320 | tf_op jit(solution)/shard_map/ppermute | solution.py:515
  266.3 2.0 collective-permute-start.34
  268.3 9.1 %collective-permute-done.35.refs_15_.refs_6_.refs_13_ = bf16[1024,256]{1,0:T(8,128)(2,1)S(1)} collective-permute-done((bf16[1024,256]{1,0:T(8,128)(2,1)S(1)}, bf16[1024,256]{1,0:T(8,128)(2,1)S(1)}, u32[]{:S(2)}, u32[]{:S(2)}) %collective-permute-start.35) | collective-permute-done | bytes 524320 | tf_op jit(solution)/shard_map/ppermute | solution.py:515
  277.4 2.0 collective-permute-start.37
  279.4 9.2 %collective-permute-done.34.refs_11_.refs_2_.refs_9_ = bf16[1024,256]{1,0:T(8,128)(2,1)S(1)} collective-permute-done((bf16[1024,256]{1,0:T(8,128)(2,1)S(1)}, bf16[1024,256]{1,0:T(8,128)(2,1)S(1)}, u32[]{:S(2)}, u32[]{:S(2)}) %collective-permute-start.34) | collective-permute-done | bytes 524320 | tf_op jit(solution)/shard_map/ppermute | solution.py:515
  288.7 2.0 collective-permute-start.36
  290.7 9.2 %collective-permute-done.37.refs_7_.refs_14_ = bf16[1024,256]{1,0:T(8,128)(2,1)S(1)} collective-permute-done((bf16[1024,256]{1,0:T(8,128)(2,1)S(1)}, bf16[1024,256]{1,0:T(8,128)(2,1)S(1)}, u32[]{:S(2)}, u32[]{:S(2)}) %collective-permute-start.37) | collective-permute-done | bytes 524320 | tf_op jit(solution)/shard_map/ppermute | solution.py:515
  299.9 2.0 collective-permute-start.39
  301.9 9.2 %collective-permute-done.36.refs_3_.refs_10_ = bf16[1024,256]{1,0:T(8,128)(2,1)S(1)} collective-permute-done((bf16[1024,256]{1,0:T(8,128)(2,1)S(1)}, bf16[1024,256]{1,0:T(8,128)(2,1)S(1)}, u32[]{:S(2)}, u32[]{:S(2)}) %collective-permute-start.36) | collective-permute-done | bytes 524320 | tf_op jit(solution)/shard_map/ppermute | solution.py:515
  311.1 2.2 collective-permute-start.38
  313.4 7.2 %col_panel.2.refs_0_ = bf16[1280,1024]{1,0:T(8,128)(2,1)} custom-call(s32[8]{0:T(128)} %compare_select_fusion.7.info, bf16[2,512,512]{2,1,0:T(8,128)(2,1)} %get-tuple-element.29.inverse_ref, bf16[512,512]{1,0:T(8,128)(2,1)} %get-tuple-element.30.pivot_ref, bf16[256,1024]{1,0:T(8,128)(2,1)} %get-tuple-element.26.panel_grads, ...), custom_call_target="tpu_custom_call" | custom-call | flops 2147483648 | bytes 5242880 | tf_op jit(solution)/shard_map/col_panel/pallas_call | solution.py:255
  320.6 1.8 collective-permute-done.39.refs_15_
  322.5 11.2 %collective-permute-done.38.refs_11_ = bf16[1024,256]{1,0:T(8,128)(2,1)} collective-permute-done((bf16[1024,256]{1,0:T(8,128)(2,1)S(1)}, bf16[1024,256]{1,0:T(8,128)(2,1)}, u32[]{:S(2)}, u32[]{:S(2)}) %collective-permute-start.38) | collective-permute-done | bytes 524320 | tf_op jit(solution)/shard_map/ppermute | solution.py:515
  333.7 7.1 %col_panel.3.refs_1_ = bf16[1280,1024]{1,0:T(8,128)(2,1)} custom-call(s32[8]{0:T(128)} %compare_select_fusion.7.info, bf16[2,512,512]{2,1,0:T(8,128)(2,1)} %get-tuple-element.29.inverse_ref, bf16[512,512]{1,0:T(8,128)(2,1)} %get-tuple-element.30.pivot_ref, bf16[256,1024]{1,0:T(8,128)(2,1)} %get-tuple-element.26.panel_grads, ...), custom_call_target="tpu_custom_call" | custom-call | flops 2147483648 | bytes 5242880 | tf_op jit(solution)/shard_map/col_panel/pallas_call | solution.py:255
  340.8 14.6 %update.2.refs_3_ = f32[4096,2048]{1,0:T(8,128)} custom-call(s32[8]{0:T(128)} %compare_select_fusion.7.info, bf16[2048,1280]{1,0:T(8,128)(2,1)} %row_panel.1.mine.other, bf16[2048,1280]{1,0:T(8,128)(2,1)} %row_panel.1.mine.other, bf16[1280,1024]{1,0:T(8,128)(2,1)} %col_panel.2.refs_0_, f32[4096,2048]{1,0:T(8,128)} %refs_2_.1), custom_call_target="tpu_custom_call" | custom-call | flops 5368709120 | bytes 24641536 | tf_op jit(solution)/shard_map/update/pallas_call | solution.py:346
  355.5 32.0 %update.3 = f32[4096,2048]{1,0:T(8,128)} custom-call(s32[8]{0:T(128)} %compare_select_fusion.7.info, bf16[2048,1280]{1,0:T(8,128)(2,1)} %row_panel.1.mine.other, bf16[2048,1280]{1,0:T(8,128)(2,1)} %collective-permute-done.27.other, bf16[1280,1024]{1,0:T(8,128)(2,1)} %col_panel.2.refs_0_, ...), custom_call_target="tpu_custom_call", output_to_operand_aliasing={{}: (6, {})} | custom-call | flops 16106127360 | bytes 68681728 | tf_op jit(solution)/shard_map/update/pallas_call | solution.py:346
  (134 shorter events, 10.2 us)
Async XLA Ops:
  1.4 6.9 %collective-permute-start.10 = (bf16[512,512]{1,0:T(8,128)(2,1)}, bf16[512,512]{1,0:T(8,128)(2,1)S(1)}, u32[]{:S(2)}, u32[]{:S(2)}) collective-permute-start(bf16[512,512]{1,0:T(8,128)(2,1)} %chunks.7.refs_0_), channel_id=1, source_target_pairs={{0,24}} | collective-permute-start | bytes 1572872 | tf_op jit(solution)/shard_map/ppermute | solution.py:498
  2.1 6.2 %collective-permute-start.9 = (bf16[512,512]{1,0:T(8,128)(2,1)}, bf16[512,512]{1,0:T(8,128)(2,1)}, u32[]{:S(2)}, u32[]{:S(2)}) collective-permute-start(bf16[512,512]{1,0:T(8,128)(2,1)} %chunks.7.refs_0_), channel_id=1, source_target_pairs={{0,16}} | collective-permute-start | bytes 1572872 | tf_op jit(solution)/shard_map/ppermute | solution.py:498
  3.6 4.7 %collective-permute-start.8 = (bf16[512,512]{1,0:T(8,128)(2,1)}, bf16[512,512]{1,0:T(8,128)(2,1)}, u32[]{:S(2)}, u32[]{:S(2)}) collective-permute-start(bf16[512,512]{1,0:T(8,128)(2,1)} %chunks.7.refs_0_), channel_id=1, source_target_pairs={{0,8}} | collective-permute-start | bytes 1572872 | tf_op jit(solution)/shard_map/ppermute | solution.py:498
  10.0 12.5 %collective-permute-start.11 = (bf16[768,1024]{1,0:T(8,128)(2,1)}, bf16[768,1024]{1,0:T(8,128)(2,1)}, u32[]{:S(2)}, u32[]{:S(2)}) collective-permute-start(bf16[768,1024]{1,0:T(8,128)(2,1)} %get-tuple-element.27), channel_id=1, source_target_pairs={{0,1},{8,9},{16,17},{24,25}} | collective-permute-start | bytes 4718600 | tf_op jit(solution)/shard_map/ppermute | solution.py:532
  11.9 2.3 collective-permute-start
  14.3 8.2 %collective-permute-start.1 = (f32[256,256]{1,0:T(8,128)S(1)}, f32[256,256]{1,0:T(8,128)S(1)}, u32[]{:S(2)}, u32[]{:S(2)}) collective-permute-start(f32[256,256]{1,0:T(8,128)S(1)} %slice_select_fusion), channel_id=1, source_target_pairs={{0,2},{1,3},{2,0},{3,1},{4,6},{5,7},{6,4},{7,5},{8,10},{9,11},{10,... | collective-permute-start | bytes 786440 | tf_op jit(solution)/shard_map/ppermute | solution.py:553
  16.4 56.2 %collective-permute-start.15 = (bf16[512,1024]{1,0:T(8,128)(2,1)}, bf16[512,1024]{1,0:T(8,128)(2,1)}, u32[]{:S(2)}, u32[]{:S(2)}) collective-permute-start(bf16[512,1024]{1,0:T(8,128)(2,1)} %get-tuple-element.32), channel_id=1, source_target_pairs={{0,1},{8,9},{16,17},{24,25}} | collective-permute-start | bytes 3145736 | tf_op jit(solution)/shard_map/ppermute | solution.py:532
  19.1 55.0 %collective-permute-start.19 = (bf16[512,1024]{1,0:T(8,128)(2,1)}, bf16[512,1024]{1,0:T(8,128)(2,1)}, u32[]{:S(2)}, u32[]{:S(2)}) collective-permute-start(bf16[512,1024]{1,0:T(8,128)(2,1)} %get-tuple-element.34), channel_id=1, source_target_pairs={{0,1},{8,9},{16,17},{24,25}} | collective-permute-start | bytes 3145736 | tf_op jit(solution)/shard_map/ppermute | solution.py:532
  20.8 56.4 %collective-permute-start.23 = (bf16[512,1024]{1,0:T(8,128)(2,1)}, bf16[512,1024]{1,0:T(8,128)(2,1)}, u32[]{:S(2)}, u32[]{:S(2)}) collective-permute-start(bf16[512,1024]{1,0:T(8,128)(2,1)} %get-tuple-element.36), channel_id=1, source_target_pairs={{0,1},{8,9},{16,17},{24,25}} | collective-permute-start | bytes 3145736 | tf_op jit(solution)/shard_map/ppermute | solution.py:532
  22.5 25.9 %copy-start.38 = (s32[1,64]{1,0:T(1,128)S(1)}, s32[1,64]{1,0:T(1,128)}, u32[]{:S(2)}) copy-start(s32[1,64]{1,0:T(1,128)} %param.11) | copy-start | bytes 772
  24.1 48.6 %copy-start.2 = (bf16[768,1024]{1,0:T(8,128)(2,1)}, bf16[768,1024]{1,0:T(8,128)(2,1)S(1)}, u32[]{:S(2)}) copy-start(bf16[768,1024]{1,0:T(8,128)(2,1)S(1)} %broadcast_select_fusion.refs_0_.refs_12_) | copy-start | bytes 4718596
  24.1 48.4 %copy-start.31 = (bf16[512,1024]{1,0:T(8,128)(2,1)S(1)}, bf16[512,1024]{1,0:T(8,128)(2,1)}, u32[]{:S(2)}) copy-start(bf16[512,1024]{1,0:T(8,128)(2,1)} %get-tuple-element.33) | copy-start | bytes 3145732
  24.1 51.6 %collective-permute-start.12 = (bf16[768,1024]{1,0:T(8,128)(2,1)S(1)}, bf16[768,1024]{1,0:T(8,128)(2,1)S(1)}, u32[]{:S(2)}, u32[]{:S(2)}) collective-permute-start(bf16[768,1024]{1,0:T(8,128)(2,1)S(1)} %broadcast_select_fusion.refs_0_.refs_12_), channel_id=1, source_target_pairs={{0,2},{1,5},{8,10},{9,13},{16,18},{17,21},{24,26},{25,29}} | collective-permute-start | bytes 4718600 | tf_op jit(solution)/shard_map/ppermute | solution.py:536
  25.7 43.1 %collective-permute-start.2 = (f32[128,256]{1,0:T(8,128)S(1)}, f32[128,256]{1,0:T(8,128)S(1)}, u32[]{:S(2)}, u32[]{:S(2)}) collective-permute-start(f32[128,256]{1,0:T(8,128)S(1)} %slice_select_fusion.1), channel_id=1, source_target_pairs={{0,4},{1,5},{2,6},{3,7},{4,0},{5,1},{6,2},{7,3},{8,12},{9,13},{10,... | collective-permute-start | bytes 393224 | tf_op jit(solution)/shard_map/ppermute | solution.py:553
  68.9 3.6 collective-permute-start.3
  72.5 6.2 %collective-permute-start.4 = (bf16[1,2,144,256]{3,2,1,0:T(8,128)(2,1)S(1)}, bf16[1,2,144,256]{3,2,1,0:T(8,128)(2,1)S(1)}, u32[]{:S(2)}, u32[]{:S(2)}) collective-permute-start(bf16[1,2,144,256]{3,2,1,0:T(8,128)(2,1)S(1)} %pad_maximum_fusion.4), channel_id=1, source_target_pairs={{0,16},{8,24},{16,0},{24,8},{1,17},{9,25},{17,1},{25,9},{2,18},{10... | collective-permute-start | bytes 442376 | tf_op jit(solution)/shard_map/ppermute | solution.py:559
  72.7 44.6 %collective-permute-start.16 = (bf16[512,1024]{1,0:T(8,128)(2,1)S(1)}, bf16[512,1024]{1,0:T(8,128)(2,1)S(1)}, u32[]{:S(2)}, u32[]{:S(2)}) collective-permute-start(bf16[512,1024]{1,0:T(8,128)(2,1)S(1)} %broadcast_select_fusion.3.refs_0_), channel_id=1, source_target_pairs={{0,2},{1,5},{8,10},{9,13},{16,18},{17,21},{24,26},{25,29}} | collective-permute-start | bytes 3145736 | tf_op jit(solution)/shard_map/ppermute | solution.py:536
  74.3 47.3 %collective-permute-start.20 = (bf16[512,1024]{1,0:T(8,128)(2,1)S(1)}, bf16[512,1024]{1,0:T(8,128)(2,1)S(1)}, u32[]{:S(2)}, u32[]{:S(2)}) collective-permute-start(bf16[512,1024]{1,0:T(8,128)(2,1)S(1)} %broadcast_select_fusion.2.refs_4_), channel_id=1, source_target_pairs={{0,2},{1,5},{8,10},{9,13},{16,18},{17,21},{24,26},{25,29}} | collective-permute-start | bytes 3145736 | tf_op jit(solution)/shard_map/ppermute | solution.py:536
  75.8 50.6 %collective-permute-start.13 = (bf16[768,1024]{1,0:T(8,128)(2,1)S(1)}, bf16[768,1024]{1,0:T(8,128)(2,1)S(1)}, u32[]{:S(2)}, u32[]{:S(2)}) collective-permute-start(bf16[768,1024]{1,0:T(8,128)(2,1)S(1)} %collective-permute-done.12.refs_1_.refs_13_), channel_id=1, source_target_pairs={{2,6},{5,7},{10,14},{13,15},{18,22},{21,23},{26,30},{29,31}} | collective-permute-start | bytes 4718600 | tf_op jit(solution)/shard_map/ppermute | solution.py:536
  77.4 49.0 %copy-start.13 = (bf16[512,1024]{1,0:T(8,128)(2,1)}, bf16[512,1024]{1,0:T(8,128)(2,1)S(1)}, u32[]{:S(2)}) copy-start(bf16[512,1024]{1,0:T(8,128)(2,1)S(1)} %broadcast_select_fusion.1.refs_8_) | copy-start | bytes 3145732
  77.4 46.6 %collective-permute-start.24 = (bf16[512,1024]{1,0:T(8,128)(2,1)S(1)}, bf16[512,1024]{1,0:T(8,128)(2,1)S(1)}, u32[]{:S(2)}, u32[]{:S(2)}) collective-permute-start(bf16[512,1024]{1,0:T(8,128)(2,1)S(1)} %broadcast_select_fusion.1.refs_8_), channel_id=1, source_target_pairs={{0,2},{1,5},{8,10},{9,13},{16,18},{17,21},{24,26},{25,29}} | collective-permute-start | bytes 3145736 | tf_op jit(solution)/shard_map/ppermute | solution.py:536
  78.7 38.5 %collective-permute-start.5 = (bf16[1,4,144,256]{3,2,1,0:T(8,128)(2,1)S(1)}, bf16[1,4,144,256]{3,2,1,0:T(8,128)(2,1)S(1)}, u32[]{:S(2)}, u32[]{:S(2)}) collective-permute-start(bf16[1,4,144,256]{3,2,1,0:T(8,128)(2,1)S(1)} %pad_maximum_fusion.3), channel_id=1, source_target_pairs={{0,4},{1,5},{2,6},{3,7},{4,0},{5,1},{6,2},{7,3},{8,12},{9,13},{10,... | collective-permute-start | bytes 884744 | tf_op jit(solution)/shard_map/ppermute | solution.py:562
  117.2 9.0 %collective-permute-start.6 = (bf16[2,4,144,256]{3,2,1,0:T(8,128)(2,1)S(1)}, bf16[2,4,144,256]{3,2,1,0:T(8,128)(2,1)S(1)}, u32[]{:S(2)}, u32[]{:S(2)}) collective-permute-start(bf16[2,4,144,256]{3,2,1,0:T(8,128)(2,1)S(1)} %pad_maximum_fusion.1), channel_id=1, source_target_pairs={{0,2},{1,3},{2,0},{3,1},{4,6},{5,7},{6,4},{7,5},{8,10},{9,11},{10,... | collective-permute-start | bytes 1769480 | tf_op jit(solution)/shard_map/ppermute | solution.py:562
  117.3 18.0 %collective-permute-start.17 = (bf16[512,1024]{1,0:T(8,128)(2,1)S(1)}, bf16[512,1024]{1,0:T(8,128)(2,1)}, u32[]{:S(2)}, u32[]{:S(2)}) collective-permute-start(bf16[512,1024]{1,0:T(8,128)(2,1)S(1)} %collective-permute-done.16.refs_1_), channel_id=1, source_target_pairs={{2,6},{5,7},{10,14},{13,15},{18,22},{21,23},{26,30},{29,31}} | collective-permute-start | bytes 3145736 | tf_op jit(solution)/shard_map/ppermute | solution.py:536
  121.6 13.7 %copy-start.27 = (bf16[512,1024]{1,0:T(8,128)(2,1)}, bf16[512,1024]{1,0:T(8,128)(2,1)S(1)}, u32[]{:S(2)}) copy-start(bf16[512,1024]{1,0:T(8,128)(2,1)S(1)} %collective-permute-done.20.refs_5_) | copy-start | bytes 3145732
  121.6 25.0 %collective-permute-start.21 = (bf16[512,1024]{1,0:T(8,128)(2,1)S(1)}, bf16[512,1024]{1,0:T(8,128)(2,1)}, u32[]{:S(2)}, u32[]{:S(2)}) collective-permute-start(bf16[512,1024]{1,0:T(8,128)(2,1)S(1)} %collective-permute-done.20.refs_5_), channel_id=1, source_target_pairs={{2,6},{5,7},{10,14},{13,15},{18,22},{21,23},{26,30},{29,31}} | collective-permute-start | bytes 3145736 | tf_op jit(solution)/shard_map/ppermute | solution.py:536
  123.9 22.7 %copy-start.28 = (bf16[512,1024]{1,0:T(8,128)(2,1)}, bf16[512,1024]{1,0:T(8,128)(2,1)S(1)}, u32[]{:S(2)}) copy-start(bf16[512,1024]{1,0:T(8,128)(2,1)S(1)} %collective-permute-done.24.refs_9_) | copy-start | bytes 3145732
  123.9 33.9 %collective-permute-start.25 = (bf16[512,1024]{1,0:T(8,128)(2,1)S(1)}, bf16[512,1024]{1,0:T(8,128)(2,1)}, u32[]{:S(2)}, u32[]{:S(2)}) collective-permute-start(bf16[512,1024]{1,0:T(8,128)(2,1)S(1)} %collective-permute-done.24.refs_9_), channel_id=1, source_target_pairs={{2,6},{5,7},{10,14},{13,15},{18,22},{21,23},{26,30},{29,31}} | collective-permute-start | bytes 3145736 | tf_op jit(solution)/shard_map/ppermute | solution.py:536
  126.3 33.2 %copy-start.25 = (bf16[4,4,144,256]{3,2,1,0:T(8,128)(2,1)}, bf16[4,4,144,256]{3,2,1,0:T(8,128)(2,1)S(1)}, u32[]{:S(2)}) copy-start(bf16[4,4,144,256]{3,2,1,0:T(8,128)(2,1)S(1)} %pad_maximum_fusion.own_ref) | copy-start | bytes 3538948
  126.3 33.2 %collective-permute-start.7 = (bf16[4,4,144,256]{3,2,1,0:T(8,128)(2,1)S(1)}, bf16[4,4,144,256]{3,2,1,0:T(8,128)(2,1)}, u32[]{:S(2)}, u32[]{:S(2)}) collective-permute-start(bf16[4,4,144,256]{3,2,1,0:T(8,128)(2,1)S(1)} %pad_maximum_fusion.own_ref), channel_id=1, source_target_pairs={{0,1},{1,0},{2,3},{3,2},{4,5},{5,4},{6,7},{7,6},{8,9},{9,8},{10,11... | collective-permute-start | bytes 3538952 | tf_op jit(solution)/shard_map/ppermute | solution.py:562
  126.4 42.5 %copy-start.6 = (bf16[768,1024]{1,0:T(8,128)(2,1)}, bf16[768,1024]{1,0:T(8,128)(2,1)S(1)}, u32[]{:S(2)}) copy-start(bf16[768,1024]{1,0:T(8,128)(2,1)S(1)} %collective-permute-done.13.refs_2_.refs_14_) | copy-start | bytes 4718596
  126.4 42.5 %collective-permute-start.14 = (bf16[768,1024]{1,0:T(8,128)(2,1)S(1)}, bf16[768,1024]{1,0:T(8,128)(2,1)}, u32[]{:S(2)}, u32[]{:S(2)}) collective-permute-start(bf16[768,1024]{1,0:T(8,128)(2,1)S(1)} %collective-permute-done.13.refs_2_.refs_14_), channel_id=1, source_target_pairs={{6,4},{7,3},{14,12},{15,11},{22,20},{23,19},{30,28},{31,27}} | collective-permute-start | bytes 4718600 | tf_op jit(solution)/shard_map/ppermute | solution.py:536
  135.4 37.6 %collective-permute-start.18 = (bf16[512,1024]{1,0:T(8,128)(2,1)}, bf16[512,1024]{1,0:T(8,128)(2,1)}, u32[]{:S(2)}, u32[]{:S(2)}) collective-permute-start(bf16[512,1024]{1,0:T(8,128)(2,1)} %collective-permute-done.17.refs_2_), channel_id=1, source_target_pairs={{6,4},{7,3},{14,12},{15,11},{22,20},{23,19},{30,28},{31,27}} | collective-permute-start | bytes 3145736 | tf_op jit(solution)/shard_map/ppermute | solution.py:536
  146.6 26.4 %collective-permute-start.22 = (bf16[512,1024]{1,0:T(8,128)(2,1)}, bf16[512,1024]{1,0:T(8,128)(2,1)}, u32[]{:S(2)}, u32[]{:S(2)}) collective-permute-start(bf16[512,1024]{1,0:T(8,128)(2,1)} %collective-permute-done.21.refs_6_), channel_id=1, source_target_pairs={{6,4},{7,3},{14,12},{15,11},{22,20},{23,19},{30,28},{31,27}} | collective-permute-start | bytes 3145736 | tf_op jit(solution)/shard_map/ppermute | solution.py:536
  157.8 15.1 %collective-permute-start.26 = (bf16[512,1024]{1,0:T(8,128)(2,1)}, bf16[512,1024]{1,0:T(8,128)(2,1)}, u32[]{:S(2)}, u32[]{:S(2)}) collective-permute-start(bf16[512,1024]{1,0:T(8,128)(2,1)} %collective-permute-done.25.refs_10_), channel_id=1, source_target_pairs={{6,4},{7,3},{14,12},{15,11},{22,20},{23,19},{30,28},{31,27}} | collective-permute-start | bytes 3145736 | tf_op jit(solution)/shard_map/ppermute | solution.py:536
  182.4 173.1 %collective-permute-start.27 = (bf16[2048,1280]{1,0:T(8,128)(2,1)}, bf16[2048,1280]{1,0:T(8,128)(2,1)}, u32[]{:S(2)}, u32[]{:S(2)}) collective-permute-start(bf16[2048,1280]{1,0:T(8,128)(2,1)} %row_panel.1.mine.other), channel_id=1, source_target_pairs={{0,1},{1,0},{2,3},{3,2},{4,5},{5,4},{6,7},{7,6},{8,9},{9,8},{10,11... | collective-permute-start | bytes 15728648 | tf_op jit(solution)/shard_map/ppermute | solution.py:573
  193.3 16.7 %collective-permute-start.31 = (bf16[1024,256]{1,0:T(8,128)(2,1)}, bf16[1024,256]{1,0:T(8,128)(2,1)S(1)}, u32[]{:S(2)}, u32[]{:S(2)}) collective-permute-start(bf16[1024,256]{1,0:T(8,128)(2,1)} %get-tuple-element.42.refs_4_), channel_id=1, source_target_pairs={{0,8},{8,16},{16,24},{1,9},{9,17},{17,25},{2,10},{10,18},{18,26},{... | collective-permute-start | bytes 1572872 | tf_op jit(solution)/shard_map/ppermute | solution.py:515
  196.5 24.8 %collective-permute-start.28 = (bf16[1024,256]{1,0:T(8,128)(2,1)}, bf16[1024,256]{1,0:T(8,128)(2,1)S(1)}, u32[]{:S(2)}, u32[]{:S(2)}) collective-permute-start(bf16[1024,256]{1,0:T(8,128)(2,1)} %get-tuple-element.39.refs_0_), channel_id=1, source_target_pairs={{0,8},{8,16},{16,24},{1,9},{9,17},{17,25},{2,10},{10,18},{18,26},{... | collective-permute-start | bytes 1572872 | tf_op jit(solution)/shard_map/ppermute | solution.py:515
  199.2 22.0 %copy-start.36 = (bf16[1024,256]{1,0:T(8,128)(2,1)S(1)}, bf16[1024,256]{1,0:T(8,128)(2,1)}, u32[]{:S(2)}) copy-start(bf16[1024,256]{1,0:T(8,128)(2,1)} %get-tuple-element.40) | copy-start | bytes 1572868
  210.1 14.3 %copy-start.18 = (bf16[1024,256]{1,0:T(8,128)(2,1)}, bf16[1024,256]{1,0:T(8,128)(2,1)S(1)}, u32[]{:S(2)}) copy-start(bf16[1024,256]{1,0:T(8,128)(2,1)S(1)} %broadcast_select_fusion.7.refs_12_) | copy-start | bytes 1572868
  210.1 22.4 %collective-permute-start.32 = (bf16[1024,256]{1,0:T(8,128)(2,1)S(1)}, bf16[1024,256]{1,0:T(8,128)(2,1)S(1)}, u32[]{:S(2)}, u32[]{:S(2)}) collective-permute-start(bf16[1024,256]{1,0:T(8,128)(2,1)S(1)} %broadcast_select_fusion.7.refs_12_), channel_id=1, source_target_pairs={{0,8},{8,16},{16,24},{1,9},{9,17},{17,25},{2,10},{10,18},{18,26},{... | collective-permute-start | bytes 1572872 | tf_op jit(solution)/shard_map/ppermute | solution.py:515
  221.3 22.4 %collective-permute-start.29 = (bf16[1024,256]{1,0:T(8,128)(2,1)S(1)}, bf16[1024,256]{1,0:T(8,128)(2,1)S(1)}, u32[]{:S(2)}, u32[]{:S(2)}) collective-permute-start(bf16[1024,256]{1,0:T(8,128)(2,1)S(1)} %broadcast_select_fusion.9.refs_8_), channel_id=1, source_target_pairs={{0,8},{8,16},{16,24},{1,9},{9,17},{17,25},{2,10},{10,18},{18,26},{... | collective-permute-start | bytes 1572872 | tf_op jit(solution)/shard_map/ppermute | solution.py:515
  224.4 19.3 %copy-start.35 = (bf16[1024,256]{1,0:T(8,128)(2,1)S(1)}, bf16[1024,256]{1,0:T(8,128)(2,1)}, u32[]{:S(2)}) copy-start(bf16[1024,256]{1,0:T(8,128)(2,1)} %get-tuple-element.41) | copy-start | bytes 1572868
  232.5 22.5 %copy-start.34 = (bf16[1024,256]{1,0:T(8,128)(2,1)S(1)}, bf16[1024,256]{1,0:T(8,128)(2,1)}, u32[]{:S(2)}) copy-start(bf16[1024,256]{1,0:T(8,128)(2,1)} %get-tuple-element.46) | copy-start | bytes 1572868
  232.5 22.4 %copy-start.20 = (bf16[1024,256]{1,0:T(8,128)(2,1)}, bf16[1024,256]{1,0:T(8,128)(2,1)S(1)}, u32[]{:S(2)}) copy-start(bf16[1024,256]{1,0:T(8,128)(2,1)S(1)} %broadcast_select_fusion.6.refs_4_) | copy-start | bytes 1572868
  232.6 22.4 %collective-permute-start.33 = (bf16[1024,256]{1,0:T(8,128)(2,1)S(1)}, bf16[1024,256]{1,0:T(8,128)(2,1)S(1)}, u32[]{:S(2)}, u32[]{:S(2)}) collective-permute-start(bf16[1024,256]{1,0:T(8,128)(2,1)S(1)} %broadcast_select_fusion.6.refs_4_), channel_id=1, source_target_pairs={{0,8},{8,16},{16,24},{1,9},{9,17},{17,25},{2,10},{10,18},{18,26},{... | collective-permute-start | bytes 1572872 | tf_op jit(solution)/shard_map/ppermute | solution.py:515
  243.7 11.3 %copy-start.10 = (bf16[1024,256]{1,0:T(8,128)(2,1)}, bf16[1024,256]{1,0:T(8,128)(2,1)S(1)}, u32[]{:S(2)}) copy-start(bf16[1024,256]{1,0:T(8,128)(2,1)S(1)} %collective-permute-done.29.refs_2_.refs_9_) | copy-start | bytes 1572868
  243.7 22.5 %copy-start.33 = (bf16[1024,256]{1,0:T(8,128)(2,1)S(1)}, bf16[1024,256]{1,0:T(8,128)(2,1)}, u32[]{:S(2)}) copy-start(bf16[1024,256]{1,0:T(8,128)(2,1)} %get-tuple-element.45) | copy-start | bytes 1572868
  243.8 22.4 %copy-start.21 = (bf16[1024,256]{1,0:T(8,128)(2,1)}, bf16[1024,256]{1,0:T(8,128)(2,1)S(1)}, u32[]{:S(2)}) copy-start(bf16[1024,256]{1,0:T(8,128)(2,1)S(1)} %broadcast_select_fusion.8.refs_0_) | copy-start | bytes 1572868
  243.8 22.4 %collective-permute-start.30 = (bf16[1024,256]{1,0:T(8,128)(2,1)S(1)}, bf16[1024,256]{1,0:T(8,128)(2,1)S(1)}, u32[]{:S(2)}, u32[]{:S(2)}) collective-permute-start(bf16[1024,256]{1,0:T(8,128)(2,1)S(1)} %broadcast_select_fusion.8.refs_0_), channel_id=1, source_target_pairs={{0,8},{8,16},{16,24},{1,9},{9,17},{17,25},{2,10},{10,18},{18,26},{... | collective-permute-start | bytes 1572872 | tf_op jit(solution)/shard_map/ppermute | solution.py:515
  254.9 11.3 %copy-start.3 = (bf16[1024,256]{1,0:T(8,128)(2,1)}, bf16[1024,256]{1,0:T(8,128)(2,1)S(1)}, u32[]{:S(2)}) copy-start(bf16[1024,256]{1,0:T(8,128)(2,1)S(1)} %collective-permute-done.33.refs_7_.refs_14_.refs_5_) | copy-start | bytes 1572868
  255.0 56.1 %copy-start.22 = (bf16[1024,256]{1,0:T(8,128)(2,1)}, bf16[1024,256]{1,0:T(8,128)(2,1)S(1)}, u32[]{:S(2)}) copy-start(bf16[1024,256]{1,0:T(8,128)(2,1)S(1)} %broadcast_select_fusion.4.refs_12_) | copy-start | bytes 1572868
  255.0 22.4 %collective-permute-start.35 = (bf16[1024,256]{1,0:T(8,128)(2,1)S(1)}, bf16[1024,256]{1,0:T(8,128)(2,1)S(1)}, u32[]{:S(2)}, u32[]{:S(2)}) collective-permute-start(bf16[1024,256]{1,0:T(8,128)(2,1)S(1)} %broadcast_select_fusion.4.refs_12_), channel_id=1, source_target_pairs={{0,8},{8,16},{16,24},{1,9},{9,17},{17,25},{2,10},{10,18},{18,26},{... | collective-permute-start | bytes 1572872 | tf_op jit(solution)/shard_map/ppermute | solution.py:515
  266.2 47.1 %copy-start.4 = (bf16[1024,256]{1,0:T(8,128)(2,1)}, bf16[1024,256]{1,0:T(8,128)(2,1)S(1)}, u32[]{:S(2)}) copy-start(bf16[1024,256]{1,0:T(8,128)(2,1)S(1)} %collective-permute-done.30.refs_3_.refs_10_.refs_1_) | copy-start | bytes 1572868
  266.3 54.3 %copy-start.23 = (bf16[1024,256]{1,0:T(8,128)(2,1)}, bf16[1024,256]{1,0:T(8,128)(2,1)S(1)}, u32[]{:S(2)}) copy-start(bf16[1024,256]{1,0:T(8,128)(2,1)S(1)} %broadcast_select_fusion.5.refs_8_) | copy-start | bytes 1572868
  266.3 22.4 %collective-permute-start.34 = (bf16[1024,256]{1,0:T(8,128)(2,1)S(1)}, bf16[1024,256]{1,0:T(8,128)(2,1)S(1)}, u32[]{:S(2)}, u32[]{:S(2)}) collective-permute-start(bf16[1024,256]{1,0:T(8,128)(2,1)S(1)} %broadcast_select_fusion.5.refs_8_), channel_id=1, source_target_pairs={{0,8},{8,16},{16,24},{1,9},{9,17},{17,25},{2,10},{10,18},{18,26},{... | collective-permute-start | bytes 1572872 | tf_op jit(solution)/shard_map/ppermute | solution.py:515
  277.4 35.9 %copy-start.7 = (bf16[1024,256]{1,0:T(8,128)(2,1)}, bf16[1024,256]{1,0:T(8,128)(2,1)S(1)}, u32[]{:S(2)}) copy-start(bf16[1024,256]{1,0:T(8,128)(2,1)S(1)} %collective-permute-done.35.refs_15_.refs_6_.refs_13_) | copy-start | bytes 1572868
  277.4 22.5 %collective-permute-start.37 = (bf16[1024,256]{1,0:T(8,128)(2,1)S(1)}, bf16[1024,256]{1,0:T(8,128)(2,1)S(1)}, u32[]{:S(2)}, u32[]{:S(2)}) collective-permute-start(bf16[1024,256]{1,0:T(8,128)(2,1)S(1)} %collective-permute-done.35.refs_15_.refs_6_.refs_13_), channel_id=1, source_target_pairs={{0,8},{8,16},{16,24},{1,9},{9,17},{17,25},{2,10},{10,18},{18,26},{... | collective-permute-start | bytes 1572872 | tf_op jit(solution)/shard_map/ppermute | solution.py:515
  288.7 24.7 %copy-start.8 = (bf16[1024,256]{1,0:T(8,128)(2,1)}, bf16[1024,256]{1,0:T(8,128)(2,1)S(1)}, u32[]{:S(2)}) copy-start(bf16[1024,256]{1,0:T(8,128)(2,1)S(1)} %collective-permute-done.34.refs_11_.refs_2_.refs_9_) | copy-start | bytes 1572868
  288.7 22.5 %collective-permute-start.36 = (bf16[1024,256]{1,0:T(8,128)(2,1)S(1)}, bf16[1024,256]{1,0:T(8,128)(2,1)S(1)}, u32[]{:S(2)}, u32[]{:S(2)}) collective-permute-start(bf16[1024,256]{1,0:T(8,128)(2,1)S(1)} %collective-permute-done.34.refs_11_.refs_2_.refs_9_), channel_id=1, source_target_pairs={{0,8},{8,16},{16,24},{1,9},{9,17},{17,25},{2,10},{10,18},{18,26},{... | collective-permute-start | bytes 1572872 | tf_op jit(solution)/shard_map/ppermute | solution.py:515
  299.9 20.7 %copy-start.14 = (bf16[1024,256]{1,0:T(8,128)(2,1)}, bf16[1024,256]{1,0:T(8,128)(2,1)S(1)}, u32[]{:S(2)}) copy-start(bf16[1024,256]{1,0:T(8,128)(2,1)S(1)} %collective-permute-done.37.refs_7_.refs_14_) | copy-start | bytes 1572868
  299.9 22.6 %collective-permute-start.39 = (bf16[1024,256]{1,0:T(8,128)(2,1)S(1)}, bf16[1024,256]{1,0:T(8,128)(2,1)}, u32[]{:S(2)}, u32[]{:S(2)}) collective-permute-start(bf16[1024,256]{1,0:T(8,128)(2,1)S(1)} %collective-permute-done.37.refs_7_.refs_14_), channel_id=1, source_target_pairs={{0,8},{8,16},{16,24},{1,9},{9,17},{17,25},{2,10},{10,18},{18,26},{... | collective-permute-start | bytes 1572872 | tf_op jit(solution)/shard_map/ppermute | solution.py:515
  311.1 22.6 %collective-permute-start.38 = (bf16[1024,256]{1,0:T(8,128)(2,1)S(1)}, bf16[1024,256]{1,0:T(8,128)(2,1)}, u32[]{:S(2)}, u32[]{:S(2)}) collective-permute-start(bf16[1024,256]{1,0:T(8,128)(2,1)S(1)} %collective-permute-done.36.refs_3_.refs_10_), channel_id=1, source_target_pairs={{0,8},{8,16},{16,24},{1,9},{9,17},{17,25},{2,10},{10,18},{18,26},{... | collective-permute-start | bytes 1572872 | tf_op jit(solution)/shard_map/ppermute | solution.py:515
  355.5 32.0 %copy-start.1 = (bf16[1024,1024]{1,0:T(8,128)(2,1)S(1)}, bf16[1024,1024]{1,0:T(8,128)(2,1)}, u32[]{:S(2)}) copy-start(bf16[1024,1024]{1,0:T(8,128)(2,1)} %param.7) | copy-start | bytes 6291460
  (15 other events, 70.2 us)
